TPU v7x, 128 devices: a whole 4x4x4 slice. The times are simulated.
128 devices in a mesh: req: 8 (over y, core), exp: 16 (over z, x).
Axes of the slice: x: 4, y: 4, z: 4, core: 2. Of those that a mesh axis runs over, the one named last changes fastest.
Arguments:
- resid: bfloat16 [8192, 2048], P(('req', 'exp')), may hold values from -27 to 27
- queries: bfloat16 [8192, 2048], P(('req', 'exp')), may hold values from -6 to 6
- cache_key: bfloat16 [256, 128, 2048], P(('req', 'exp')), may hold values from -6 to 6
- cache_value: bfloat16 [256, 128, 2048], P(('req', 'exp')), may hold values from -6 to 6
- page_table: int32 [32, 8], P('req'), may hold values from 0 to 31, as said below
- row_request: int32 [8192], P('req'), may hold values from 0 to 3, as said below
- row_position: int32 [8192], P('req'), may hold values from 0 to 1023, as said below
- out_proj: bfloat16 [2048, 2048], P('exp'), may hold values from -0.375 to 0.375
- norm_gain: float32 [2048], replicated, may hold values from 0.5 to 1.5
- expert_gate: bfloat16 [128, 2048, 1408], P(('req', 'exp')), as said below
- expert_up: bfloat16 [128, 2048, 1408], P(('req', 'exp')), as said below
- expert_down: bfloat16 [128, 1408, 2048], P(('req', 'exp')), as said below
- shared_gate: bfloat16 [2048, 5632], P(None, 'exp'), may hold values from -0.125 to 0.125
- shared_up: bfloat16 [2048, 5632], P(None, 'exp'), may hold values from -0.125 to 0.125
- shared_down: bfloat16 [5632, 2048], P('exp'), may hold values from -0.078125 to 0.078125
- shared_scalar: bfloat16 [2048], replicated, may hold values from -0.375 to 0.375
- slot_expert: int32 [128], replicated, may hold values from 0 to 59, as said below
- route_expert: int32 [8192, 4], replicated, may hold values from 0 to 59, as said below
- route_gate: float32 [8192, 4], P(('req', 'exp')), may hold values from 0.05 to 0.5
Outputs:
- output: bfloat16 [8192, 2048], P(('req', 'exp'))
Inputs may be any that keep to these rules, and one draw needn't show every extreme that they name: `page_table`: within each request group the table names each of the group's 32 pages once; page p of group g lies on the device of req index g and exp index p // 2. `row_request`: each group's rows are in order of request; every request has one row or more; half of the requests of a group have exactly one row. `row_position`: the rows of one request hold consecutive positions ending at the request's length minus one. `slot_expert`: every expert is held by one slot or more. `route_expert`: each row names 4 different experts. In each aligned block of 64 rows (the rows of one device) no expert is named more than 6 times, and one expert is named exactly 6 times in every block. `expert_gate`: slots that hold the same expert hold equal weights. `expert_up`: slots that hold the same expert hold equal weights. `expert_down`: slots that hold the same expert hold equal weights.
All inputs are finite; a program needn't handle non-finite values.
Results may differ from a plain program's by a relative error of at most 0.006.
Values may be sent and summed in bfloat16 or wider, within the bound.
A program may use at most 128 MiB of HBM per device.

v0:
```python
import jax
import jax.numpy as jnp
from jax import lax
from jax.sharding import PartitionSpec as P

HEADS = 16
HEAD_DIM = 128
TOPK = 4


def expert_block(rows, gate_w, up_w, down_w):
    gate = jnp.dot(rows, gate_w, preferred_element_type=jnp.float32)
    upper = jnp.dot(rows, up_w, preferred_element_type=jnp.float32)
    hidden = (jax.nn.silu(gate) * upper).astype(jnp.bfloat16)
    return jnp.dot(hidden, down_w, preferred_element_type=jnp.float32).astype(jnp.bfloat16)


def rms_normed(stream, norm_gain):
    scale_row = lax.rsqrt(jnp.mean(stream * stream, axis=1, keepdims=True) + 1e-06)
    return (stream * scale_row * norm_gain[None, :]).astype(jnp.bfloat16)


def gather_exp(piece, count):
    spread = jnp.broadcast_to(piece[None], (count,) + piece.shape)
    got = lax.all_to_all(spread, "exp", 0, 0, tiled=True)
    return got.reshape((count * piece.shape[0],) + piece.shape[1:])


def shards(
    resid,
    queries,
    cache_key,
    cache_value,
    page_table,
    row_request,
    row_position,
    out_proj,
    norm_gain,
    expert_gate,
    expert_up,
    expert_down,
    shared_gate,
    shared_up,
    shared_down,
    shared_scalar,
    slot_expert,
    route_expert,
    route_gate,
):
    exp_count = lax.axis_size("exp")
    req_count = lax.axis_size("req")
    slot_count = exp_count * req_count
    exp_index = lax.axis_index("exp")
    own_slot = lax.axis_index("req") * exp_count + exp_index
    tok_rows = resid.shape[0]
    model_width = resid.shape[1]
    group_rows = row_request.shape[0]
    pages_here = cache_key.shape[0]
    page_len = cache_key.shape[1]
    req_slots = page_table.shape[0]
    max_pages = page_table.shape[1]
    capacity = 3 * tok_rows * TOPK // slot_count

    key_count = pages_here * page_len
    group_keys = exp_count * key_count
    by_head = jnp.concatenate(
        [
            queries.reshape(tok_rows, HEADS, HEAD_DIM).transpose(1, 0, 2),
            cache_key.reshape(key_count, HEADS, HEAD_DIM).transpose(1, 0, 2),
            cache_value.reshape(key_count, HEADS, HEAD_DIM).transpose(1, 0, 2),
        ],
        axis=1,
    )
    got_cols = lax.all_to_all(by_head, "exp", 0, 0, tiled=True)
    query_cols = got_cols[:, :tok_rows].reshape(group_rows, HEAD_DIM)
    key_cols = got_cols[:, tok_rows:tok_rows + key_count].reshape(group_keys, HEAD_DIM)
    value_cols = got_cols[:, tok_rows + key_count:].reshape(group_keys, HEAD_DIM)
    page_ids = jnp.arange(exp_count * pages_here, dtype=jnp.int32)
    hits = (page_table[None, :, :] == page_ids[:, None, None]).astype(jnp.int32)
    page_request = jnp.sum(
        hits * jnp.arange(req_slots, dtype=jnp.int32)[None, :, None], axis=(1, 2)
    )
    page_slot = jnp.sum(hits * jnp.arange(max_pages, dtype=jnp.int32)[None, None, :], axis=(1, 2))
    key_position = (
        page_slot[:, None] * page_len + jnp.arange(page_len, dtype=jnp.int32)[None, :]
    ).reshape(-1)
    key_request = jnp.repeat(page_request, page_len)
    visible = (row_request[:, None] == key_request[None, :]) & (
        key_position[None, :] <= row_position[:, None]
    )
    scores = jnp.dot(
        query_cols, key_cols.T, preferred_element_type=jnp.float32
    ) * HEAD_DIM ** (-0.5)
    scores = jnp.where(visible, scores, -1e30)
    top = jnp.max(scores, axis=1)
    weights = jnp.where(visible, jnp.exp(scores - top[:, None]), 0.0)
    denominators = jnp.sum(weights, axis=1)
    numerators = jnp.dot(
        weights.astype(jnp.bfloat16), value_cols, preferred_element_type=jnp.float32
    )
    attention = (numerators / denominators[:, None]).astype(jnp.bfloat16)
    mixed_part = jnp.dot(attention, out_proj, preferred_element_type=jnp.float32)
    mixed = jnp.sum(
        lax.all_to_all(
            mixed_part.astype(jnp.bfloat16).reshape(exp_count, tok_rows, model_width),
            "exp", 0, 0, tiled=True,
        ).astype(jnp.float32),
        axis=0,
    )
    stream = resid.astype(jnp.float32) + mixed
    normed = rms_normed(stream, norm_gain)

    piece = gather_exp(normed, exp_count)
    gate = jnp.dot(piece, shared_gate, preferred_element_type=jnp.float32)
    upper = jnp.dot(piece, shared_up, preferred_element_type=jnp.float32)
    shared_hidden = (jax.nn.silu(gate) * upper).astype(jnp.bfloat16)
    shared_part = jnp.dot(
        shared_hidden, shared_down, preferred_element_type=jnp.float32
    ).astype(jnp.bfloat16)
    shared_out = jnp.sum(
        lax.all_to_all(
            shared_part.reshape(exp_count, tok_rows, model_width), "exp", 0, 0, tiled=True
        ).astype(jnp.float32),
        axis=0,
    )
    shared_scale = jax.nn.sigmoid(
        jnp.dot(normed, shared_scalar, preferred_element_type=jnp.float32)
    )

    slot_ids = jnp.arange(slot_count, dtype=jnp.int32)
    same_expert = slot_expert[:, None] == slot_expert[None, :]
    copy_rank = jnp.sum(
        (same_expert & (slot_ids[None, :] < slot_ids[:, None])).astype(jnp.int32), axis=1
    )
    own_routes = lax.dynamic_slice_in_dim(route_expert, own_slot * tok_rows, tok_rows, 0).reshape(
        -1
    )
    holds = own_routes[:, None] == slot_expert[None, :]
    chosen = holds & (copy_rank[None, :] == 0)
    target = jnp.sum(jnp.where(chosen, slot_ids[None, :], 0), axis=1)
    onehot = chosen.astype(jnp.int32)
    position = jnp.sum(jnp.cumsum(onehot, axis=0) * onehot, axis=1) - 1
    buffer_index = target * capacity + position
    entry_rows = jnp.repeat(normed, TOPK, axis=0)
    outgoing = (
        jnp.zeros((slot_count * capacity, model_width), jnp.bfloat16)
        .at[buffer_index]
        .set(entry_rows)
    )
    outgoing = outgoing.reshape(slot_count, capacity, model_width)
    incoming = lax.all_to_all(outgoing, ("req", "exp"), split_axis=0, concat_axis=0, tiled=True)
    answered = expert_block(
        incoming.reshape(-1, model_width), expert_gate[0], expert_up[0], expert_down[0]
    ).reshape(slot_count, capacity, model_width)
    returned = lax.all_to_all(
        answered, ("req", "exp"), split_axis=0, concat_axis=0, tiled=True
    ).reshape(-1, model_width)
    expert_out = returned[buffer_index].reshape(tok_rows, TOPK, model_width)
    routed = jnp.sum(expert_out.astype(jnp.float32) * route_gate[:, :, None], axis=1)
    return (stream + shared_scale[:, None] * shared_out + routed).astype(jnp.bfloat16)


def solution(mesh):
    placed = (
        P(("req", "exp"), None),
        P(("req", "exp"), None),
        P(("req", "exp"), None, None),
        P(("req", "exp"), None, None),
        P("req", None),
        P("req"),
        P("req"),
        P("exp", None),
        P(),
        P(("req", "exp"), None, None),
        P(("req", "exp"), None, None),
        P(("req", "exp"), None, None),
        P(None, "exp"),
        P(None, "exp"),
        P("exp", None),
        P(),
        P(),
        P(),
        P(("req", "exp"), None),
    )
    return jax.shard_map(
        shards, mesh=mesh, in_specs=placed, out_specs=P(("req", "exp"), None), check_vma=False
    )
```

profile of v0, /device:TPU:0, one launch (start us, length us, event | category | flops | bytes accessed | tf_op | source)
XLA Modules:
  0.0 414.4 jit_solution(5283262446033798624)
XLA Ops:
  0.0 0.0 copy-start
  0.0 1.6 copy.47
  1.6 1.5 copy.48
  3.0 0.0 copy-done.3
  3.1 0.2 pad_maximum_fusion
  3.4 0.0 copy-start.11
  3.4 2.0 copy.40
  5.4 8.1 %all-to-all-start = ((bf16[16,576,128]{2,1,0:T(8,128)(2,1)}), bf16[16,576,128]{2,1,0:T(8,128)(2,1)}, u32[]{:S(2)}, u32[]{:S(2)}) async-start(bf16[16,576,128]{2,1,0:T(8,128)(2,1)} %copy.40), calls=%async_computation | async-start | bytes 4718592 | tf_op jit(solution)/shard_map/all_to_all | solution.py:74
  13.5 0.0 copy-done.11
  13.5 0.1 select_reduce_fusion.2
  13.6 0.1 add_bitcast_fusion
  13.7 35.4 %all-to-all-done = bf16[16,576,128]{2,1,0:T(8,128)(2,1)} async-done(((bf16[16,576,128]{2,1,0:T(8,128)(2,1)}), bf16[16,576,128]{2,1,0:T(8,128)(2,1)}, u32[]{:S(2)}, u32[]{:S(2)}) %all-to-all-start) | async-done | bytes 2359328 | tf_op jit(solution)/shard_map/all_to_all | solution.py:74
  49.1 1.7 fusion.49
  50.8 1.0 slice.22
  51.8 0.0 copy-done.6
  51.8 4.8 %fusion = (f32[1024]{0:T(1024)S(1)}, f32[1024,4096]{1,0:T(8,128)S(1)}) fusion(s32[4096]{0:T(1024)S(1)} %get-tuple-element.13, s32[4096]{0:T(1024)S(1)} %get-tuple-element.14, s32[1024]{0:T(1024)S(1)} %copy-done.6, s32[1024]{0:T(1024)S(1)} %copy-done.7, bf16[1024,128]{1,0:T(8,128)(2,1)S(1)} %bitcast.87, bf16[4096,128]{1,0:T(8,128)(2,1)S(1)} %bitcast.83), kind=kOutput, calls=%fused_computation.5 | convolution fusion | flops 1098906624 | bytes 18132992 | tf_op jit(solution)/shard_map/dot_general | solution.py:91
  56.6 0.0 copy-start.12
  56.6 6.1 %fusion.1 = f32[1024]{0:T(1024)S(1)} fusion(f32[1024,4096]{1,0:T(8,128)S(1)} %get-tuple-element.12, f32[1024]{0:T(1024)S(1)} %get-tuple-element.11, s32[4096]{0:T(1024)S(1)} %get-tuple-element.13, s32[4096]{0:T(1024)S(1)} %get-tuple-element.14, s32[1024]{0:T(1024)S(1)} %copy-done.6, s32[1024]{0:T(1024)S(1)} %copy-done.7), kind=kLoop, calls=%fused_computation.6 | loop fusion | flops 33553408 | bytes 16826368 | tf_op jit(solution)/shard_map/reduce_sum | solution.py:97
  62.7 0.0 copy-done.1
  62.7 0.0 copy-done.12
  62.7 12.0 %convolution_convert_fusion.1 = bf16[1024,2048]{1,0:T(8,128)(2,1)} fusion(bf16[128,2048]{1,0:T(8,128)(2,1)S(1)} %copy-done.12, bf16[4096,128]{1,0:T(8,128)(2,1)S(1)} %bitcast.82, f32[1024,4096]{1,0:T(8,128)} %copy-done.1, f32[1024]{0:T(1024)S(1)} %get-tuple-element.11, s32[4096]{0:T(1024)S(1)} %get-tuple-element.13, s32[4096]{0:T(1024)S(1)} %get-tuple-element.14, ...), kind=kOutput, calls=%fused_computation.19 | convolution fusion | flops 1646526464 | bytes 22593536 | tf_op jit(solution)/shard_map/dot_general | solution.py:102
  74.7 4.8 %all-to-all-start.1 = ((bf16[16,64,2048]{2,1,0:T(8,128)(2,1)}), bf16[16,64,2048]{2,1,0:T(8,128)(2,1)}, u32[]{:S(2)}, u32[]{:S(2)}) async-start(bf16[16,64,2048]{2,1,0:T(8,128)(2,1)} %bitcast.75), calls=%async_computation.1 | async-start | bytes 8388608 | tf_op jit(solution)/shard_map/all_to_all | solution.py:104
  79.6 0.0 copy-start.2
  79.6 0.0 copy-start.5
  79.6 0.8 constant_dynamic-slice_fusion
  80.4 0.1 copy.41
  80.5 0.1 eq.93
  80.6 0.1 eq.84
  80.7 0.1 copy.43
  80.8 0.0 copy-done.9
  80.8 0.2 convert_reduce_fusion.2
  81.0 0.2 fusion.35
  81.3 0.2 select_reduce_fusion
  81.6 58.5 %all-to-all-done.1 = bf16[16,64,2048]{2,1,0:T(8,128)(2,1)} async-done(((bf16[16,64,2048]{2,1,0:T(8,128)(2,1)}), bf16[16,64,2048]{2,1,0:T(8,128)(2,1)}, u32[]{:S(2)}, u32[]{:S(2)}) %all-to-all-start.1) | async-done | bytes 4194336 | tf_op jit(solution)/shard_map/all_to_all | solution.py:104
  140.1 3.0 convert_reduce_fusion.1
  143.1 0.2 multiply_reduce_fusion.1
  143.3 0.1 multiply_convert_fusion.1
  143.4 0.5 broadcast_in_dim.30
  143.9 1.1 reshape.169
  145.0 5.0 %scatter_custom_fusion = bf16[768,2048]{1,0:T(8,128)(2,1)} fusion(s32[256]{0:T(256)S(1)} %bitcast.89, bf16[256,2048]{1,0:T(8,128)(2,1)} %reshape.169, bf16[]{:T(256)} %constant.16.clone.1), kind=kCustom, calls=%fused_computation.23 | custom fusion | bytes 3146240 | tf_op jit(solution)/shard_map/scatter | solution.py:148
  150.0 6.3 %reshape.152 = bf16[128,6,2048]{2,1,0:T(8,128)(2,1)} reshape(bf16[768,2048]{1,0:T(8,128)(2,1)} %scatter_custom_fusion) | data formatting | bytes 6291456 | tf_op jit(solution)/shard_map/reshape | solution.py:150
  156.3 58.9 %all_to_all.30 = bf16[128,6,2048]{2,1,0:T(8,128)(2,1)} all-to-all(bf16[128,6,2048]{2,1,0:T(8,128)(2,1)} %reshape.152), channel_id=1, replica_groups=mesh['req'=8,'exp'=16] {'req','exp'}, dimensions={0} | all-to-all | bytes 6291456 | tf_op jit(solution)/shard_map/all_to_all | solution.py:151
  215.1 2.5 broadcast_in_dim.26
  217.6 4.8 %all-to-all-start.2 = ((bf16[16,64,2048]{2,1,0:T(8,128)(2,1)}), bf16[16,64,2048]{2,1,0:T(8,128)(2,1)}, u32[]{:S(2)}, u32[]{:S(2)}) async-start(bf16[16,64,2048]{2,1,0:T(8,128)(2,1)} %broadcast_in_dim.26), calls=%async_computation.2 | async-start | bytes 8388608 | tf_op jit(solution)/shard_map/all_to_all | solution.py:25
  222.4 6.3 %reshape.153 = bf16[768,2048]{1,0:T(8,128)(2,1)} reshape(bf16[128,6,2048]{2,1,0:T(8,128)(2,1)} %all_to_all.30) | data formatting | bytes 6291456 | tf_op jit(solution)/shard_map/reshape | solution.py:153
  228.7 9.7 %fusion.7 = f32[768,1408]{1,0:T(8,128)} fusion(bf16[768,2048]{1,0:T(8,128)(2,1)} %reshape.153, bf16[1,2048,1408]{2,1,0:T(8,128)(2,1)} %param.29), kind=kOutput, calls=%fused_computation.13 | convolution fusion | flops 4429185024 | bytes 13238272 | tf_op jit(solution)/shard_map/dot_general | solution.py:13
  238.4 16.9 %fusion.13 = bf16[768,2048]{1,0:T(8,128)(2,1)} fusion(bf16[1,1408,2048]{2,1,0:T(8,128)(2,1)} %param.30, f32[768,1408]{1,0:T(8,128)} %fusion.7, bf16[768,2048]{1,0:T(8,128)(2,1)} %reshape.153, bf16[1,2048,1408]{2,1,0:T(8,128)(2,1)} %param.28), kind=kOutput, calls=%fused_computation.20 | convolution fusion | flops 8866430976 | bytes 22151168 | tf_op jit(solution)/shard_map/dot_general | solution.py:15
  255.3 6.3 %reshape.154 = bf16[128,6,2048]{2,1,0:T(8,128)(2,1)} reshape(bf16[768,2048]{1,0:T(8,128)(2,1)} %fusion.13) | data formatting | bytes 6291456 | tf_op jit(solution)/shard_map/reshape | solution.py:154
  261.6 24.1 %all-to-all-done.2 = bf16[16,64,2048]{2,1,0:T(8,128)(2,1)} async-done(((bf16[16,64,2048]{2,1,0:T(8,128)(2,1)}), bf16[16,64,2048]{2,1,0:T(8,128)(2,1)}, u32[]{:S(2)}, u32[]{:S(2)}) %all-to-all-start.2) | async-done | bytes 4194336 | tf_op jit(solution)/shard_map/all_to_all | solution.py:25
  285.7 5.9 %all-to-all-start.5 = ((bf16[128,6,2048]{2,1,0:T(8,128)(2,1)}), bf16[128,6,2048]{2,1,0:T(8,128)(2,1)}, u32[]{:S(2)}, u32[]{:S(2)}) async-start(bf16[128,6,2048]{2,1,0:T(8,128)(2,1)} %reshape.154), calls=%async_computation.5 | async-start | bytes 8388608 | tf_op jit(solution)/shard_map/all_to_all | solution.py:155
  291.6 5.4 %fusion.50 = f32[1024,352]{0,1:T(8,128)} fusion(bf16[1024,2048]{1,0:T(8,128)(2,1)} %bitcast.10, bf16[2048,352]{0,1:T(8,128)(2,1)} %param.31), kind=kOutput, calls=%fused_computation.72 | convolution fusion | flops 1476395008 | bytes 7077888 | tf_op jit(solution)/shard_map/dot_general | solution.py:114
  297.0 8.9 %convolution_convert_fusion = bf16[1024,2048]{1,0:T(8,128)(2,1)} fusion(bf16[352,2048]{1,0:T(8,128)(2,1)S(1)} %copy-done, bf16[1024,2048]{1,0:T(8,128)(2,1)} %bitcast.10, bf16[2048,352]{0,1:T(8,128)(2,1)} %param.32, f32[1024,352]{0,1:T(8,128)} %fusion.50), kind=kOutput, calls=%fused_computation.18 | convolution fusion | flops 2957049856 | bytes 12713984 | tf_op jit(solution)/shard_map/dot_general | solution.py:117
  305.9 36.4 %all-to-all-done.5 = bf16[128,6,2048]{2,1,0:T(8,128)(2,1)} async-done(((bf16[128,6,2048]{2,1,0:T(8,128)(2,1)}), bf16[128,6,2048]{2,1,0:T(8,128)(2,1)}, u32[]{:S(2)}, u32[]{:S(2)}) %all-to-all-start.5) | async-done | bytes 3145760 | tf_op jit(solution)/shard_map/all_to_all | solution.py:155
  342.3 4.9 %all-to-all-start.3 = ((bf16[16,64,2048]{2,1,0:T(8,128)(2,1)}), bf16[16,64,2048]{2,1,0:T(8,128)(2,1)}, u32[]{:S(2)}, u32[]{:S(2)}) async-start(bf16[16,64,2048]{2,1,0:T(8,128)(2,1)} %bitcast.76), calls=%async_computation.3 | async-start | bytes 8388608 | tf_op jit(solution)/shard_map/all_to_all | solution.py:121
  347.3 0.7 copy.45
  348.0 0.0 copy-done.8
  348.0 0.2 fusion.22
  348.2 6.4 %reshape.155 = bf16[768,2048]{1,0:T(8,128)(2,1)} reshape(bf16[128,6,2048]{2,1,0:T(8,128)(2,1)} %all-to-all-done.5) | data formatting | bytes 6291456 | tf_op jit(solution)/shard_map/reshape | solution.py:157
  354.5 4.7 %gather_fusion = bf16[256,2048]{1,0:T(8,128)(2,1)S(1)} fusion(bf16[768,2048]{1,0:T(8,128)(2,1)} %reshape.155, s32[1024]{0:T(1024)S(1)} %pad_clamp_fusion), kind=kCustom, calls=%fused_computation | custom fusion | bytes 2098176 | tf_op jit(solution)/shard_map/gather | solution.py:158
  359.2 1.7 reshape.156
  361.0 3.2 multiply_reduce_fusion
  364.1 46.4 %all-to-all-done.3 = bf16[16,64,2048]{2,1,0:T(8,128)(2,1)} async-done(((bf16[16,64,2048]{2,1,0:T(8,128)(2,1)}), bf16[16,64,2048]{2,1,0:T(8,128)(2,1)}, u32[]{:S(2)}, u32[]{:S(2)}) %all-to-all-start.3) | async-done | bytes 4194336 | tf_op jit(solution)/shard_map/all_to_all | solution.py:121
  410.6 3.0 convert_reduce_fusion
  413.6 0.8 add_convert_fusion
  (28 shorter events, 0.2 us)
Async XLA Ops:
  0.0 297.0 %copy-start = (bf16[352,2048]{1,0:T(8,128)(2,1)S(1)}, bf16[352,2048]{1,0:T(8,128)(2,1)}, u32[]{:S(2)}) copy-start(bf16[352,2048]{1,0:T(8,128)(2,1)} %param.33) | copy-start | bytes 4325380
  0.0 3.0 copy-start.3
  3.4 10.2 %copy-start.11 = (s32[4,8]{1,0:T(4,128)S(1)}, s32[4,8]{1,0:T(4,128)}, u32[]{:S(2)}) copy-start(s32[4,8]{1,0:T(4,128)} %param.23) | copy-start | bytes 388
  5.4 46.4 %copy-start.6 = (s32[1024]{0:T(1024)S(1)}, s32[1024]{0:T(1024)}, u32[]{:S(2)}) copy-start(s32[1024]{0:T(1024)} %param.25) | copy-start | bytes 12292
  5.4 46.4 %copy-start.7 = (s32[1024]{0:T(1024)S(1)}, s32[1024]{0:T(1024)}, u32[]{:S(2)}) copy-start(s32[1024]{0:T(1024)} %param.24) | copy-start | bytes 12292
  5.4 43.7 %all-to-all-start = ((bf16[16,576,128]{2,1,0:T(8,128)(2,1)}), bf16[16,576,128]{2,1,0:T(8,128)(2,1)}, u32[]{:S(2)}, u32[]{:S(2)}) async-start(bf16[16,576,128]{2,1,0:T(8,128)(2,1)} %copy.40), calls=%async_computation | async-start | bytes 4718592 | tf_op jit(solution)/shard_map/all_to_all | solution.py:74
  56.6 6.2 %copy-start.1 = (f32[1024,4096]{1,0:T(8,128)}, f32[1024,4096]{1,0:T(8,128)S(1)}, u32[]{:S(2)}) copy-start(f32[1024,4096]{1,0:T(8,128)S(1)} %get-tuple-element.12) | copy-start | bytes 50331652
  56.6 6.2 %copy-start.12 = (bf16[128,2048]{1,0:T(8,128)(2,1)S(1)}, bf16[128,2048]{1,0:T(8,128)(2,1)}, u32[]{:S(2)}) copy-start(bf16[128,2048]{1,0:T(8,128)(2,1)} %param.26) | copy-start | bytes 1572868
  74.7 6.1 %copy-start.9 = (s32[128]{0:T(128)S(1)}, s32[128]{0:T(128)}, u32[]{:S(2)}) copy-start(s32[128]{0:T(128)} %param.35) | copy-start | bytes 1540
  74.7 65.4 %all-to-all-start.1 = ((bf16[16,64,2048]{2,1,0:T(8,128)(2,1)}), bf16[16,64,2048]{2,1,0:T(8,128)(2,1)}, u32[]{:S(2)}, u32[]{:S(2)}) async-start(bf16[16,64,2048]{2,1,0:T(8,128)(2,1)} %bitcast.75), calls=%async_computation.1 | async-start | bytes 8388608 | tf_op jit(solution)/shard_map/all_to_all | solution.py:104
  79.6 63.5 %copy-start.2 = (bf16[64,2048]{1,0:T(8,128)(2,1)S(1)}, bf16[64,2048]{1,0:T(8,128)(2,1)}, u32[]{:S(2)}) copy-start(bf16[64,2048]{1,0:T(8,128)(2,1)} %param.19) | copy-start | bytes 786436
  79.6 63.7 %copy-start.5 = (f32[2048]{0:T(1024)S(1)}, f32[2048]{0:T(1024)}, u32[]{:S(2)}) copy-start(f32[2048]{0:T(1024)} %param.27) | copy-start | bytes 24580
  217.6 68.1 %all-to-all-start.2 = ((bf16[16,64,2048]{2,1,0:T(8,128)(2,1)}), bf16[16,64,2048]{2,1,0:T(8,128)(2,1)}, u32[]{:S(2)}, u32[]{:S(2)}) async-start(bf16[16,64,2048]{2,1,0:T(8,128)(2,1)} %broadcast_in_dim.26), calls=%async_computation.2 | async-start | bytes 8388608 | tf_op jit(solution)/shard_map/all_to_all | solution.py:25
  285.7 56.6 %all-to-all-start.5 = ((bf16[128,6,2048]{2,1,0:T(8,128)(2,1)}), bf16[128,6,2048]{2,1,0:T(8,128)(2,1)}, u32[]{:S(2)}, u32[]{:S(2)}) async-start(bf16[128,6,2048]{2,1,0:T(8,128)(2,1)} %reshape.154), calls=%async_computation.5 | async-start | bytes 8388608 | tf_op jit(solution)/shard_map/all_to_all | solution.py:155
  342.3 5.0 %copy-start.10 = (f32[64,4]{0,1:T(4,128)S(1)}, f32[64,4]{0,1:T(4,128)}, u32[]{:S(2)}) copy-start(f32[64,4]{0,1:T(4,128)} %param.37) | copy-start | bytes 3076
  342.3 5.7 %copy-start.8 = (bf16[2048]{0:T(1024)(128)(2,1)S(1)}, bf16[2048]{0:T(1024)(128)(2,1)}, u32[]{:S(2)}) copy-start(bf16[2048]{0:T(1024)(128)(2,1)} %param.34) | copy-start | bytes 12292
  342.3 68.3 %all-to-all-start.3 = ((bf16[16,64,2048]{2,1,0:T(8,128)(2,1)}), bf16[16,64,2048]{2,1,0:T(8,128)(2,1)}, u32[]{:S(2)}, u32[]{:S(2)}) async-start(bf16[16,64,2048]{2,1,0:T(8,128)(2,1)} %bitcast.76), calls=%async_computation.3 | async-start | bytes 8388608 | tf_op jit(solution)/shard_map/all_to_all | solution.py:121
  354.5 6.4 %copy-start.4 = (f32[64,4]{1,0:T(8,128)S(1)}, f32[64,4]{1,0:T(8,128)}, u32[]{:S(2)}) copy-start(f32[64,4]{1,0:T(8,128)} %copy.45) | copy-start | bytes 3076
where the time goes:
time: 416 us; the launch traced here: 414 us
  waiting for transfers between devices  201 us (48%)
  blocking collectives  58.9 us (14%)
  matrix products  57.8 us (14%)
  local copies, waits for them, and re-layouts  50.5 us (12%)
  starting transfers between devices  28.6 us (7%)
  other arithmetic  17.5 us (4%)
    all_to_all x1, blocking collectives, shards(): lax.all_to_all(outgoing, ('req', 'exp'), split_axis=0, concat_axis=0, til...  58.9 us
    all_to_all x1, waiting for transfers between devices, shards(): lax.all_to_all(mixed_part.astype(jnp.bfloat16).reshape(exp_count, tok_row...  58.5 us
    all_to_all x1, waiting for transfers between devices, shards(): lax.all_to_all(shared_part.reshape(exp_count, tok_rows, model_width), 'ex...  46.4 us
    all_to_all x1, waiting for transfers between devices, shards(): lax.all_to_all(answered, ('req', 'exp'), split_axis=0, concat_axis=0, til...  36.4 us
    all_to_all x1, waiting for transfers between devices, shards(): got_cols = lax.all_to_all(by_head, 'exp', 0, 0, tiled=True)  35.4 us
    all_to_all x1, waiting for transfers between devices, gather_exp(): got = lax.all_to_all(spread, 'exp', 0, 0, tiled=True)  24.1 us
    dot_general x1, matrix products, expert_block(): jnp.dot(hidden, down_w, preferred_element_type=jnp.float32)  16.9 us
    dot_general x1, matrix products, shards(): jnp.dot(attention, out_proj, preferred_element_type=jnp.float32)  12 us
  transfers between devices with their start and end apart: 5, of which 5 were waited for; matrix products, arithmetic and copies ran while one was open for 17% of the time, Pallas kernels for 0%

commit v1 on v0

--- a/solution.py
+++ b/solution.py
@@ -1,6 +1,7 @@
 import jax
 import jax.numpy as jnp
 from jax import lax
+from jax.experimental import pallas as pl
 from jax.sharding import PartitionSpec as P
 
 HEADS = 16
@@ -18,6 +19,49 @@
 def rms_normed(stream, norm_gain):
     scale_row = lax.rsqrt(jnp.mean(stream * stream, axis=1, keepdims=True) + 1e-06)
     return (stream * scale_row * norm_gain[None, :]).astype(jnp.bfloat16)
+
+
+def head_attention_kernel(q_ref, k_ref, v_ref, rreq_ref, rpos_ref, kreq_ref, kpos_ref, o_ref):
+    scores = lax.dot_general(
+        q_ref[...], k_ref[...], (((1,), (1,)), ((), ())), preferred_element_type=jnp.float32
+    ) * HEAD_DIM ** (-0.5)
+    visible = (rreq_ref[...] == kreq_ref[...]) & (kpos_ref[...] <= rpos_ref[...])
+    scores = jnp.where(visible, scores, -1e30)
+    top = jnp.max(scores, axis=1, keepdims=True)
+    weights = jnp.where(visible, jnp.exp(scores - top), 0.0)
+    denominators = jnp.sum(weights, axis=1, keepdims=True)
+    numerators = jnp.dot(
+        weights.astype(jnp.bfloat16), v_ref[...], preferred_element_type=jnp.float32
+    )
+    o_ref[...] = (numerators / denominators).astype(o_ref.dtype)
+
+
+def head_attention(query_cols, key_cols, value_cols, row_request, row_position, key_request, key_position):
+    rows, width = query_cols.shape
+    keys = key_cols.shape[0]
+    tile = 128
+    row_spec = pl.BlockSpec((tile, width), lambda i: (i, 0))
+    whole = pl.BlockSpec((keys, width), lambda i: (0, 0))
+    row_int = pl.BlockSpec((tile, 1), lambda i: (i, 0))
+    key_int = pl.BlockSpec((1, keys), lambda i: (0, 0))
+    return pl.pallas_call(
+        head_attention_kernel,
+        grid=(rows // tile,),
+        out_shape=jax.ShapeDtypeStruct((rows, width), jnp.bfloat16),
+        in_specs=[row_spec, whole, whole, row_int, row_int, key_int, key_int],
+        out_specs=row_spec,
+        cost_estimate=pl.CostEstimate(
+            flops=4 * rows * keys * width, transcendentals=rows * keys, bytes_accessed=3 * keys * width * 2
+        ),
+    )(
+        query_cols,
+        key_cols,
+        value_cols,
+        row_request.reshape(rows, 1),
+        row_position.reshape(rows, 1),
+        key_request.reshape(1, keys),
+        key_position.reshape(1, keys),
+    )
 
 
 def gather_exp(piece, count):
@@ -85,20 +129,9 @@
         page_slot[:, None] * page_len + jnp.arange(page_len, dtype=jnp.int32)[None, :]
     ).reshape(-1)
     key_request = jnp.repeat(page_request, page_len)
-    visible = (row_request[:, None] == key_request[None, :]) & (
-        key_position[None, :] <= row_position[:, None]
-    )
-    scores = jnp.dot(
-        query_cols, key_cols.T, preferred_element_type=jnp.float32
-    ) * HEAD_DIM ** (-0.5)
-    scores = jnp.where(visible, scores, -1e30)
-    top = jnp.max(scores, axis=1)
-    weights = jnp.where(visible, jnp.exp(scores - top[:, None]), 0.0)
-    denominators = jnp.sum(weights, axis=1)
-    numerators = jnp.dot(
-        weights.astype(jnp.bfloat16), value_cols, preferred_element_type=jnp.float32
-    )
-    attention = (numerators / denominators[:, None]).astype(jnp.bfloat16)
+    attention = head_attention(
+        query_cols, key_cols, value_cols, row_request, row_position, key_request, key_position
+    )
     mixed_part = jnp.dot(attention, out_proj, preferred_element_type=jnp.float32)
     mixed = jnp.sum(
         lax.all_to_all(

time: 416 us -> 414 us (level)
  Pallas kernels: 0 us -> 14.3 us
  matrix products: 57.8 us -> 45.2 us
  other arithmetic: 17.5 us -> 13.3 us
    pallas_call x0 -> x1, Pallas kernels: none -> 14.3 us  [head_attention(): pl.pallas_call(head_attention_kernel, grid=(rows // tile,), out_shape=jax...]
    dot_general x1, matrix products: 12 us -> 4.12 us  [shards(): jnp.dot(attention, out_proj, preferred_element_type=jnp.float32)]
    reduce_sum x2 -> x1, other arithmetic: 6.22 us -> 0.09 us  [shards(): jnp.sum(hits * jnp.arange(max_pages, dtype=jnp.int32)[None, None, :], axi...]
    dot_general x1 -> x0, matrix products: 4.77 us -> none  [shards(): jnp.dot(query_cols, key_cols.T, preferred_element_type=jnp.float32)]
  transfers between devices with their start and end apart: 5 -> 5, of which waited for: 5 -> 5; matrix products, arithmetic and copies ran while one was open for 17% -> 18% of each run, Pallas kernels for 0% -> 0%
where the time goes in v1:
time: 414 us; the launch traced here: 412 us
  waiting for transfers between devices  198 us (48%)
  blocking collectives  58.9 us (14%)
  local copies, waits for them, and re-layouts  53.9 us (13%)
  matrix products  45.2 us (11%)
  starting transfers between devices  28.2 us (7%)
  Pallas kernels  14.3 us (3%)
  other arithmetic  13.3 us (3%)
    all_to_all x1, blocking collectives, shards(): lax.all_to_all(outgoing, ('req', 'exp'), split_axis=0, concat_axis=0, til...  58.9 us
    all_to_all x1, waiting for transfers between devices, shards(): lax.all_to_all(mixed_part.astype(jnp.bfloat16).reshape(exp_count, tok_row...  58.6 us
    all_to_all x1, waiting for transfers between devices, shards(): lax.all_to_all(shared_part.reshape(exp_count, tok_rows, model_width), 'ex...  46.4 us
    all_to_all x1, waiting for transfers between devices, shards(): lax.all_to_all(answered, ('req', 'exp'), split_axis=0, concat_axis=0, til...  36.4 us
    all_to_all x1, waiting for transfers between devices, shards(): got_cols = lax.all_to_all(by_head, 'exp', 0, 0, tiled=True)  32.7 us
    all_to_all x1, waiting for transfers between devices, gather_exp(): got = lax.all_to_all(spread, 'exp', 0, 0, tiled=True)  24.1 us
    dot_general x1, matrix products, expert_block(): jnp.dot(hidden, down_w, preferred_element_type=jnp.float32)  16.9 us
    pallas_call x1, Pallas kernels, head_attention(): pl.pallas_call(head_attention_kernel, grid=(rows // tile,), out_shape=jax...  14.3 us
  transfers between devices with their start and end apart: 5, of which 5 were waited for; matrix products, arithmetic and copies ran while one was open for 18% of the time, Pallas kernels for 0%

profile of v1, /device:TPU:0, one launch (start us, length us, event | category | flops | bytes accessed | tf_op | source)
XLA Modules:
  0.0 412.4 jit_solution(2666867676791228674)
XLA Ops:
  0.0 0.0 copy-start
  0.0 1.6 copy.45
  1.6 1.5 copy.46
  3.1 0.0 copy-done.3
  3.1 0.1 bitcast_bitcast_fusion
  3.1 0.5 copy_bitcast_fusion
  3.7 0.0 copy-start.6
  3.7 0.0 copy-start.7
  3.7 0.0 copy-start.11
  3.7 1.6 pad_maximum_fusion
  5.3 8.0 %all-to-all-start = ((bf16[16,576,128]{2,1,0:T(8,128)(2,1)}), bf16[16,576,128]{2,1,0:T(8,128)(2,1)}, u32[]{:S(2)}, u32[]{:S(2)}) async-start(bf16[16,576,128]{2,1,0:T(8,128)(2,1)} %pad_maximum_fusion), calls=%async_computation | async-start | bytes 4718592 | tf_op jit(solution)/shard_map/all_to_all | solution.py:118
  13.3 1.1 copy.37.rreq_ref
  14.4 1.0 copy.38.rpos_ref
  15.4 0.0 copy-done.11
  15.4 0.1 select_reduce_fusion.1
  15.5 0.7 iota_add_fusion
  16.2 32.7 %all-to-all-done = bf16[16,576,128]{2,1,0:T(8,128)(2,1)} async-done(((bf16[16,576,128]{2,1,0:T(8,128)(2,1)}), bf16[16,576,128]{2,1,0:T(8,128)(2,1)}, u32[]{:S(2)}, u32[]{:S(2)}) %all-to-all-start) | async-done | bytes 2359328 | tf_op jit(solution)/shard_map/all_to_all | solution.py:118
  48.9 3.1 fusion.29
  52.0 1.7 slice.22
  53.7 0.7 broadcast_in_dim.16
  54.4 14.3 %shard_map.181 = bf16[1024,128]{1,0:T(8,128)(2,1)} custom-call(bf16[1024,128]{1,0:T(8,128)(2,1)} %bitcast.86, bf16[4096,128]{1,0:T(8,128)(2,1)} %bitcast.83, bf16[4096,128]{1,0:T(8,128)(2,1)} %bitcast.82, s32[1024,1]{1,0:T(8,128)} %copy.37.rreq_ref, s32[1024,1]{1,0:T(8,128)} %copy.38.rpos_ref, s32[1,4096]{1,0:T(1,128)} %bitcast.89, s32[1,4096]{1,0:T(1,128)} %bitcast.88), custom_call_target="tpu_custom_call" | custom-call | flops 2147483648 | bytes 3145728 | tf_op jit(solution)/shard_map/pallas_call | solution.py:47
  68.7 4.1 convolution_convert_fusion.1
  72.8 4.7 %all-to-all-start.1 = ((bf16[16,64,2048]{2,1,0:T(8,128)(2,1)}), bf16[16,64,2048]{2,1,0:T(8,128)(2,1)}, u32[]{:S(2)}, u32[]{:S(2)}) async-start(bf16[16,64,2048]{2,1,0:T(8,128)(2,1)} %bitcast.76), calls=%async_computation.1 | async-start | bytes 8388608 | tf_op jit(solution)/shard_map/all_to_all | solution.py:137
  77.4 0.0 copy-start.1
  77.5 0.0 copy-start.5
  77.5 0.8 constant_dynamic-slice_fusion
  78.3 0.1 copy.39
  78.4 0.1 eq.74
  78.5 0.1 eq.65
  78.6 0.1 copy.41
  78.7 0.2 convert_reduce_fusion.2
  78.9 0.2 fusion.21
  79.2 0.2 select_reduce_fusion
  79.5 58.6 %all-to-all-done.1 = bf16[16,64,2048]{2,1,0:T(8,128)(2,1)} async-done(((bf16[16,64,2048]{2,1,0:T(8,128)(2,1)}), bf16[16,64,2048]{2,1,0:T(8,128)(2,1)}, u32[]{:S(2)}, u32[]{:S(2)}) %all-to-all-start.1) | async-done | bytes 4194336 | tf_op jit(solution)/shard_map/all_to_all | solution.py:137
  138.0 3.0 convert_reduce_fusion.1
  141.0 0.2 multiply_reduce_fusion.1
  141.2 0.1 multiply_convert_fusion.1
  141.4 0.5 broadcast_in_dim.21
  141.9 1.1 reshape.180
  143.0 5.0 %scatter_custom_fusion = bf16[768,2048]{1,0:T(8,128)(2,1)} fusion(s32[256]{0:T(256)S(1)} %bitcast.92, bf16[256,2048]{1,0:T(8,128)(2,1)} %reshape.180, bf16[]{:T(256)} %constant.22.clone.1), kind=kCustom, calls=%fused_computation.16 | custom fusion | bytes 3146240 | tf_op jit(solution)/shard_map/scatter | solution.py:181
  148.0 6.3 %reshape.163 = bf16[128,6,2048]{2,1,0:T(8,128)(2,1)} reshape(bf16[768,2048]{1,0:T(8,128)(2,1)} %scatter_custom_fusion) | data formatting | bytes 6291456 | tf_op jit(solution)/shard_map/reshape | solution.py:183
  154.2 58.9 %all_to_all.30 = bf16[128,6,2048]{2,1,0:T(8,128)(2,1)} all-to-all(bf16[128,6,2048]{2,1,0:T(8,128)(2,1)} %reshape.163), channel_id=1, replica_groups=mesh['req'=8,'exp'=16] {'req','exp'}, dimensions={0} | all-to-all | bytes 6291456 | tf_op jit(solution)/shard_map/all_to_all | solution.py:184
  213.1 2.5 broadcast_in_dim.17
  215.6 4.8 %all-to-all-start.2 = ((bf16[16,64,2048]{2,1,0:T(8,128)(2,1)}), bf16[16,64,2048]{2,1,0:T(8,128)(2,1)}, u32[]{:S(2)}, u32[]{:S(2)}) async-start(bf16[16,64,2048]{2,1,0:T(8,128)(2,1)} %broadcast_in_dim.17), calls=%async_computation.2 | async-start | bytes 8388608 | tf_op jit(solution)/shard_map/all_to_all | solution.py:69
  220.3 6.3 %reshape.164 = bf16[768,2048]{1,0:T(8,128)(2,1)} reshape(bf16[128,6,2048]{2,1,0:T(8,128)(2,1)} %all_to_all.30) | data formatting | bytes 6291456 | tf_op jit(solution)/shard_map/reshape | solution.py:186
  226.7 9.7 %fusion.2 = f32[768,1408]{1,0:T(8,128)} fusion(bf16[768,2048]{1,0:T(8,128)(2,1)} %reshape.164, bf16[1,2048,1408]{2,1,0:T(8,128)(2,1)} %param.29), kind=kOutput, calls=%fused_computation.6 | convolution fusion | flops 4429185024 | bytes 13238272 | tf_op jit(solution)/shard_map/dot_general | solution.py:14
  236.3 16.9 %fusion.8 = bf16[768,2048]{1,0:T(8,128)(2,1)} fusion(bf16[1,1408,2048]{2,1,0:T(8,128)(2,1)} %param.30, f32[768,1408]{1,0:T(8,128)} %fusion.2, bf16[768,2048]{1,0:T(8,128)(2,1)} %reshape.164, bf16[1,2048,1408]{2,1,0:T(8,128)(2,1)} %param.28), kind=kOutput, calls=%fused_computation.13 | convolution fusion | flops 8866430976 | bytes 22151168 | tf_op jit(solution)/shard_map/dot_general | solution.py:16
  253.3 6.3 %reshape.165 = bf16[128,6,2048]{2,1,0:T(8,128)(2,1)} reshape(bf16[768,2048]{1,0:T(8,128)(2,1)} %fusion.8) | data formatting | bytes 6291456 | tf_op jit(solution)/shard_map/reshape | solution.py:187
  259.5 24.1 %all-to-all-done.2 = bf16[16,64,2048]{2,1,0:T(8,128)(2,1)} async-done(((bf16[16,64,2048]{2,1,0:T(8,128)(2,1)}), bf16[16,64,2048]{2,1,0:T(8,128)(2,1)}, u32[]{:S(2)}, u32[]{:S(2)}) %all-to-all-start.2) | async-done | bytes 4194336 | tf_op jit(solution)/shard_map/all_to_all | solution.py:69
  283.6 5.9 %all-to-all-start.5 = ((bf16[128,6,2048]{2,1,0:T(8,128)(2,1)}), bf16[128,6,2048]{2,1,0:T(8,128)(2,1)}, u32[]{:S(2)}, u32[]{:S(2)}) async-start(bf16[128,6,2048]{2,1,0:T(8,128)(2,1)} %reshape.165), calls=%async_computation.5 | async-start | bytes 8388608 | tf_op jit(solution)/shard_map/all_to_all | solution.py:188
  289.5 5.4 %fusion.30 = f32[1024,352]{0,1:T(8,128)} fusion(bf16[1024,2048]{1,0:T(8,128)(2,1)} %bitcast.12, bf16[2048,352]{0,1:T(8,128)(2,1)} %param.31), kind=kOutput, calls=%fused_computation.61 | convolution fusion | flops 1476395008 | bytes 7077888 | tf_op jit(solution)/shard_map/dot_general | solution.py:147
  295.0 0.0 copy-done
  295.0 8.9 %convolution_convert_fusion = bf16[1024,2048]{1,0:T(8,128)(2,1)} fusion(bf16[352,2048]{1,0:T(8,128)(2,1)S(1)} %copy-done, bf16[1024,2048]{1,0:T(8,128)(2,1)} %bitcast.12, bf16[2048,352]{0,1:T(8,128)(2,1)} %param.32, f32[1024,352]{0,1:T(8,128)} %fusion.30), kind=kOutput, calls=%fused_computation.11 | convolution fusion | flops 2957049856 | bytes 12713984 | tf_op jit(solution)/shard_map/dot_general | solution.py:150
  303.9 36.4 %all-to-all-done.5 = bf16[128,6,2048]{2,1,0:T(8,128)(2,1)} async-done(((bf16[128,6,2048]{2,1,0:T(8,128)(2,1)}), bf16[128,6,2048]{2,1,0:T(8,128)(2,1)}, u32[]{:S(2)}, u32[]{:S(2)}) %all-to-all-start.5) | async-done | bytes 3145760 | tf_op jit(solution)/shard_map/all_to_all | solution.py:188
  340.3 4.9 %all-to-all-start.3 = ((bf16[16,64,2048]{2,1,0:T(8,128)(2,1)}), bf16[16,64,2048]{2,1,0:T(8,128)(2,1)}, u32[]{:S(2)}, u32[]{:S(2)}) async-start(bf16[16,64,2048]{2,1,0:T(8,128)(2,1)} %bitcast.77), calls=%async_computation.3 | async-start | bytes 8388608 | tf_op jit(solution)/shard_map/all_to_all | solution.py:154
  345.2 0.7 copy.43
  345.9 0.2 fusion.17
  346.1 6.4 %reshape.166 = bf16[768,2048]{1,0:T(8,128)(2,1)} reshape(bf16[128,6,2048]{2,1,0:T(8,128)(2,1)} %all-to-all-done.5) | data formatting | bytes 6291456 | tf_op jit(solution)/shard_map/reshape | solution.py:190
  352.5 4.7 %gather_fusion = bf16[256,2048]{1,0:T(8,128)(2,1)S(1)} fusion(bf16[768,2048]{1,0:T(8,128)(2,1)} %reshape.166, s32[1024]{0:T(1024)S(1)} %pad_clamp_fusion), kind=kCustom, calls=%fused_computation | custom fusion | bytes 2098176 | tf_op jit(solution)/shard_map/gather | solution.py:191
  357.1 1.7 reshape.167
  358.9 3.2 multiply_reduce_fusion
  362.0 46.4 %all-to-all-done.3 = bf16[16,64,2048]{2,1,0:T(8,128)(2,1)} async-done(((bf16[16,64,2048]{2,1,0:T(8,128)(2,1)}), bf16[16,64,2048]{2,1,0:T(8,128)(2,1)}, u32[]{:S(2)}, u32[]{:S(2)}) %all-to-all-start.3) | async-done | bytes 4194336 | tf_op jit(solution)/shard_map/all_to_all | solution.py:154
  408.5 3.0 convert_reduce_fusion
  411.5 0.8 add_convert_fusion
  (28 shorter events, 0.1 us)
Async XLA Ops:
  0.0 295.0 %copy-start = (bf16[352,2048]{1,0:T(8,128)(2,1)S(1)}, bf16[352,2048]{1,0:T(8,128)(2,1)}, u32[]{:S(2)}) copy-start(bf16[352,2048]{1,0:T(8,128)(2,1)} %param.33) | copy-start | bytes 4325380
  0.0 3.1 copy-start.3
  3.7 9.6 %copy-start.6 = (s32[1024]{0:T(1024)S(1)}, s32[1024]{0:T(1024)}, u32[]{:S(2)}) copy-start(s32[1024]{0:T(1024)} %param.24) | copy-start | bytes 12292
  3.7 10.7 %copy-start.7 = (s32[1024]{0:T(1024)S(1)}, s32[1024]{0:T(1024)}, u32[]{:S(2)}) copy-start(s32[1024]{0:T(1024)} %param.25) | copy-start | bytes 12292
  3.7 11.7 %copy-start.11 = (s32[4,8]{1,0:T(4,128)S(1)}, s32[4,8]{1,0:T(4,128)}, u32[]{:S(2)}) copy-start(s32[4,8]{1,0:T(4,128)} %param.23) | copy-start | bytes 388
  5.3 43.6 %all-to-all-start = ((bf16[16,576,128]{2,1,0:T(8,128)(2,1)}), bf16[16,576,128]{2,1,0:T(8,128)(2,1)}, u32[]{:S(2)}, u32[]{:S(2)}) async-start(bf16[16,576,128]{2,1,0:T(8,128)(2,1)} %pad_maximum_fusion), calls=%async_computation | async-start | bytes 4718592 | tf_op jit(solution)/shard_map/all_to_all | solution.py:118
  52.0 16.7 %copy-start.2 = (bf16[128,2048]{1,0:T(8,128)(2,1)S(1)}, bf16[128,2048]{1,0:T(8,128)(2,1)}, u32[]{:S(2)}) copy-start(bf16[128,2048]{1,0:T(8,128)(2,1)} %param.26) | copy-start | bytes 1572868
  72.8 5.9 %copy-start.9 = (s32[128]{0:T(128)S(1)}, s32[128]{0:T(128)}, u32[]{:S(2)}) copy-start(s32[128]{0:T(128)} %param.35) | copy-start | bytes 1540
  72.8 65.2 %all-to-all-start.1 = ((bf16[16,64,2048]{2,1,0:T(8,128)(2,1)}), bf16[16,64,2048]{2,1,0:T(8,128)(2,1)}, u32[]{:S(2)}, u32[]{:S(2)}) async-start(bf16[16,64,2048]{2,1,0:T(8,128)(2,1)} %bitcast.76), calls=%async_computation.1 | async-start | bytes 8388608 | tf_op jit(solution)/shard_map/all_to_all | solution.py:137
  77.4 63.6 %copy-start.1 = (bf16[64,2048]{1,0:T(8,128)(2,1)S(1)}, bf16[64,2048]{1,0:T(8,128)(2,1)}, u32[]{:S(2)}) copy-start(bf16[64,2048]{1,0:T(8,128)(2,1)} %param.19) | copy-start | bytes 786436
  77.5 63.8 %copy-start.5 = (f32[2048]{0:T(1024)S(1)}, f32[2048]{0:T(1024)}, u32[]{:S(2)}) copy-start(f32[2048]{0:T(1024)} %param.27) | copy-start | bytes 24580
  215.6 68.1 %all-to-all-start.2 = ((bf16[16,64,2048]{2,1,0:T(8,128)(2,1)}), bf16[16,64,2048]{2,1,0:T(8,128)(2,1)}, u32[]{:S(2)}, u32[]{:S(2)}) async-start(bf16[16,64,2048]{2,1,0:T(8,128)(2,1)} %broadcast_in_dim.17), calls=%async_computation.2 | async-start | bytes 8388608 | tf_op jit(solution)/shard_map/all_to_all | solution.py:69
  283.6 56.6 %all-to-all-start.5 = ((bf16[128,6,2048]{2,1,0:T(8,128)(2,1)}), bf16[128,6,2048]{2,1,0:T(8,128)(2,1)}, u32[]{:S(2)}, u32[]{:S(2)}) async-start(bf16[128,6,2048]{2,1,0:T(8,128)(2,1)} %reshape.165), calls=%async_computation.5 | async-start | bytes 8388608 | tf_op jit(solution)/shard_map/all_to_all | solution.py:188
  340.3 4.9 %copy-start.10 = (f32[64,4]{0,1:T(4,128)S(1)}, f32[64,4]{0,1:T(4,128)}, u32[]{:S(2)}) copy-start(f32[64,4]{0,1:T(4,128)} %param.37) | copy-start | bytes 3076
  340.3 5.6 %copy-start.8 = (bf16[2048]{0:T(1024)(128)(2,1)S(1)}, bf16[2048]{0:T(1024)(128)(2,1)}, u32[]{:S(2)}) copy-start(bf16[2048]{0:T(1024)(128)(2,1)} %param.34) | copy-start | bytes 12292
  340.3 68.2 %all-to-all-start.3 = ((bf16[16,64,2048]{2,1,0:T(8,128)(2,1)}), bf16[16,64,2048]{2,1,0:T(8,128)(2,1)}, u32[]{:S(2)}, u32[]{:S(2)}) async-start(bf16[16,64,2048]{2,1,0:T(8,128)(2,1)} %bitcast.77), calls=%async_computation.3 | async-start | bytes 8388608 | tf_op jit(solution)/shard_map/all_to_all | solution.py:154
  352.5 6.4 %copy-start.4 = (f32[64,4]{1,0:T(8,128)S(1)}, f32[64,4]{1,0:T(8,128)}, u32[]{:S(2)}) copy-start(f32[64,4]{1,0:T(8,128)} %copy.43) | copy-start | bytes 3076

commit v2 on v1

--- a/solution.py
+++ b/solution.py
@@ -143,19 +143,16 @@
     stream = resid.astype(jnp.float32) + mixed
     normed = rms_normed(stream, norm_gain)
 
-    piece = gather_exp(normed, exp_count)
+    piece = lax.all_gather(normed, "exp", axis=0, tiled=True)
     gate = jnp.dot(piece, shared_gate, preferred_element_type=jnp.float32)
     upper = jnp.dot(piece, shared_up, preferred_element_type=jnp.float32)
     shared_hidden = (jax.nn.silu(gate) * upper).astype(jnp.bfloat16)
     shared_part = jnp.dot(
         shared_hidden, shared_down, preferred_element_type=jnp.float32
     ).astype(jnp.bfloat16)
-    shared_out = jnp.sum(
-        lax.all_to_all(
-            shared_part.reshape(exp_count, tok_rows, model_width), "exp", 0, 0, tiled=True
-        ).astype(jnp.float32),
-        axis=0,
-    )
+    shared_out = lax.psum_scatter(
+        shared_part, "exp", scatter_dimension=0, tiled=True
+    ).astype(jnp.float32)
     shared_scale = jax.nn.sigmoid(
         jnp.dot(normed, shared_scalar, preferred_element_type=jnp.float32)
     )

time: 414 us -> 362 us (0.87)
  waiting for transfers between devices: 198 us -> 147 us
  between operations: 0.3 us -> 13.6 us
  blocking collectives: 58.9 us -> 54 us
    all_to_all x3 -> x1, waiting for transfers between devices: 129 us -> 0.01 us  [shards(): lax.all_to_all(outgoing, ('req', 'exp'), split_axis=0, concat_axis=0, til...]
    all_gather x0 -> x1, waiting for transfers between devices: none -> 63 us  [shards(): piece = lax.all_gather(normed, 'exp', axis=0, tiled=True)]
    all_to_all x1, waiting for transfers between devices: 36.4 us -> 50.5 us  [shards(): lax.all_to_all(answered, ('req', 'exp'), split_axis=0, concat_axis=0, til...]
    all_to_all x3 -> x1, starting transfers between devices: 14.3 us -> 6.66 us  [shards(): lax.all_to_all(outgoing, ('req', 'exp'), split_axis=0, concat_axis=0, til...]
    all_to_all x1, blocking collectives: 58.9 us -> 54 us  [shards(): lax.all_to_all(mixed_part.astype(jnp.bfloat16).reshape(exp_count, tok_row...]
    all_to_all x1, starting transfers between devices: 5.89 us -> 10.3 us  [shards(): lax.all_to_all(answered, ('req', 'exp'), split_axis=0, concat_axis=0, til...]
  transfers between devices with their start and end apart: 5 -> 5, of which waited for: 5 -> 4; matrix products, arithmetic and copies ran while one was open for 18% -> 25% of each run, Pallas kernels for 0% -> 0%
where the time goes in v2:
time: 362 us; the launch traced here: 360 us
  waiting for transfers between devices  147 us (41%)
  blocking collectives  54 us (15%)
  local copies, waits for them, and re-layouts  52.7 us (15%)
  matrix products  43 us (12%)
  starting transfers between devices  25.4 us (7%)
  Pallas kernels  14.3 us (4%)
  between operations  13.6 us (4%)
  other arithmetic  10.1 us (3%)
    all_gather x1, waiting for transfers between devices, shards(): piece = lax.all_gather(normed, 'exp', axis=0, tiled=True)  63 us
    all_to_all x1, blocking collectives, shards(): lax.all_to_all(mixed_part.astype(jnp.bfloat16).reshape(exp_count, tok_row...  54 us
    all_to_all x1, waiting for transfers between devices, shards(): lax.all_to_all(answered, ('req', 'exp'), split_axis=0, concat_axis=0, til...  50.5 us
    all_to_all x1, waiting for transfers between devices, shards(): got_cols = lax.all_to_all(by_head, 'exp', 0, 0, tiled=True)  32.6 us
    dot_general x1, matrix products, expert_block(): jnp.dot(hidden, down_w, preferred_element_type=jnp.float32)  17 us
    pallas_call x1, Pallas kernels, head_attention(): pl.pallas_call(head_attention_kernel, grid=(rows // tile,), out_shape=jax...  14.3 us
    all_to_all x1, starting transfers between devices, shards(): lax.all_to_all(answered, ('req', 'exp'), split_axis=0, concat_axis=0, til...  10.3 us
    dot_general x1, matrix products, expert_block(): upper = jnp.dot(rows, up_w, preferred_element_type=jnp.float32)  9.65 us
  transfers between devices with their start and end apart: 5, of which 4 were waited for; matrix products, arithmetic and copies ran while one was open for 25% of the time, Pallas kernels for 0%

profile of v2, /device:TPU:0, one launch (start us, length us, event | category | flops | bytes accessed | tf_op | source)
XLA Modules:
  0.0 359.8 jit_solution(357889919599537429)
XLA Ops:
  6.5 0.0 copy-start
  6.5 1.6 copy.45
  8.1 1.5 copy.46
  9.6 0.0 copy-done.6
  9.6 0.1 bitcast_bitcast_fusion
  9.7 0.5 copy_bitcast_fusion
  10.2 1.6 pad_maximum_fusion
  11.8 8.1 %all-to-all-start = ((bf16[16,576,128]{2,1,0:T(8,128)(2,1)}), bf16[16,576,128]{2,1,0:T(8,128)(2,1)}, u32[]{:S(2)}, u32[]{:S(2)}) async-start(bf16[16,576,128]{2,1,0:T(8,128)(2,1)} %pad_maximum_fusion), calls=%async_computation | async-start | bytes 4718592 | tf_op jit(solution)/shard_map/all_to_all | solution.py:118
  20.0 0.0 all-gather.2.cloned.1.call-start
  20.0 0.0 copy-done.8
  20.0 1.1 copy.37.rreq_ref
  21.1 0.0 copy-done.9
  21.1 1.0 copy.38.rpos_ref
  22.1 0.0 copy-done.13
  22.1 0.1 select_reduce_fusion.1
  22.2 0.7 iota_add_fusion
  22.9 32.6 %all-to-all-done = bf16[16,576,128]{2,1,0:T(8,128)(2,1)} async-done(((bf16[16,576,128]{2,1,0:T(8,128)(2,1)}), bf16[16,576,128]{2,1,0:T(8,128)(2,1)}, u32[]{:S(2)}, u32[]{:S(2)}) %all-to-all-start) | async-done | bytes 2359328 | tf_op jit(solution)/shard_map/all_to_all | solution.py:118
  55.5 3.1 fusion.29
  58.6 1.7 slice.22
  60.3 0.7 broadcast_in_dim.14
  60.9 14.3 %shard_map.181 = bf16[1024,128]{1,0:T(8,128)(2,1)} custom-call(bf16[1024,128]{1,0:T(8,128)(2,1)} %bitcast.83, bf16[4096,128]{1,0:T(8,128)(2,1)} %bitcast.80, bf16[4096,128]{1,0:T(8,128)(2,1)} %bitcast.79, s32[1024,1]{1,0:T(8,128)} %copy.37.rreq_ref, s32[1024,1]{1,0:T(8,128)} %copy.38.rpos_ref, s32[1,4096]{1,0:T(1,128)} %bitcast.86, s32[1,4096]{1,0:T(1,128)} %bitcast.85), custom_call_target="tpu_custom_call" | custom-call | flops 2147483648 | bytes 3145728 | tf_op jit(solution)/shard_map/pallas_call | solution.py:47
  75.3 0.0 copy-done.5
  75.3 2.2 convolution_convert_fusion.1
  77.5 54.0 %all_to_all.20 = bf16[16,64,2048]{2,1,0:T(8,128)(2,1)S(1)} all-to-all(bf16[16,64,2048]{2,1,0:T(8,128)(2,1)S(1)} %bitcast.74), channel_id=1, replica_groups=mesh['req'=8,'exp'=16] {'exp'}, dimensions={0} | all-to-all | bytes 8388608 | tf_op jit(solution)/shard_map/all_to_all | solution.py:137
  131.5 0.8 convert_reduce_fusion
  132.2 0.2 copy-done.4
  132.4 0.2 multiply_reduce_fusion.1
  132.6 0.6 copy-done.2
  133.2 0.8 multiply_convert_fusion.1
  134.1 0.0 all-gather.2.cloned.1.call-update
  134.1 0.8 constant_dynamic-slice_fusion
  134.8 0.1 copy.39
  134.9 0.1 eq.74
  135.1 0.1 eq.65
  135.2 0.1 copy.41
  135.3 0.2 convert_reduce_fusion.1
  135.5 0.2 fusion.21
  135.8 0.2 select_reduce_fusion
  136.0 1.4 broadcast_in_dim.18
  137.5 0.3 reshape.171
  137.8 4.3 %scatter_custom_fusion = bf16[768,2048]{1,0:T(8,128)(2,1)} fusion(s32[256]{0:T(256)S(1)} %bitcast.89, bf16[256,2048]{1,0:T(8,128)(2,1)S(1)} %reshape.171, bf16[]{:T(256)} %constant.22.clone.1), kind=kCustom, calls=%fused_computation.15 | custom fusion | bytes 3145730 | tf_op jit(solution)/shard_map/scatter | solution.py:178
  142.1 6.3 %reshape.154 = bf16[128,6,2048]{2,1,0:T(8,128)(2,1)} reshape(bf16[768,2048]{1,0:T(8,128)(2,1)} %scatter_custom_fusion) | data formatting | bytes 6291456 | tf_op jit(solution)/shard_map/reshape | solution.py:180
  148.4 6.7 %all-to-all-start.2 = ((bf16[128,6,2048]{2,1,0:T(8,128)(2,1)}), bf16[128,6,2048]{2,1,0:T(8,128)(2,1)}, u32[]{:S(2)}, u32[]{:S(2)}) async-start(bf16[128,6,2048]{2,1,0:T(8,128)(2,1)} %reshape.154), calls=%async_computation.3 | async-start | bytes 8388608 | tf_op jit(solution)/shard_map/all_to_all | solution.py:181
  155.0 0.2 reduce-scatter.2.cloned.1.call-start
  155.3 63.0 %all-gather.2.cloned.1.call-done = bf16[1024,2048]{1,0:T(8,128)(2,1)} async-done(((bf16[64,2048]{1,0:T(8,128)(2,1)}), bf16[1024,2048]{1,0:T(8,128)(2,1)}) %all-gather.2.cloned.1.call-update) | async-done | bytes 4194320 | tf_op jit(solution)/shard_map/all_gather | solution.py:146
  218.3 0.0 copy-done.14
  218.3 5.0 %fusion.30 = f32[1024,352]{0,1:T(8,128)} fusion(bf16[1024,2048]{1,0:T(8,128)(2,1)} %all-gather.2.cloned.1.call-done, bf16[2048,352]{0,1:T(8,128)(2,1)S(1)} %copy-done.14), kind=kOutput, calls=%fused_computation.60 | convolution fusion | flops 1476395008 | bytes 7077888 | tf_op jit(solution)/shard_map/dot_general | solution.py:147
  223.2 9.0 %convolution_convert_fusion = bf16[1024,2048]{1,0:T(8,128)(2,1)} fusion(bf16[352,2048]{1,0:T(8,128)(2,1)S(1)} %copy-done, bf16[1024,2048]{1,0:T(8,128)(2,1)} %all-gather.2.cloned.1.call-done, bf16[2048,352]{0,1:T(8,128)(2,1)} %param.32, f32[1024,352]{0,1:T(8,128)} %fusion.30), kind=kOutput, calls=%fused_computation.10 | convolution fusion | flops 2957049856 | bytes 12713984 | tf_op jit(solution)/shard_map/dot_general | solution.py:150
  232.2 0.0 reduce-scatter.2.cloned.1.call-update
  232.3 0.0 all-to-all-done.2
  232.3 6.3 %reshape.155 = bf16[768,2048]{1,0:T(8,128)(2,1)} reshape(bf16[128,6,2048]{2,1,0:T(8,128)(2,1)} %all-to-all-done.2) | data formatting | bytes 6291456 | tf_op jit(solution)/shard_map/reshape | solution.py:183
  238.6 9.7 %fusion.2 = f32[768,1408]{1,0:T(8,128)} fusion(bf16[768,2048]{1,0:T(8,128)(2,1)} %reshape.155, bf16[1,2048,1408]{2,1,0:T(8,128)(2,1)} %param.29), kind=kOutput, calls=%fused_computation.5 | convolution fusion | flops 4429185024 | bytes 13238272 | tf_op jit(solution)/shard_map/dot_general | solution.py:14
  248.3 17.0 %fusion.8 = bf16[768,2048]{1,0:T(8,128)(2,1)} fusion(bf16[1,1408,2048]{2,1,0:T(8,128)(2,1)} %param.30, f32[768,1408]{1,0:T(8,128)} %fusion.2, bf16[768,2048]{1,0:T(8,128)(2,1)} %reshape.155, bf16[1,2048,1408]{2,1,0:T(8,128)(2,1)} %param.28), kind=kOutput, calls=%fused_computation.12 | convolution fusion | flops 8866430976 | bytes 22151168 | tf_op jit(solution)/shard_map/dot_general | solution.py:16
  265.2 6.3 %reshape.156 = bf16[128,6,2048]{2,1,0:T(8,128)(2,1)} reshape(bf16[768,2048]{1,0:T(8,128)(2,1)} %fusion.8) | data formatting | bytes 6291456 | tf_op jit(solution)/shard_map/reshape | solution.py:184
  271.6 10.3 %all-to-all-start.3 = ((bf16[128,6,2048]{2,1,0:T(8,128)(2,1)}), bf16[128,6,2048]{2,1,0:T(8,128)(2,1)}, u32[]{:S(2)}, u32[]{:S(2)}) async-start(bf16[128,6,2048]{2,1,0:T(8,128)(2,1)} %reshape.156), calls=%async_computation.4 | async-start | bytes 8388608 | tf_op jit(solution)/shard_map/all_to_all | solution.py:185
  281.9 0.7 copy.43
  282.7 0.2 fusion.17
  282.8 50.5 %all-to-all-done.3 = bf16[128,6,2048]{2,1,0:T(8,128)(2,1)} async-done(((bf16[128,6,2048]{2,1,0:T(8,128)(2,1)}), bf16[128,6,2048]{2,1,0:T(8,128)(2,1)}, u32[]{:S(2)}, u32[]{:S(2)}) %all-to-all-start.3) | async-done | bytes 3145760 | tf_op jit(solution)/shard_map/all_to_all | solution.py:185
  333.3 6.4 %reshape.157 = bf16[768,2048]{1,0:T(8,128)(2,1)} reshape(bf16[128,6,2048]{2,1,0:T(8,128)(2,1)} %all-to-all-done.3) | data formatting | bytes 6291456 | tf_op jit(solution)/shard_map/reshape | solution.py:187
  339.7 5.8 %gather_fusion = bf16[256,2048]{1,0:T(8,128)(2,1)} fusion(bf16[768,2048]{1,0:T(8,128)(2,1)} %reshape.157, s32[1024]{0:T(1024)S(1)} %pad_clamp_fusion), kind=kCustom, calls=%fused_computation | custom fusion | bytes 2098176 | tf_op jit(solution)/shard_map/gather | solution.py:188
  345.5 1.7 reshape.158
  347.2 3.1 multiply_reduce_fusion
  350.3 0.5 reduce-scatter.2.cloned.1.call-done
  350.8 2.2 add_convert_fusion
  (34 shorter events, 0.2 us)
Async XLA Ops:
  6.5 216.7 %copy-start = (bf16[352,2048]{1,0:T(8,128)(2,1)S(1)}, bf16[352,2048]{1,0:T(8,128)(2,1)}, u32[]{:S(2)}) copy-start(bf16[352,2048]{1,0:T(8,128)(2,1)} %param.33) | copy-start | bytes 4325380
  6.5 3.1 copy-start.6
  11.8 8.2 %copy-start.8 = (s32[1024]{0:T(1024)S(1)}, s32[1024]{0:T(1024)}, u32[]{:S(2)}) copy-start(s32[1024]{0:T(1024)} %param.24) | copy-start | bytes 12292
  11.8 9.3 %copy-start.9 = (s32[1024]{0:T(1024)S(1)}, s32[1024]{0:T(1024)}, u32[]{:S(2)}) copy-start(s32[1024]{0:T(1024)} %param.25) | copy-start | bytes 12292
  11.8 10.3 %copy-start.13 = (s32[4,8]{1,0:T(4,128)S(1)}, s32[4,8]{1,0:T(4,128)}, u32[]{:S(2)}) copy-start(s32[4,8]{1,0:T(4,128)} %param.23) | copy-start | bytes 388
  11.8 43.7 %all-to-all-start = ((bf16[16,576,128]{2,1,0:T(8,128)(2,1)}), bf16[16,576,128]{2,1,0:T(8,128)(2,1)}, u32[]{:S(2)}, u32[]{:S(2)}) async-start(bf16[16,576,128]{2,1,0:T(8,128)(2,1)} %pad_maximum_fusion), calls=%async_computation | async-start | bytes 4718592 | tf_op jit(solution)/shard_map/all_to_all | solution.py:118
  20.0 198.3 %all-gather.2.cloned.1.call-start = ((), (), s32[]{:S(2)}) async-start(), calls=%async_computation.5 | async-start | bytes 4456448 | tf_op jit(solution)/shard_map/all_gather | solution.py:146
  60.9 14.3 %copy-start.5 = (bf16[128,2048]{1,0:T(8,128)(2,1)S(1)}, bf16[128,2048]{1,0:T(8,128)(2,1)}, u32[]{:S(2)}) copy-start(bf16[128,2048]{1,0:T(8,128)(2,1)} %param.26) | copy-start | bytes 1572868
  131.5 1.0 copy-start.4
  131.5 1.8 copy-start.7
  131.5 3.8 %copy-start.11 = (s32[128]{0:T(128)S(1)}, s32[128]{0:T(128)}, u32[]{:S(2)}) copy-start(s32[128]{0:T(128)} %param.35) | copy-start | bytes 1540
  132.4 0.8 copy-start.2
  148.4 69.9 %copy-start.14 = (bf16[2048,352]{0,1:T(8,128)(2,1)S(1)}, bf16[2048,352]{0,1:T(8,128)(2,1)}, u32[]{:S(2)}) copy-start(bf16[2048,352]{0,1:T(8,128)(2,1)} %param.31) | copy-start | bytes 4325380
  148.4 83.9 %all-to-all-start.2 = ((bf16[128,6,2048]{2,1,0:T(8,128)(2,1)}), bf16[128,6,2048]{2,1,0:T(8,128)(2,1)}, u32[]{:S(2)}, u32[]{:S(2)}) async-start(bf16[128,6,2048]{2,1,0:T(8,128)(2,1)} %reshape.154), calls=%async_computation.3 | async-start | bytes 8388608 | tf_op jit(solution)/shard_map/all_to_all | solution.py:181
  155.0 195.8 %reduce-scatter.2.cloned.1.call-start = ((), (), s32[]{:S(2)}) async-start(), calls=%async_computation.6 | async-start | bytes 4456448 | tf_op jit(solution)/shard_map/reduce_scatter | solution.py:153
  271.6 10.4 %copy-start.12 = (f32[64,4]{0,1:T(4,128)S(1)}, f32[64,4]{0,1:T(4,128)}, u32[]{:S(2)}) copy-start(f32[64,4]{0,1:T(4,128)} %param.37) | copy-start | bytes 3076
  271.6 11.1 %copy-start.10 = (bf16[2048]{0:T(1024)(128)(2,1)S(1)}, bf16[2048]{0:T(1024)(128)(2,1)}, u32[]{:S(2)}) copy-start(bf16[2048]{0:T(1024)(128)(2,1)} %param.34) | copy-start | bytes 12292
  271.6 11.1 %copy-start.3 = (bf16[64,2048]{1,0:T(8,128)(2,1)S(1)}, bf16[64,2048]{1,0:T(8,128)(2,1)}, u32[]{:S(2)}) copy-start(bf16[64,2048]{1,0:T(8,128)(2,1)} %multiply_convert_fusion.1) | copy-start | bytes 786436
  271.6 61.8 %all-to-all-start.3 = ((bf16[128,6,2048]{2,1,0:T(8,128)(2,1)}), bf16[128,6,2048]{2,1,0:T(8,128)(2,1)}, u32[]{:S(2)}, u32[]{:S(2)}) async-start(bf16[128,6,2048]{2,1,0:T(8,128)(2,1)} %reshape.156), calls=%async_computation.4 | async-start | bytes 8388608 | tf_op jit(solution)/shard_map/all_to_all | solution.py:185
  339.7 13.3 %copy-start.1 = (bf16[352,2048]{1,0:T(8,128)(2,1)S(1)}, bf16[352,2048]{1,0:T(8,128)(2,1)}, u32[]{:S(2)}) copy-start(bf16[352,2048]{1,0:T(8,128)(2,1)} %param.33) | copy-start | bytes 4325380
Sparse Core Ops, SparseCore 0:
  134.2 83.9 all-gather.1
  232.4 118.3 reduce-scatter.1

commit v3 on v2

--- a/solution.py
+++ b/solution.py
@@ -170,23 +170,39 @@
     target = jnp.sum(jnp.where(chosen, slot_ids[None, :], 0), axis=1)
     onehot = chosen.astype(jnp.int32)
     position = jnp.sum(jnp.cumsum(onehot, axis=0) * onehot, axis=1) - 1
-    buffer_index = target * capacity + position
-    entry_rows = jnp.repeat(normed, TOPK, axis=0)
-    outgoing = (
-        jnp.zeros((slot_count * capacity, model_width), jnp.bfloat16)
-        .at[buffer_index]
-        .set(entry_rows)
-    )
-    outgoing = outgoing.reshape(slot_count, capacity, model_width)
+    places = jnp.arange(capacity, dtype=jnp.int32)
+    entry_of = (target[:, None, None] == slot_ids[None, :, None]) & (
+        position[:, None, None] == places[None, None, :]
+    )
+    row_of_entry = jnp.arange(tok_rows * TOPK, dtype=jnp.int32) // TOPK
+    row_match = row_of_entry[:, None] == jnp.arange(tok_rows, dtype=jnp.int32)[None, :]
+    picks = jnp.einsum(
+        "esc,ei->sci",
+        entry_of.astype(jnp.bfloat16),
+        row_match.astype(jnp.bfloat16),
+        preferred_element_type=jnp.float32,
+    ).astype(jnp.bfloat16)
+    outgoing = jnp.einsum(
+        "sci,id->scd", picks, normed, preferred_element_type=jnp.float32
+    ).astype(jnp.bfloat16)
     incoming = lax.all_to_all(outgoing, ("req", "exp"), split_axis=0, concat_axis=0, tiled=True)
-    answered = expert_block(
-        incoming.reshape(-1, model_width), expert_gate[0], expert_up[0], expert_down[0]
-    ).reshape(slot_count, capacity, model_width)
-    returned = lax.all_to_all(
-        answered, ("req", "exp"), split_axis=0, concat_axis=0, tiled=True
-    ).reshape(-1, model_width)
-    expert_out = returned[buffer_index].reshape(tok_rows, TOPK, model_width)
-    routed = jnp.sum(expert_out.astype(jnp.float32) * route_gate[:, :, None], axis=1)
+    answered = expert_block(incoming, expert_gate[0], expert_up[0], expert_down[0])
+    returned = lax.all_to_all(answered, ("req", "exp"), split_axis=0, concat_axis=0, tiled=True)
+    combine = jnp.sum(
+        jnp.where(
+            entry_of.reshape(tok_rows, TOPK, slot_count, capacity),
+            route_gate[:, :, None, None],
+            0.0,
+        ),
+        axis=1,
+    )
+    routed = jnp.einsum(
+        "rsc,scd->rd",
+        combine,
+        returned.astype(jnp.float32),
+        precision=lax.Precision.HIGHEST,
+        preferred_element_type=jnp.float32,
+    )
     return (stream + shared_scale[:, None] * shared_out + routed).astype(jnp.bfloat16)
 
 

time: 362 us -> 372 us (1.028)
  waiting for transfers between devices: 147 us -> 177 us
  local copies, waits for them, and re-layouts: 52.7 us -> 25.2 us
  matrix products: 43 us -> 57.9 us
  other arithmetic: 10.1 us -> 5.36 us
    reshape x5 -> x0, local copies, waits for them, and re-layouts: 25.6 us -> none  [the longest x1 6.37 us: shards(): returned = lax.all_to_all(answered, ('req', 'exp'), split_axis=0, concat_...]
    reduce_scatter x1, waiting for transfers between devices: 0.47 us -> 23.1 us  [shards(): lax.psum_scatter(shared_part, 'exp', scatter_dimension=0, tiled=True)]
    dot_general x0 -> x2, matrix products: none -> 11.6 us  [the longest x1 7.67 us: shards(): jnp.einsum('rsc,scd->rd', combine, returned.astype(jnp.float32), precisio...]
    convert_element_type x1 -> x2, local copies, waits for them, and re-layouts: 1.73 us -> 11.3 us  [the longest x1 5.69 us: shards(): outgoing = jnp.einsum('sci,id->scd', picks, normed, preferred_element_typ...]
    all_gather x1, waiting for transfers between devices: 63 us -> 69 us  [shards(): piece = lax.all_gather(normed, 'exp', axis=0, tiled=True)]
    gather x1 -> x0, local copies, waits for them, and re-layouts: 5.76 us -> none  [shards(): expert_out = returned[buffer_index].reshape(tok_rows, TOPK, model_width)]
    scatter x1 -> x0, local copies, waits for them, and re-layouts: 4.3 us -> none  [shards(): outgoing = jnp.zeros((slot_count * capacity, model_width), jnp.bfloat16)....]
  transfers between devices with their start and end apart: 5 -> 5, of which waited for: 4 -> 4; matrix products, arithmetic and copies ran while one was open for 25% -> 18% of each run, Pallas kernels for 0% -> 0%
where the time goes in v3:
time: 372 us; the launch traced here: 371 us
  waiting for transfers between devices  177 us (48%)
  matrix products  57.9 us (16%)
  blocking collectives  53.9 us (14%)
  local copies, waits for them, and re-layouts  25.2 us (7%)
  starting transfers between devices  23.9 us (6%)
  Pallas kernels  14.3 us (4%)
  between operations  13.7 us (4%)
  other arithmetic  5.36 us (1%)
    all_gather x1, waiting for transfers between devices, shards(): piece = lax.all_gather(normed, 'exp', axis=0, tiled=True)  69 us
    all_to_all x1, blocking collectives, shards(): lax.all_to_all(mixed_part.astype(jnp.bfloat16).reshape(exp_count, tok_row...  53.9 us
    all_to_all x1, waiting for transfers between devices, shards(): lax.all_to_all(answered, ('req', 'exp'), split_axis=0, concat_axis=0, til...  52.2 us
    all_to_all x1, waiting for transfers between devices, shards(): got_cols = lax.all_to_all(by_head, 'exp', 0, 0, tiled=True)  32.6 us
    reduce_scatter x1, waiting for transfers between devices, shards(): lax.psum_scatter(shared_part, 'exp', scatter_dimension=0, tiled=True)  23.1 us
    dot_general x1, matrix products, expert_block(): jnp.dot(hidden, down_w, preferred_element_type=jnp.float32)  18.4 us
    pallas_call x1, Pallas kernels, head_attention(): pl.pallas_call(head_attention_kernel, grid=(rows // tile,), out_shape=jax...  14.3 us
    dot_general x1, matrix products, expert_block(): upper = jnp.dot(rows, up_w, preferred_element_type=jnp.float32)  11.1 us
  transfers between devices with their start and end apart: 5, of which 4 were waited for; matrix products, arithmetic and copies ran while one was open for 18% of the time, Pallas kernels for 0%

profile of v3, /device:TPU:0, one launch (start us, length us, event | category | flops | bytes accessed | tf_op | source)
XLA Modules:
  0.0 371.2 jit_solution(10477694965537249385)
XLA Ops:
  6.5 0.0 copy-start
  6.5 1.1 bitcast_bitcast_fusion
  7.7 1.5 copy.66
  9.1 1.5 copy.67
  10.6 0.5 copy_bitcast_fusion
  11.1 0.0 copy-start.6
  11.1 0.0 copy-start.7
  11.2 0.0 copy-start.11
  11.2 1.6 pad_maximum_fusion
  12.8 8.0 %all-to-all-start = ((bf16[16,576,128]{2,1,0:T(8,128)(2,1)}), bf16[16,576,128]{2,1,0:T(8,128)(2,1)}, u32[]{:S(2)}, u32[]{:S(2)}) async-start(bf16[16,576,128]{2,1,0:T(8,128)(2,1)} %pad_maximum_fusion), calls=%async_computation | async-start | bytes 4718592 | tf_op jit(solution)/shard_map/all_to_all | solution.py:118
  20.8 0.0 all-gather.2.cloned.1.call-start
  20.8 0.0 copy-done.6
  20.8 1.1 copy.52.rreq_ref
  21.9 0.0 copy-done.7
  21.9 1.0 copy.53.rpos_ref
  22.9 0.1 select_reduce_fusion.2
  23.0 0.7 iota_add_fusion
  23.7 32.6 %all-to-all-done = bf16[16,576,128]{2,1,0:T(8,128)(2,1)} async-done(((bf16[16,576,128]{2,1,0:T(8,128)(2,1)}), bf16[16,576,128]{2,1,0:T(8,128)(2,1)}, u32[]{:S(2)}, u32[]{:S(2)}) %all-to-all-start) | async-done | bytes 2359328 | tf_op jit(solution)/shard_map/all_to_all | solution.py:118
  56.3 1.7 slice.20
  58.0 3.1 fusion.49
  61.1 0.7 broadcast_in_dim.18
  61.8 14.3 %shard_map.181 = bf16[1024,128]{1,0:T(8,128)(2,1)} custom-call(bf16[1024,128]{1,0:T(8,128)(2,1)} %bitcast.99, bf16[4096,128]{1,0:T(8,128)(2,1)} %bitcast.96, bf16[4096,128]{1,0:T(8,128)(2,1)} %bitcast.95, s32[1024,1]{1,0:T(8,128)} %copy.52.rreq_ref, s32[1024,1]{1,0:T(8,128)} %copy.53.rpos_ref, s32[1,4096]{1,0:T(1,128)} %bitcast.102, s32[1,4096]{1,0:T(1,128)} %bitcast.101), custom_call_target="tpu_custom_call" | custom-call | flops 2147483648 | bytes 3145728 | tf_op jit(solution)/shard_map/pallas_call | solution.py:47
  76.1 2.2 convolution_convert_fusion.1
  78.2 53.9 %all_to_all.20 = bf16[16,64,2048]{2,1,0:T(8,128)(2,1)S(1)} all-to-all(bf16[16,64,2048]{2,1,0:T(8,128)(2,1)S(1)} %bitcast.90), channel_id=1, replica_groups=mesh['req'=8,'exp'=16] {'exp'}, dimensions={0} | all-to-all | bytes 8388608 | tf_op jit(solution)/shard_map/all_to_all | solution.py:137
  132.2 0.8 convert_reduce_fusion
  133.0 0.2 copy-done.2
  133.1 0.2 multiply_reduce_fusion
  133.3 0.8 multiply_convert_fusion.1
  134.2 0.0 all-gather.2.cloned.1.call-update
  134.2 0.8 constant_dynamic-slice_fusion
  134.9 0.1 copy.54
  135.0 0.1 eq.143
  135.1 0.1 eq.130
  135.3 0.1 copy.57
  135.4 0.2 convert_reduce_fusion.1
  135.6 0.2 fusion.37
  135.9 0.2 select_reduce_fusion.1
  136.1 0.1 iota_compare_fusion
  136.2 3.9 %convolution_convert_fusion.2 = bf16[128,6,2048]{2,0,1:T(8,128)(2,1)} fusion(pred[256,6]{0,1:T(8,128)(4,1)S(1)} %iota_compare_fusion.6, pred[256,128]{1,0:T(8,128)(4,1)S(1)} %iota_compare_fusion, bf16[64,2048]{1,0:T(8,128)(2,1)} %multiply_convert_fusion.1, s32[256]{0:T(256)S(1)} %and_select_fusion), kind=kOutput, calls=%fused_computation.10 | convolution fusion | flops 228327424 | bytes 3443200 | tf_op jit(solution)/shard_map/sci,id->scd/dot_general | solution.py:185
  140.2 5.7 %copy.60 = bf16[128,6,2048]{2,1,0:T(8,128)(2,1)} copy(bf16[128,6,2048]{2,0,1:T(8,128)(2,1)} %convolution_convert_fusion.2) | data formatting | bytes 6291456 | tf_op jit(solution)/shard_map/convert_element_type | solution.py:187
  145.8 6.6 %all-to-all-start.2 = ((bf16[128,6,2048]{2,1,0:T(8,128)(2,1)}), bf16[128,6,2048]{2,1,0:T(8,128)(2,1)}, u32[]{:S(2)}, u32[]{:S(2)}) async-start(bf16[128,6,2048]{2,1,0:T(8,128)(2,1)} %copy.60), calls=%async_computation.3 | async-start | bytes 8388608 | tf_op jit(solution)/shard_map/all_to_all | solution.py:188
  152.4 0.2 reduce-scatter.2.cloned.1.call-start
  152.7 69.0 %all-gather.2.cloned.1.call-done = bf16[1024,2048]{1,0:T(8,128)(2,1)} async-done(((bf16[64,2048]{1,0:T(8,128)(2,1)}), bf16[1024,2048]{1,0:T(8,128)(2,1)}) %all-gather.2.cloned.1.call-update) | async-done | bytes 4194320 | tf_op jit(solution)/shard_map/all_gather | solution.py:146
  221.7 5.4 %fusion.50 = f32[1024,352]{0,1:T(8,128)} fusion(bf16[1024,2048]{1,0:T(8,128)(2,1)} %all-gather.2.cloned.1.call-done, bf16[2048,352]{0,1:T(8,128)(2,1)} %param.31), kind=kOutput, calls=%fused_computation.76 | convolution fusion | flops 1476395008 | bytes 7077888 | tf_op jit(solution)/shard_map/dot_general | solution.py:147
  227.1 9.0 %convolution_convert_fusion = bf16[1024,2048]{1,0:T(8,128)(2,1)} fusion(bf16[352,2048]{1,0:T(8,128)(2,1)S(1)} %copy-done, bf16[1024,2048]{1,0:T(8,128)(2,1)} %all-gather.2.cloned.1.call-done, bf16[2048,352]{0,1:T(8,128)(2,1)} %param.32, f32[1024,352]{0,1:T(8,128)} %fusion.50), kind=kOutput, calls=%fused_computation.8 | convolution fusion | flops 2957049856 | bytes 12713984 | tf_op jit(solution)/shard_map/dot_general | solution.py:150
  236.1 0.0 reduce-scatter.2.cloned.1.call-update
  236.1 0.0 all-to-all-done.2
  236.1 11.1 %fusion.2 = f32[128,6,1408]{2,0,1:T(8,128)} fusion(bf16[1,2048,1408]{2,1,0:T(8,128)(2,1)} %param.29, bf16[128,6,2048]{2,1,0:T(8,128)(2,1)} %all-to-all-done.2), kind=kOutput, calls=%fused_computation.3 | convolution fusion | flops 4429185024 | bytes 13238272 | tf_op jit(solution)/shard_map/dot_general | solution.py:14
  247.2 18.4 %fusion.8 = bf16[128,6,2048]{2,0,1:T(8,128)(2,1)} fusion(bf16[1,1408,2048]{2,1,0:T(8,128)(2,1)} %param.30, f32[128,6,1408]{2,0,1:T(8,128)} %fusion.2, bf16[1,2048,1408]{2,1,0:T(8,128)(2,1)} %param.28, bf16[128,6,2048]{2,1,0:T(8,128)(2,1)} %all-to-all-done.2), kind=kOutput, calls=%fused_computation.11 | convolution fusion | flops 8866430976 | bytes 22151168 | tf_op jit(solution)/shard_map/dot_general | solution.py:16
  265.7 5.6 %copy.63 = bf16[128,6,2048]{2,1,0:T(8,128)(2,1)} copy(bf16[128,6,2048]{2,0,1:T(8,128)(2,1)} %fusion.8) | data formatting | bytes 6291456 | tf_op jit(solution)/shard_map/convert_element_type | solution.py:16
  271.3 9.0 %all-to-all-start.3 = ((bf16[128,6,2048]{2,1,0:T(8,128)(2,1)}), bf16[128,6,2048]{2,1,0:T(8,128)(2,1)}, u32[]{:S(2)}, u32[]{:S(2)}) async-start(bf16[128,6,2048]{2,1,0:T(8,128)(2,1)} %copy.63), calls=%async_computation.4 | async-start | bytes 8388608 | tf_op jit(solution)/shard_map/all_to_all | solution.py:190
  280.3 0.0 copy-start.1
  280.3 0.1 sub.13
  280.4 0.1 eq.139
  280.5 0.0 copy-done.8
  280.6 0.1 copy.59
  280.6 0.1 copy.55
  280.7 0.1 iota_compare_fusion.1
  280.9 0.3 select_reduce_fusion
  281.2 0.0 copy-done.3
  281.2 0.2 fusion.28
  281.4 52.2 %all-to-all-done.3 = bf16[128,6,2048]{2,1,0:T(8,128)(2,1)} async-done(((bf16[128,6,2048]{2,1,0:T(8,128)(2,1)}), bf16[128,6,2048]{2,1,0:T(8,128)(2,1)}, u32[]{:S(2)}, u32[]{:S(2)}) %all-to-all-start.3) | async-done | bytes 3145760 | tf_op jit(solution)/shard_map/all_to_all | solution.py:190
  333.5 23.1 %reduce-scatter.2.cloned.1.call-done = bf16[64,2048]{1,0:T(8,128)(2,1)} async-done(((bf16[1024,2048]{1,0:T(8,128)(2,1)}), bf16[64,2048]{1,0:T(8,128)(2,1)}) %reduce-scatter.2.cloned.1.call-update) | async-done | bytes 262160 | tf_op jit(solution)/shard_map/reduce_scatter | solution.py:153
  356.6 7.7 %fusion.19 = bf16[64,2048]{1,0:T(8,128)(2,1)} fusion(f32[64,128,6]{1,0,2:T(8,128)S(1)} %select_reduce_fusion, bf16[128,6,2048]{2,1,0:T(8,128)(2,1)} %all-to-all-done.3, bf16[64,2048]{1,0:T(8,128)(2,1)} %reduce-scatter.2.cloned.1.call-done, f32[64]{0:T(128)S(1)} %fusion.28, f32[64,2048]{1,0:T(8,128)S(1)} %convert_reduce_fusion, ...), kind=kOutput, calls=%fused_computation.17 | convolution fusion | flops 1208877056 | bytes 4653312 | tf_op jit(solution)/shard_map/rsc,scd->rd/dot_general | solution.py:199
  (28 shorter events, 0.2 us)
Async XLA Ops:
  6.5 220.6 %copy-start = (bf16[352,2048]{1,0:T(8,128)(2,1)S(1)}, bf16[352,2048]{1,0:T(8,128)(2,1)}, u32[]{:S(2)}) copy-start(bf16[352,2048]{1,0:T(8,128)(2,1)} %param.33) | copy-start | bytes 4325380
  11.1 9.7 %copy-start.6 = (s32[1024]{0:T(1024)S(1)}, s32[1024]{0:T(1024)}, u32[]{:S(2)}) copy-start(s32[1024]{0:T(1024)} %param.24) | copy-start | bytes 12292
  11.1 10.7 %copy-start.7 = (s32[1024]{0:T(1024)S(1)}, s32[1024]{0:T(1024)}, u32[]{:S(2)}) copy-start(s32[1024]{0:T(1024)} %param.25) | copy-start | bytes 12292
  11.2 11.8 %copy-start.11 = (s32[4,8]{1,0:T(4,128)S(1)}, s32[4,8]{1,0:T(4,128)}, u32[]{:S(2)}) copy-start(s32[4,8]{1,0:T(4,128)} %param.23) | copy-start | bytes 388
  12.8 43.6 %all-to-all-start = ((bf16[16,576,128]{2,1,0:T(8,128)(2,1)}), bf16[16,576,128]{2,1,0:T(8,128)(2,1)}, u32[]{:S(2)}, u32[]{:S(2)}) async-start(bf16[16,576,128]{2,1,0:T(8,128)(2,1)} %pad_maximum_fusion), calls=%async_computation | async-start | bytes 4718592 | tf_op jit(solution)/shard_map/all_to_all | solution.py:118
  20.8 200.9 %all-gather.2.cloned.1.call-start = ((), (), s32[]{:S(2)}) async-start(), calls=%async_computation.5 | async-start | bytes 4456448 | tf_op jit(solution)/shard_map/all_gather | solution.py:146
  61.1 15.0 %copy-start.4 = (bf16[128,2048]{1,0:T(8,128)(2,1)S(1)}, bf16[128,2048]{1,0:T(8,128)(2,1)}, u32[]{:S(2)}) copy-start(bf16[128,2048]{1,0:T(8,128)(2,1)} %param.26) | copy-start | bytes 1572868
  132.2 1.0 copy-start.2
  132.2 1.1 copy-start.5
  132.2 3.2 copy-start.10
  145.8 90.3 %all-to-all-start.2 = ((bf16[128,6,2048]{2,1,0:T(8,128)(2,1)}), bf16[128,6,2048]{2,1,0:T(8,128)(2,1)}, u32[]{:S(2)}, u32[]{:S(2)}) async-start(bf16[128,6,2048]{2,1,0:T(8,128)(2,1)} %copy.60), calls=%async_computation.3 | async-start | bytes 8388608 | tf_op jit(solution)/shard_map/all_to_all | solution.py:188
  152.4 204.2 %reduce-scatter.2.cloned.1.call-start = ((), (), s32[]{:S(2)}) async-start(), calls=%async_computation.6 | async-start | bytes 4456448 | tf_op jit(solution)/shard_map/reduce_scatter | solution.py:153
  271.3 9.2 %copy-start.8 = (bf16[2048]{0:T(1024)(128)(2,1)S(1)}, bf16[2048]{0:T(1024)(128)(2,1)}, u32[]{:S(2)}) copy-start(bf16[2048]{0:T(1024)(128)(2,1)} %param.34) | copy-start | bytes 12292
  271.3 9.5 %copy-start.9 = (f32[64,4]{0,1:T(4,128)S(1)}, f32[64,4]{0,1:T(4,128)}, u32[]{:S(2)}) copy-start(f32[64,4]{0,1:T(4,128)} %param.37) | copy-start | bytes 3076
  271.3 9.9 %copy-start.3 = (bf16[64,2048]{1,0:T(8,128)(2,1)S(1)}, bf16[64,2048]{1,0:T(8,128)(2,1)}, u32[]{:S(2)}) copy-start(bf16[64,2048]{1,0:T(8,128)(2,1)} %multiply_convert_fusion.1) | copy-start | bytes 786436
  271.3 62.2 %all-to-all-start.3 = ((bf16[128,6,2048]{2,1,0:T(8,128)(2,1)}), bf16[128,6,2048]{2,1,0:T(8,128)(2,1)}, u32[]{:S(2)}, u32[]{:S(2)}) async-start(bf16[128,6,2048]{2,1,0:T(8,128)(2,1)} %copy.63), calls=%async_computation.4 | async-start | bytes 8388608 | tf_op jit(solution)/shard_map/all_to_all | solution.py:190
  280.3 84.0 %copy-start.1 = (bf16[352,2048]{1,0:T(8,128)(2,1)S(1)}, bf16[352,2048]{1,0:T(8,128)(2,1)}, u32[]{:S(2)}) copy-start(bf16[352,2048]{1,0:T(8,128)(2,1)} %param.33) | copy-start | bytes 4325380
Sparse Core Ops, SparseCore 0:
  134.3 87.3 all-gather.1
  236.3 120.3 reduce-scatter.1

commit v4 on v3

--- a/solution.py
+++ b/solution.py
@@ -143,7 +143,7 @@
     stream = resid.astype(jnp.float32) + mixed
     normed = rms_normed(stream, norm_gain)
 
-    piece = lax.all_gather(normed, "exp", axis=0, tiled=True)
+    piece = gather_exp(normed, exp_count)
     gate = jnp.dot(piece, shared_gate, preferred_element_type=jnp.float32)
     upper = jnp.dot(piece, shared_up, preferred_element_type=jnp.float32)
     shared_hidden = (jax.nn.silu(gate) * upper).astype(jnp.bfloat16)
@@ -188,21 +188,13 @@
     incoming = lax.all_to_all(outgoing, ("req", "exp"), split_axis=0, concat_axis=0, tiled=True)
     answered = expert_block(incoming, expert_gate[0], expert_up[0], expert_down[0])
     returned = lax.all_to_all(answered, ("req", "exp"), split_axis=0, concat_axis=0, tiled=True)
-    combine = jnp.sum(
-        jnp.where(
-            entry_of.reshape(tok_rows, TOPK, slot_count, capacity),
-            route_gate[:, :, None, None],
-            0.0,
-        ),
-        axis=1,
-    )
-    routed = jnp.einsum(
-        "rsc,scd->rd",
-        combine,
-        returned.astype(jnp.float32),
-        precision=lax.Precision.HIGHEST,
+    chosen_rows = jnp.einsum(
+        "rksc,scd->rkd",
+        entry_of.reshape(tok_rows, TOPK, slot_count, capacity).astype(jnp.bfloat16),
+        returned,
         preferred_element_type=jnp.float32,
     )
+    routed = jnp.sum(chosen_rows * route_gate[:, :, None], axis=1)
     return (stream + shared_scale[:, None] * shared_out + routed).astype(jnp.bfloat16)
 
 

time: 372 us -> 372 us (level)
  waiting for transfers between devices: 177 us -> 171 us
  starting transfers between devices: 23.9 us -> 28.9 us
    all_gather x1 -> x0, waiting for transfers between devices: 69 us -> none  [shards(): piece = lax.all_gather(normed, 'exp', axis=0, tiled=True)]
    all_to_all x0 -> x1, waiting for transfers between devices: none -> 47.3 us  [gather_exp(): got = lax.all_to_all(spread, 'exp', 0, 0, tiled=True)]
    all_to_all x1, waiting for transfers between devices: 0.01 us -> 38 us  [shards(): lax.all_to_all(outgoing, ('req', 'exp'), split_axis=0, concat_axis=0, til...]
    reduce_scatter x1, waiting for transfers between devices: 23.1 us -> 0.02 us  [shards(): lax.psum_scatter(shared_part, 'exp', scatter_dimension=0, tiled=True)]
    all_to_all x0 -> x1, starting transfers between devices: none -> 4.68 us  [gather_exp(): got = lax.all_to_all(spread, 'exp', 0, 0, tiled=True)]
  transfers between devices with their start and end apart: 5 -> 5, of which waited for: 4 -> 4; matrix products, arithmetic and copies ran while one was open for 18% -> 19% of each run, Pallas kernels for 0% -> 0%
where the time goes in v4:
time: 372 us; the launch traced here: 370 us
  waiting for transfers between devices  171 us (46%)
  matrix products  55.7 us (15%)
  blocking collectives  54 us (15%)
  starting transfers between devices  28.9 us (8%)
  local copies, waits for them, and re-layouts  26.7 us (7%)
  Pallas kernels  14.3 us (4%)
  between operations  13.7 us (4%)
  other arithmetic  6.1 us (2%)
    all_to_all x1, blocking collectives, shards(): lax.all_to_all(mixed_part.astype(jnp.bfloat16).reshape(exp_count, tok_row...  54 us
    all_to_all x1, waiting for transfers between devices, shards(): lax.all_to_all(answered, ('req', 'exp'), split_axis=0, concat_axis=0, til...  52.8 us
    all_to_all x1, waiting for transfers between devices, gather_exp(): got = lax.all_to_all(spread, 'exp', 0, 0, tiled=True)  47.3 us
    all_to_all x1, waiting for transfers between devices, shards(): lax.all_to_all(outgoing, ('req', 'exp'), split_axis=0, concat_axis=0, til...  38 us
    all_to_all x1, waiting for transfers between devices, shards(): got_cols = lax.all_to_all(by_head, 'exp', 0, 0, tiled=True)  32.7 us
    dot_general x1, matrix products, expert_block(): jnp.dot(hidden, down_w, preferred_element_type=jnp.float32)  18.7 us
    pallas_call x1, Pallas kernels, head_attention(): pl.pallas_call(head_attention_kernel, grid=(rows // tile,), out_shape=jax...  14.3 us
    dot_general x1, matrix products, expert_block(): upper = jnp.dot(rows, up_w, preferred_element_type=jnp.float32)  11.2 us
  transfers between devices with their start and end apart: 5, of which 4 were waited for; matrix products, arithmetic and copies ran while one was open for 19% of the time, Pallas kernels for 0%

profile of v4, /device:TPU:0, one launch (start us, length us, event | category | flops | bytes accessed | tf_op | source)
XLA Modules:
  0.0 370.1 jit_solution(2167601248649916919)
XLA Ops:
  6.5 0.0 copy-start
  6.5 1.6 copy.68
  8.1 1.5 copy.69
  9.6 0.0 copy-done.4
  9.6 0.1 bitcast_bitcast_fusion
  9.7 0.5 copy_bitcast_fusion
  10.2 0.0 copy-start.6
  10.2 0.0 copy-start.7
  10.2 0.0 copy-start.10
  10.3 1.6 pad_maximum_fusion
  11.8 8.0 %all-to-all-start = ((bf16[16,576,128]{2,1,0:T(8,128)(2,1)}), bf16[16,576,128]{2,1,0:T(8,128)(2,1)}, u32[]{:S(2)}, u32[]{:S(2)}) async-start(bf16[16,576,128]{2,1,0:T(8,128)(2,1)} %pad_maximum_fusion), calls=%async_computation | async-start | bytes 4718592 | tf_op jit(solution)/shard_map/all_to_all | solution.py:118
  19.9 1.1 copy.53.rreq_ref
  20.9 1.0 copy.54.rpos_ref
  22.0 0.1 select_reduce_fusion.1
  22.1 0.7 iota_add_fusion
  22.7 32.7 %all-to-all-done = bf16[16,576,128]{2,1,0:T(8,128)(2,1)} async-done(((bf16[16,576,128]{2,1,0:T(8,128)(2,1)}), bf16[16,576,128]{2,1,0:T(8,128)(2,1)}, u32[]{:S(2)}, u32[]{:S(2)}) %all-to-all-start) | async-done | bytes 2359328 | tf_op jit(solution)/shard_map/all_to_all | solution.py:118
  55.4 3.1 fusion.53
  58.5 1.7 slice.20
  60.2 0.7 broadcast_in_dim.12
  60.9 14.3 %shard_map.181 = bf16[1024,128]{1,0:T(8,128)(2,1)} custom-call(bf16[1024,128]{1,0:T(8,128)(2,1)} %bitcast.109, bf16[4096,128]{1,0:T(8,128)(2,1)} %bitcast.106, bf16[4096,128]{1,0:T(8,128)(2,1)} %bitcast.105, s32[1024,1]{1,0:T(8,128)} %copy.53.rreq_ref, s32[1024,1]{1,0:T(8,128)} %copy.54.rpos_ref, s32[1,4096]{1,0:T(1,128)} %bitcast.112, s32[1,4096]{1,0:T(1,128)} %bitcast.111), custom_call_target="tpu_custom_call" | custom-call | flops 2147483648 | bytes 3145728 | tf_op jit(solution)/shard_map/pallas_call | solution.py:47
  75.2 2.2 convolution_convert_fusion.1
  77.4 54.0 %all_to_all.25 = bf16[16,64,2048]{2,1,0:T(8,128)(2,1)S(1)} all-to-all(bf16[16,64,2048]{2,1,0:T(8,128)(2,1)S(1)} %bitcast.100), channel_id=1, replica_groups=mesh['req'=8,'exp'=16] {'exp'}, dimensions={0} | all-to-all | bytes 8388608 | tf_op jit(solution)/shard_map/all_to_all | solution.py:137
  131.4 0.8 convert_reduce_fusion
  132.1 0.2 copy-done.2
  132.3 0.2 multiply_reduce_fusion
  132.5 0.1 multiply_convert_fusion.1
  132.6 2.5 broadcast_in_dim.13
  135.1 4.7 %all-to-all-start.2 = ((bf16[16,64,2048]{2,1,0:T(8,128)(2,1)}), bf16[16,64,2048]{2,1,0:T(8,128)(2,1)}, u32[]{:S(2)}, u32[]{:S(2)}) async-start(bf16[16,64,2048]{2,1,0:T(8,128)(2,1)} %broadcast_in_dim.13), calls=%async_computation.2 | async-start | bytes 8388608 | tf_op jit(solution)/shard_map/all_to_all | solution.py:69
  139.8 0.8 constant_dynamic-slice_fusion
  140.6 0.1 copy.55
  140.7 0.1 eq.143
  140.8 0.1 eq.130
  140.9 0.1 copy.58
  141.0 0.0 copy-done.9
  141.0 0.2 convert_reduce_fusion.1
  141.2 0.2 fusion.41
  141.5 0.2 select_reduce_fusion
  141.8 0.1 iota_compare_fusion
  141.9 2.9 convolution_convert_fusion.2
  144.8 5.6 %copy.61 = bf16[128,6,2048]{2,1,0:T(8,128)(2,1)} copy(bf16[128,6,2048]{2,0,1:T(8,128)(2,1)} %convolution_convert_fusion.2) | data formatting | bytes 6291456 | tf_op jit(solution)/shard_map/convert_element_type | solution.py:187
  150.4 47.3 %all-to-all-done.2 = bf16[16,64,2048]{2,1,0:T(8,128)(2,1)} async-done(((bf16[16,64,2048]{2,1,0:T(8,128)(2,1)}), bf16[16,64,2048]{2,1,0:T(8,128)(2,1)}, u32[]{:S(2)}, u32[]{:S(2)}) %all-to-all-start.2) | async-done | bytes 4194336 | tf_op jit(solution)/shard_map/all_to_all | solution.py:69
  197.7 8.0 %all-to-all-start.3 = ((bf16[128,6,2048]{2,1,0:T(8,128)(2,1)}), bf16[128,6,2048]{2,1,0:T(8,128)(2,1)}, u32[]{:S(2)}, u32[]{:S(2)}) async-start(bf16[128,6,2048]{2,1,0:T(8,128)(2,1)} %copy.61), calls=%async_computation.4 | async-start | bytes 8388608 | tf_op jit(solution)/shard_map/all_to_all | solution.py:188
  205.7 0.2 reduce-scatter.2.cloned.1.call-start
  205.9 5.4 %fusion.54 = f32[1024,352]{0,1:T(8,128)} fusion(bf16[1024,2048]{1,0:T(8,128)(2,1)} %bitcast.12, bf16[2048,352]{0,1:T(8,128)(2,1)} %param.31), kind=kOutput, calls=%fused_computation.80 | convolution fusion | flops 1476395008 | bytes 7077888 | tf_op jit(solution)/shard_map/dot_general | solution.py:147
  211.3 9.0 %convolution_convert_fusion = bf16[1024,2048]{1,0:T(8,128)(2,1)} fusion(bf16[352,2048]{1,0:T(8,128)(2,1)S(1)} %copy-done, bf16[1024,2048]{1,0:T(8,128)(2,1)} %bitcast.12, bf16[2048,352]{0,1:T(8,128)(2,1)} %param.32, f32[1024,352]{0,1:T(8,128)} %fusion.54), kind=kOutput, calls=%fused_computation.8 | convolution fusion | flops 2957049856 | bytes 12713984 | tf_op jit(solution)/shard_map/dot_general | solution.py:150
  220.3 0.0 reduce-scatter.2.cloned.1.call-update
  220.4 38.0 %all-to-all-done.3 = bf16[128,6,2048]{2,1,0:T(8,128)(2,1)} async-done(((bf16[128,6,2048]{2,1,0:T(8,128)(2,1)}), bf16[128,6,2048]{2,1,0:T(8,128)(2,1)}, u32[]{:S(2)}, u32[]{:S(2)}) %all-to-all-start.3) | async-done | bytes 3145760 | tf_op jit(solution)/shard_map/all_to_all | solution.py:188
  258.4 11.2 %fusion.2 = f32[128,6,1408]{2,0,1:T(8,128)} fusion(bf16[1,2048,1408]{2,1,0:T(8,128)(2,1)} %param.29, bf16[128,6,2048]{2,1,0:T(8,128)(2,1)} %all-to-all-done.3), kind=kOutput, calls=%fused_computation.3 | convolution fusion | flops 4429185024 | bytes 13238272 | tf_op jit(solution)/shard_map/dot_general | solution.py:14
  269.6 18.7 %fusion.8 = bf16[128,6,2048]{2,0,1:T(8,128)(2,1)} fusion(bf16[1,1408,2048]{2,1,0:T(8,128)(2,1)} %param.30, f32[128,6,1408]{2,0,1:T(8,128)} %fusion.2, bf16[1,2048,1408]{2,1,0:T(8,128)(2,1)} %param.28, bf16[128,6,2048]{2,1,0:T(8,128)(2,1)} %all-to-all-done.3), kind=kOutput, calls=%fused_computation.11 | convolution fusion | flops 8866430976 | bytes 22151168 | tf_op jit(solution)/shard_map/dot_general | solution.py:16
  288.2 5.6 %copy.64 = bf16[128,6,2048]{2,1,0:T(8,128)(2,1)} copy(bf16[128,6,2048]{2,0,1:T(8,128)(2,1)} %fusion.8) | data formatting | bytes 6291456 | tf_op jit(solution)/shard_map/convert_element_type | solution.py:16
  293.8 8.0 %all-to-all-start.4 = ((bf16[128,6,2048]{2,1,0:T(8,128)(2,1)}), bf16[128,6,2048]{2,1,0:T(8,128)(2,1)}, u32[]{:S(2)}, u32[]{:S(2)}) async-start(bf16[128,6,2048]{2,1,0:T(8,128)(2,1)} %copy.64), calls=%async_computation.5 | async-start | bytes 8388608 | tf_op jit(solution)/shard_map/all_to_all | solution.py:190
  301.8 0.1 eq.139
  302.0 0.1 sub.13
  302.1 0.1 copy.56
  302.1 0.1 copy.60
  302.3 0.1 iota_compare_fusion.1
  302.4 0.0 copy-start.1
  302.4 0.2 fusion.29
  302.5 52.8 %all-to-all-done.4 = bf16[128,6,2048]{2,1,0:T(8,128)(2,1)} async-done(((bf16[128,6,2048]{2,1,0:T(8,128)(2,1)}), bf16[128,6,2048]{2,1,0:T(8,128)(2,1)}, u32[]{:S(2)}, u32[]{:S(2)}) %all-to-all-start.4) | async-done | bytes 3145760 | tf_op jit(solution)/shard_map/all_to_all | solution.py:190
  355.3 0.0 copy-done.11
  355.3 6.1 %fusion.22 = f32[64,2048]{1,0:T(8,128)S(1)} fusion(bf16[128,6,2048]{2,1,0:T(8,128)(2,1)} %all-to-all-done.4, f32[64,4]{0,1:T(4,128)S(1)} %copy-done.11, pred[64,4,6]{0,2,1:T(8,128)(4,1)S(1)} %iota_compare_fusion.4, pred[64,4,128]{2,0,1:T(8,128)(4,1)S(1)} %iota_compare_fusion.1), kind=kOutput, calls=%fused_computation.21 | convolution fusion | flops 806420480 | bytes 3705344 | tf_op jit(solution)/shard_map/rksc,scd->rkd/dot_general | solution.py:191
  361.4 0.0 reduce-scatter.2.cloned.1.call-done
  361.5 1.8 add_convert_fusion
  363.3 0.0 copy-done.1
  (28 shorter events, 0.2 us)
Async XLA Ops:
  6.5 204.8 %copy-start = (bf16[352,2048]{1,0:T(8,128)(2,1)S(1)}, bf16[352,2048]{1,0:T(8,128)(2,1)}, u32[]{:S(2)}) copy-start(bf16[352,2048]{1,0:T(8,128)(2,1)} %param.33) | copy-start | bytes 4325380
  6.5 3.1 copy-start.4
  10.2 9.6 %copy-start.6 = (s32[1024]{0:T(1024)S(1)}, s32[1024]{0:T(1024)}, u32[]{:S(2)}) copy-start(s32[1024]{0:T(1024)} %param.24) | copy-start | bytes 12292
  10.2 10.7 %copy-start.7 = (s32[1024]{0:T(1024)S(1)}, s32[1024]{0:T(1024)}, u32[]{:S(2)}) copy-start(s32[1024]{0:T(1024)} %param.25) | copy-start | bytes 12292
  10.2 11.7 %copy-start.10 = (s32[4,8]{1,0:T(4,128)S(1)}, s32[4,8]{1,0:T(4,128)}, u32[]{:S(2)}) copy-start(s32[4,8]{1,0:T(4,128)} %param.23) | copy-start | bytes 388
  11.8 43.6 %all-to-all-start = ((bf16[16,576,128]{2,1,0:T(8,128)(2,1)}), bf16[16,576,128]{2,1,0:T(8,128)(2,1)}, u32[]{:S(2)}, u32[]{:S(2)}) async-start(bf16[16,576,128]{2,1,0:T(8,128)(2,1)} %pad_maximum_fusion), calls=%async_computation | async-start | bytes 4718592 | tf_op jit(solution)/shard_map/all_to_all | solution.py:118
  58.5 16.7 %copy-start.3 = (bf16[128,2048]{1,0:T(8,128)(2,1)S(1)}, bf16[128,2048]{1,0:T(8,128)(2,1)}, u32[]{:S(2)}) copy-start(bf16[128,2048]{1,0:T(8,128)(2,1)} %param.26) | copy-start | bytes 1572868
  131.4 1.0 copy-start.2
  131.4 1.1 copy-start.5
  135.1 5.9 %copy-start.9 = (s32[128]{0:T(128)S(1)}, s32[128]{0:T(128)}, u32[]{:S(2)}) copy-start(s32[128]{0:T(128)} %param.35) | copy-start | bytes 1540
  135.1 62.5 %all-to-all-start.2 = ((bf16[16,64,2048]{2,1,0:T(8,128)(2,1)}), bf16[16,64,2048]{2,1,0:T(8,128)(2,1)}, u32[]{:S(2)}, u32[]{:S(2)}) async-start(bf16[16,64,2048]{2,1,0:T(8,128)(2,1)} %broadcast_in_dim.13), calls=%async_computation.2 | async-start | bytes 8388608 | tf_op jit(solution)/shard_map/all_to_all | solution.py:69
  197.7 60.7 %all-to-all-start.3 = ((bf16[128,6,2048]{2,1,0:T(8,128)(2,1)}), bf16[128,6,2048]{2,1,0:T(8,128)(2,1)}, u32[]{:S(2)}, u32[]{:S(2)}) async-start(bf16[128,6,2048]{2,1,0:T(8,128)(2,1)} %copy.61), calls=%async_computation.4 | async-start | bytes 8388608 | tf_op jit(solution)/shard_map/all_to_all | solution.py:188
  205.7 155.8 %reduce-scatter.2.cloned.1.call-start = ((), (), s32[]{:S(2)}) async-start(), calls=%async_computation.6 | async-start | bytes 4456448 | tf_op jit(solution)/shard_map/reduce_scatter | solution.py:153
  293.8 8.4 %copy-start.8 = (bf16[2048]{0:T(1024)(128)(2,1)S(1)}, bf16[2048]{0:T(1024)(128)(2,1)}, u32[]{:S(2)}) copy-start(bf16[2048]{0:T(1024)(128)(2,1)} %param.34) | copy-start | bytes 12292
  293.8 61.5 %copy-start.11 = (f32[64,4]{0,1:T(4,128)S(1)}, f32[64,4]{0,1:T(4,128)}, u32[]{:S(2)}) copy-start(f32[64,4]{0,1:T(4,128)} %param.37) | copy-start | bytes 3076
  293.8 61.5 %all-to-all-start.4 = ((bf16[128,6,2048]{2,1,0:T(8,128)(2,1)}), bf16[128,6,2048]{2,1,0:T(8,128)(2,1)}, u32[]{:S(2)}, u32[]{:S(2)}) async-start(bf16[128,6,2048]{2,1,0:T(8,128)(2,1)} %copy.64), calls=%async_computation.5 | async-start | bytes 8388608 | tf_op jit(solution)/shard_map/all_to_all | solution.py:190
  302.4 60.9 %copy-start.1 = (bf16[352,2048]{1,0:T(8,128)(2,1)S(1)}, bf16[352,2048]{1,0:T(8,128)(2,1)}, u32[]{:S(2)}) copy-start(bf16[352,2048]{1,0:T(8,128)(2,1)} %param.33) | copy-start | bytes 4325380
Sparse Core Ops, SparseCore 0:
  220.5 134.3 reduce-scatter.1

commit v5 on v2

--- a/solution.py
+++ b/solution.py
@@ -2,6 +2,7 @@
 import jax.numpy as jnp
 from jax import lax
 from jax.experimental import pallas as pl
+from jax.experimental.pallas import tpu as pltpu
 from jax.sharding import PartitionSpec as P
 
 HEADS = 16
@@ -21,46 +22,80 @@
     return (stream * scale_row * norm_gain[None, :]).astype(jnp.bfloat16)
 
 
-def head_attention_kernel(q_ref, k_ref, v_ref, rreq_ref, rpos_ref, kreq_ref, kpos_ref, o_ref):
-    scores = lax.dot_general(
-        q_ref[...], k_ref[...], (((1,), (1,)), ((), ())), preferred_element_type=jnp.float32
-    ) * HEAD_DIM ** (-0.5)
-    visible = (rreq_ref[...] == kreq_ref[...]) & (kpos_ref[...] <= rpos_ref[...])
-    scores = jnp.where(visible, scores, -1e30)
-    top = jnp.max(scores, axis=1, keepdims=True)
-    weights = jnp.where(visible, jnp.exp(scores - top), 0.0)
-    denominators = jnp.sum(weights, axis=1, keepdims=True)
-    numerators = jnp.dot(
-        weights.astype(jnp.bfloat16), v_ref[...], preferred_element_type=jnp.float32
-    )
-    o_ref[...] = (numerators / denominators).astype(o_ref.dtype)
-
-
-def head_attention(query_cols, key_cols, value_cols, row_request, row_position, key_request, key_position):
+def head_attention_kernel(lo_ref, hi_ref, q_ref, k_ref, v_ref, first_ref, last_ref, o_ref):
+    tile = pl.program_id(0)
+    block = 128
+    query = q_ref[...]
+    first = first_ref[...]
+    last = last_ref[...]
+
+    def scores_of(b):
+        start = pl.multiple_of(b * block, block)
+        keys = k_ref[pl.ds(start, block), :]
+        scores = lax.dot_general(
+            query, keys, (((1,), (1,)), ((), ())), preferred_element_type=jnp.float32
+        ) * HEAD_DIM ** (-0.5)
+        index = start + lax.broadcasted_iota(jnp.int32, (1, block), 1)
+        visible = (index >= first) & (index <= last)
+        return jnp.where(visible, scores, -1e30), visible
+
+    def top_step(b, top):
+        return jnp.maximum(top, jnp.max(scores_of(b)[0], axis=1, keepdims=True))
+
+    rows = query.shape[0]
+    top = lax.fori_loop(
+        lo_ref[tile], hi_ref[tile] + 1, top_step, jnp.full((rows, 1), -1e30, jnp.float32)
+    )
+
+    def sum_step(b, carry):
+        den, num = carry
+        scores, visible = scores_of(b)
+        weights = jnp.where(visible, jnp.exp(scores - top), 0.0)
+        start = pl.multiple_of(b * block, block)
+        num = num + jnp.dot(
+            weights.astype(jnp.bfloat16), v_ref[pl.ds(start, block), :],
+            preferred_element_type=jnp.float32,
+        )
+        return den + jnp.sum(weights, axis=1, keepdims=True), num
+
+    den, num = lax.fori_loop(
+        lo_ref[tile],
+        hi_ref[tile] + 1,
+        sum_step,
+        (jnp.zeros((rows, 1), jnp.float32), jnp.zeros((rows, HEAD_DIM), jnp.float32)),
+    )
+    o_ref[...] = (num / den).astype(o_ref.dtype)
+
+
+def head_attention(query_cols, key_cols, value_cols, first_key, last_key):
     rows, width = query_cols.shape
     keys = key_cols.shape[0]
     tile = 128
-    row_spec = pl.BlockSpec((tile, width), lambda i: (i, 0))
-    whole = pl.BlockSpec((keys, width), lambda i: (0, 0))
-    row_int = pl.BlockSpec((tile, 1), lambda i: (i, 0))
-    key_int = pl.BlockSpec((1, keys), lambda i: (0, 0))
+    lo = jnp.min(first_key.reshape(rows // tile, tile), axis=1) // 128
+    hi = jnp.max(last_key.reshape(rows // tile, tile), axis=1) // 128
+    row_spec = pl.BlockSpec((tile, width), lambda i, lo_ref, hi_ref: (i, 0))
+    whole = pl.BlockSpec((keys, width), lambda i, lo_ref, hi_ref: (0, 0))
+    row_int = pl.BlockSpec((tile, 1), lambda i, lo_ref, hi_ref: (i, 0))
     return pl.pallas_call(
         head_attention_kernel,
-        grid=(rows // tile,),
+        grid_spec=pltpu.PrefetchScalarGridSpec(
+            num_scalar_prefetch=2,
+            grid=(rows // tile,),
+            in_specs=[row_spec, whole, whole, row_int, row_int],
+            out_specs=row_spec,
+        ),
         out_shape=jax.ShapeDtypeStruct((rows, width), jnp.bfloat16),
-        in_specs=[row_spec, whole, whole, row_int, row_int, key_int, key_int],
-        out_specs=row_spec,
         cost_estimate=pl.CostEstimate(
-            flops=4 * rows * keys * width, transcendentals=rows * keys, bytes_accessed=3 * keys * width * 2
+            flops=rows * keys * width, transcendentals=rows * keys // 4, bytes_accessed=3 * keys * width * 2
         ),
     )(
+        lo.astype(jnp.int32),
+        hi.astype(jnp.int32),
         query_cols,
         key_cols,
         value_cols,
-        row_request.reshape(rows, 1),
-        row_position.reshape(rows, 1),
-        key_request.reshape(1, keys),
-        key_position.reshape(1, keys),
+        first_key.reshape(rows, 1),
+        last_key.reshape(rows, 1),
     )
 
 
@@ -119,18 +154,22 @@
     query_cols = got_cols[:, :tok_rows].reshape(group_rows, HEAD_DIM)
     key_cols = got_cols[:, tok_rows:tok_rows + key_count].reshape(group_keys, HEAD_DIM)
     value_cols = got_cols[:, tok_rows + key_count:].reshape(group_keys, HEAD_DIM)
-    page_ids = jnp.arange(exp_count * pages_here, dtype=jnp.int32)
-    hits = (page_table[None, :, :] == page_ids[:, None, None]).astype(jnp.int32)
-    page_request = jnp.sum(
-        hits * jnp.arange(req_slots, dtype=jnp.int32)[None, :, None], axis=(1, 2)
-    )
-    page_slot = jnp.sum(hits * jnp.arange(max_pages, dtype=jnp.int32)[None, None, :], axis=(1, 2))
-    key_position = (
-        page_slot[:, None] * page_len + jnp.arange(page_len, dtype=jnp.int32)[None, :]
-    ).reshape(-1)
-    key_request = jnp.repeat(page_request, page_len)
+    group_pages = exp_count * pages_here
+    page_order = page_table.reshape(-1)
+    pick_page = (
+        page_order[:, None] == jnp.arange(group_pages, dtype=jnp.int32)[None, :]
+    ).astype(jnp.bfloat16)
+    sorted_keys = jnp.dot(
+        pick_page, key_cols.reshape(group_pages, page_len * HEAD_DIM),
+        preferred_element_type=jnp.float32,
+    ).astype(jnp.bfloat16).reshape(group_keys, HEAD_DIM)
+    sorted_values = jnp.dot(
+        pick_page, value_cols.reshape(group_pages, page_len * HEAD_DIM),
+        preferred_element_type=jnp.float32,
+    ).astype(jnp.bfloat16).reshape(group_keys, HEAD_DIM)
+    first_key = row_request * (max_pages * page_len)
     attention = head_attention(
-        query_cols, key_cols, value_cols, row_request, row_position, key_request, key_position
+        query_cols, sorted_keys, sorted_values, first_key, first_key + row_position
     )
     mixed_part = jnp.dot(attention, out_proj, preferred_element_type=jnp.float32)
     mixed = jnp.sum(

time: 362 us -> 387 us (1.069)
  Pallas kernels: 14.3 us -> 33.1 us
    pallas_call x1, Pallas kernels: 14.3 us -> 33.1 us  [head_attention(): pl.pallas_call(head_attention_kernel, grid_spec=pltpu.PrefetchScalarGridS...]
  transfers between devices with their start and end apart: 5 -> 5, of which waited for: 4 -> 4; matrix products, arithmetic and copies ran while one was open for 25% -> 23% of each run, Pallas kernels for 0% -> 0%
where the time goes in v5:
time: 387 us; the launch traced here: 385 us
  waiting for transfers between devices  146 us (38%)
  blocking collectives  56.5 us (15%)
  local copies, waits for them, and re-layouts  56.4 us (15%)
  matrix products  43.9 us (11%)
  Pallas kernels  33.1 us (9%)
  starting transfers between devices  24.9 us (6%)
  between operations  13.7 us (4%)
  other arithmetic  10.1 us (3%)
    all_gather x1, waiting for transfers between devices, shards(): piece = lax.all_gather(normed, 'exp', axis=0, tiled=True)  62.7 us
    all_to_all x1, blocking collectives, shards(): lax.all_to_all(mixed_part.astype(jnp.bfloat16).reshape(exp_count, tok_row...  56.5 us
    all_to_all x1, waiting for transfers between devices, shards(): lax.all_to_all(answered, ('req', 'exp'), split_axis=0, concat_axis=0, til...  50.5 us
    pallas_call x1, Pallas kernels, head_attention(): pl.pallas_call(head_attention_kernel, grid_spec=pltpu.PrefetchScalarGridS...  33.1 us
    all_to_all x1, waiting for transfers between devices, shards(): got_cols = lax.all_to_all(by_head, 'exp', 0, 0, tiled=True)  32.6 us
    dot_general x1, matrix products, expert_block(): jnp.dot(hidden, down_w, preferred_element_type=jnp.float32)  17 us
    all_to_all x1, starting transfers between devices, shards(): lax.all_to_all(answered, ('req', 'exp'), split_axis=0, concat_axis=0, til...  10.6 us
    dot_general x1, matrix products, expert_block(): upper = jnp.dot(rows, up_w, preferred_element_type=jnp.float32)  9.66 us
  transfers between devices with their start and end apart: 5, of which 4 were waited for; matrix products, arithmetic and copies ran while one was open for 23% of the time, Pallas kernels for 0%

profile of v5, /device:TPU:0, one launch (start us, length us, event | category | flops | bytes accessed | tf_op | source)
XLA Modules:
  0.0 384.9 jit_solution(9265833432823006273)
XLA Ops:
  6.5 1.6 copy.45
  8.1 1.5 copy.46
  9.6 0.1 bitcast_bitcast_fusion
  9.7 0.5 copy_bitcast_fusion
  10.2 1.6 pad_maximum_fusion
  11.8 8.1 %all-to-all-start = ((bf16[16,576,128]{2,1,0:T(8,128)(2,1)}), bf16[16,576,128]{2,1,0:T(8,128)(2,1)}, u32[]{:S(2)}, u32[]{:S(2)}) async-start(bf16[16,576,128]{2,1,0:T(8,128)(2,1)} %pad_maximum_fusion), calls=%async_computation | async-start | bytes 4718592 | tf_op jit(solution)/shard_map/all_to_all | solution.py:153
  20.0 0.0 all-gather.2.cloned.1.call-start
  20.0 0.1 eq.64
  20.1 0.1 bitcast_reduce_fusion
  20.2 1.0 copy.38.last_ref
  21.3 1.1 copy.37.first_ref
  22.4 0.6 and_select_fusion
  22.9 32.6 %all-to-all-done = bf16[16,576,128]{2,1,0:T(8,128)(2,1)} async-done(((bf16[16,576,128]{2,1,0:T(8,128)(2,1)}), bf16[16,576,128]{2,1,0:T(8,128)(2,1)}, u32[]{:S(2)}, u32[]{:S(2)}) %all-to-all-start) | async-done | bytes 2359328 | tf_op jit(solution)/shard_map/all_to_all | solution.py:153
  55.5 2.7 fusion.33
  58.3 0.5 reshape_reshape.6
  58.7 0.5 convolution_convert_fusion.1
  59.2 1.3 reshape.129.k_ref
  60.5 1.5 reshape_reshape.7
  62.1 0.5 convolution_convert_fusion
  62.5 0.0 copy-start.5
  62.5 1.3 reshape.130.v_ref
  63.9 1.7 slice.22
  65.5 33.1 %shard_map.181 = bf16[1024,128]{1,0:T(8,128)(2,1)} custom-call(s32[8]{0:T(128)} %get-tuple-element.15.lo_ref, s32[8]{0:T(128)} %get-tuple-element.14.hi_ref, bf16[1024,128]{1,0:T(8,128)(2,1)} %bitcast.81, bf16[4096,128]{1,0:T(8,128)(2,1)} %reshape.129.k_ref, bf16[4096,128]{1,0:T(8,128)(2,1)} %reshape.130.v_ref, s32[1024,1]{1,0:T(8,128)} %copy.37.first_ref, ...), custom_call_target="tpu_custom_call" | custom-call | flops 536870912 | bytes 3145728 | tf_op jit(solution)/shard_map/pallas_call | solution.py:79
  98.7 2.2 convolution_convert_fusion.3
  100.9 56.5 %all_to_all.20 = bf16[16,64,2048]{2,1,0:T(8,128)(2,1)S(1)} all-to-all(bf16[16,64,2048]{2,1,0:T(8,128)(2,1)S(1)} %bitcast.76), channel_id=1, replica_groups=mesh['req'=8,'exp'=16] {'exp'}, dimensions={0} | all-to-all | bytes 8388608 | tf_op jit(solution)/shard_map/all_to_all | solution.py:176
  157.4 0.8 convert_reduce_fusion
  158.2 0.2 copy-done.4
  158.3 0.2 multiply_reduce_fusion.1
  158.5 0.6 copy-done.2
  159.2 0.8 multiply_convert_fusion.1
  160.0 0.0 all-gather.2.cloned.1.call-update
  160.0 0.8 constant_dynamic-slice_fusion
  160.8 0.1 copy.39
  160.9 0.1 eq.77
  161.0 0.1 eq.68
  161.1 0.1 copy.41
  161.2 0.2 convert_reduce_fusion.1
  161.4 0.2 fusion.21
  161.7 0.2 select_reduce_fusion
  161.9 1.4 broadcast_in_dim.19
  163.4 0.3 reshape.153
  163.7 4.3 %scatter_custom_fusion = bf16[768,2048]{1,0:T(8,128)(2,1)} fusion(s32[256]{0:T(256)S(1)} %bitcast.87, bf16[256,2048]{1,0:T(8,128)(2,1)S(1)} %reshape.153, bf16[]{:T(256)} %constant.63.clone.1), kind=kCustom, calls=%fused_computation.17 | custom fusion | bytes 3145730 | tf_op jit(solution)/shard_map/scatter | solution.py:217
  168.0 6.3 %reshape.136 = bf16[128,6,2048]{2,1,0:T(8,128)(2,1)} reshape(bf16[768,2048]{1,0:T(8,128)(2,1)} %scatter_custom_fusion) | data formatting | bytes 6291456 | tf_op jit(solution)/shard_map/reshape | solution.py:219
  174.2 6.0 %all-to-all-start.2 = ((bf16[128,6,2048]{2,1,0:T(8,128)(2,1)}), bf16[128,6,2048]{2,1,0:T(8,128)(2,1)}, u32[]{:S(2)}, u32[]{:S(2)}) async-start(bf16[128,6,2048]{2,1,0:T(8,128)(2,1)} %reshape.136), calls=%async_computation.3 | async-start | bytes 8388608 | tf_op jit(solution)/shard_map/all_to_all | solution.py:220
  180.2 0.2 reduce-scatter.2.cloned.1.call-start
  180.4 62.7 %all-gather.2.cloned.1.call-done = bf16[1024,2048]{1,0:T(8,128)(2,1)} async-done(((bf16[64,2048]{1,0:T(8,128)(2,1)}), bf16[1024,2048]{1,0:T(8,128)(2,1)}) %all-gather.2.cloned.1.call-update) | async-done | bytes 4194320 | tf_op jit(solution)/shard_map/all_gather | solution.py:185
  243.2 5.0 %fusion.34 = f32[1024,352]{0,1:T(8,128)} fusion(bf16[1024,2048]{1,0:T(8,128)(2,1)} %all-gather.2.cloned.1.call-done, bf16[2048,352]{0,1:T(8,128)(2,1)S(1)} %copy-done.14), kind=kOutput, calls=%fused_computation.72 | convolution fusion | flops 1476395008 | bytes 7077888 | tf_op jit(solution)/shard_map/dot_general | solution.py:186
  248.2 9.0 %convolution_convert_fusion.2 = bf16[1024,2048]{1,0:T(8,128)(2,1)} fusion(bf16[352,2048]{1,0:T(8,128)(2,1)S(1)} %copy-done, bf16[1024,2048]{1,0:T(8,128)(2,1)} %all-gather.2.cloned.1.call-done, bf16[2048,352]{0,1:T(8,128)(2,1)} %param.32, f32[1024,352]{0,1:T(8,128)} %fusion.34), kind=kOutput, calls=%fused_computation.12 | convolution fusion | flops 2957049856 | bytes 12713984 | tf_op jit(solution)/shard_map/dot_general | solution.py:189
  257.2 0.0 reduce-scatter.2.cloned.1.call-update
  257.2 0.0 all-to-all-done.2
  257.2 6.3 %reshape.137 = bf16[768,2048]{1,0:T(8,128)(2,1)} reshape(bf16[128,6,2048]{2,1,0:T(8,128)(2,1)} %all-to-all-done.2) | data formatting | bytes 6291456 | tf_op jit(solution)/shard_map/reshape | solution.py:222
  263.5 9.7 %fusion.2 = f32[768,1408]{1,0:T(8,128)} fusion(bf16[768,2048]{1,0:T(8,128)(2,1)} %reshape.137, bf16[1,2048,1408]{2,1,0:T(8,128)(2,1)} %param.29), kind=kOutput, calls=%fused_computation.7 | convolution fusion | flops 4429185024 | bytes 13238272 | tf_op jit(solution)/shard_map/dot_general | solution.py:15
  273.2 17.0 %fusion.8 = bf16[768,2048]{1,0:T(8,128)(2,1)} fusion(bf16[1,1408,2048]{2,1,0:T(8,128)(2,1)} %param.30, f32[768,1408]{1,0:T(8,128)} %fusion.2, bf16[768,2048]{1,0:T(8,128)(2,1)} %reshape.137, bf16[1,2048,1408]{2,1,0:T(8,128)(2,1)} %param.28), kind=kOutput, calls=%fused_computation.14 | convolution fusion | flops 8866430976 | bytes 22151168 | tf_op jit(solution)/shard_map/dot_general | solution.py:17
  290.2 6.3 %reshape.138 = bf16[128,6,2048]{2,1,0:T(8,128)(2,1)} reshape(bf16[768,2048]{1,0:T(8,128)(2,1)} %fusion.8) | data formatting | bytes 6291456 | tf_op jit(solution)/shard_map/reshape | solution.py:223
  296.5 10.6 %all-to-all-start.3 = ((bf16[128,6,2048]{2,1,0:T(8,128)(2,1)}), bf16[128,6,2048]{2,1,0:T(8,128)(2,1)}, u32[]{:S(2)}, u32[]{:S(2)}) async-start(bf16[128,6,2048]{2,1,0:T(8,128)(2,1)} %reshape.138), calls=%async_computation.4 | async-start | bytes 8388608 | tf_op jit(solution)/shard_map/all_to_all | solution.py:224
  307.1 0.7 copy.43
  307.8 0.2 fusion.17
  308.0 50.5 %all-to-all-done.3 = bf16[128,6,2048]{2,1,0:T(8,128)(2,1)} async-done(((bf16[128,6,2048]{2,1,0:T(8,128)(2,1)}), bf16[128,6,2048]{2,1,0:T(8,128)(2,1)}, u32[]{:S(2)}, u32[]{:S(2)}) %all-to-all-start.3) | async-done | bytes 3145760 | tf_op jit(solution)/shard_map/all_to_all | solution.py:224
  358.5 6.3 %reshape.139 = bf16[768,2048]{1,0:T(8,128)(2,1)} reshape(bf16[128,6,2048]{2,1,0:T(8,128)(2,1)} %all-to-all-done.3) | data formatting | bytes 6291456 | tf_op jit(solution)/shard_map/reshape | solution.py:226
  364.9 5.8 %gather_fusion = bf16[256,2048]{1,0:T(8,128)(2,1)} fusion(bf16[768,2048]{1,0:T(8,128)(2,1)} %reshape.139, s32[1024]{0:T(1024)S(1)} %pad_clamp_fusion), kind=kCustom, calls=%fused_computation | custom fusion | bytes 2098176 | tf_op jit(solution)/shard_map/gather | solution.py:227
  370.6 1.7 reshape.140
  372.4 3.1 multiply_reduce_fusion
  375.5 0.4 reduce-scatter.2.cloned.1.call-done
  375.9 2.2 add_convert_fusion
  (40 shorter events, 0.2 us)
Async XLA Ops:
  6.5 241.6 %copy-start = (bf16[352,2048]{1,0:T(8,128)(2,1)S(1)}, bf16[352,2048]{1,0:T(8,128)(2,1)}, u32[]{:S(2)}) copy-start(bf16[352,2048]{1,0:T(8,128)(2,1)} %param.33) | copy-start | bytes 4325380
  6.5 3.1 copy-start.6
  11.8 8.2 %copy-start.13 = (s32[4,8]{1,0:T(4,128)S(1)}, s32[4,8]{1,0:T(4,128)}, u32[]{:S(2)}) copy-start(s32[4,8]{1,0:T(4,128)} %param.23) | copy-start | bytes 388
  11.8 8.3 %copy-start.7 = (s32[1024]{0:T(1024)S(1)}, s32[1024]{0:T(1024)}, u32[]{:S(2)}) copy-start(s32[1024]{0:T(1024)} %param.24) | copy-start | bytes 12292
  11.8 8.3 %copy-start.10 = (s32[1024]{0:T(1024)S(1)}, s32[1024]{0:T(1024)}, u32[]{:S(2)}) copy-start(s32[1024]{0:T(1024)} %param.25) | copy-start | bytes 12292
  11.8 43.7 %all-to-all-start = ((bf16[16,576,128]{2,1,0:T(8,128)(2,1)}), bf16[16,576,128]{2,1,0:T(8,128)(2,1)}, u32[]{:S(2)}, u32[]{:S(2)}) async-start(bf16[16,576,128]{2,1,0:T(8,128)(2,1)} %pad_maximum_fusion), calls=%async_computation | async-start | bytes 4718592 | tf_op jit(solution)/shard_map/all_to_all | solution.py:153
  20.0 223.2 %all-gather.2.cloned.1.call-start = ((), (), s32[]{:S(2)}) async-start(), calls=%async_computation.5 | async-start | bytes 4456448 | tf_op jit(solution)/shard_map/all_gather | solution.py:185
  62.5 36.1 %copy-start.5 = (bf16[128,2048]{1,0:T(8,128)(2,1)S(1)}, bf16[128,2048]{1,0:T(8,128)(2,1)}, u32[]{:S(2)}) copy-start(bf16[128,2048]{1,0:T(8,128)(2,1)} %param.26) | copy-start | bytes 1572868
  157.4 1.0 copy-start.4
  157.4 1.8 copy-start.8
  157.4 3.8 copy-start.11
  158.3 0.8 copy-start.2
  174.2 68.9 %copy-start.14 = (bf16[2048,352]{0,1:T(8,128)(2,1)S(1)}, bf16[2048,352]{0,1:T(8,128)(2,1)}, u32[]{:S(2)}) copy-start(bf16[2048,352]{0,1:T(8,128)(2,1)} %param.31) | copy-start | bytes 4325380
  174.2 82.9 %all-to-all-start.2 = ((bf16[128,6,2048]{2,1,0:T(8,128)(2,1)}), bf16[128,6,2048]{2,1,0:T(8,128)(2,1)}, u32[]{:S(2)}, u32[]{:S(2)}) async-start(bf16[128,6,2048]{2,1,0:T(8,128)(2,1)} %reshape.136), calls=%async_computation.3 | async-start | bytes 8388608 | tf_op jit(solution)/shard_map/all_to_all | solution.py:220
  180.2 195.7 %reduce-scatter.2.cloned.1.call-start = ((), (), s32[]{:S(2)}) async-start(), calls=%async_computation.6 | async-start | bytes 4456448 | tf_op jit(solution)/shard_map/reduce_scatter | solution.py:192
  296.5 10.6 %copy-start.12 = (f32[64,4]{0,1:T(4,128)S(1)}, f32[64,4]{0,1:T(4,128)}, u32[]{:S(2)}) copy-start(f32[64,4]{0,1:T(4,128)} %param.37) | copy-start | bytes 3076
  296.5 11.3 %copy-start.9 = (bf16[2048]{0:T(1024)(128)(2,1)S(1)}, bf16[2048]{0:T(1024)(128)(2,1)}, u32[]{:S(2)}) copy-start(bf16[2048]{0:T(1024)(128)(2,1)} %param.34) | copy-start | bytes 12292
  296.5 11.3 %copy-start.3 = (bf16[64,2048]{1,0:T(8,128)(2,1)S(1)}, bf16[64,2048]{1,0:T(8,128)(2,1)}, u32[]{:S(2)}) copy-start(bf16[64,2048]{1,0:T(8,128)(2,1)} %multiply_convert_fusion.1) | copy-start | bytes 786436
  296.5 62.0 %all-to-all-start.3 = ((bf16[128,6,2048]{2,1,0:T(8,128)(2,1)}), bf16[128,6,2048]{2,1,0:T(8,128)(2,1)}, u32[]{:S(2)}, u32[]{:S(2)}) async-start(bf16[128,6,2048]{2,1,0:T(8,128)(2,1)} %reshape.138), calls=%async_computation.4 | async-start | bytes 8388608 | tf_op jit(solution)/shard_map/all_to_all | solution.py:224
  364.9 13.2 %copy-start.1 = (bf16[352,2048]{1,0:T(8,128)(2,1)S(1)}, bf16[352,2048]{1,0:T(8,128)(2,1)}, u32[]{:S(2)}) copy-start(bf16[352,2048]{1,0:T(8,128)(2,1)} %param.33) | copy-start | bytes 4325380
Sparse Core Ops, SparseCore 0:
  160.1 83.0 all-gather.1
  257.3 118.5 reduce-scatter.1

commit v6 on v2

--- a/solution.py
+++ b/solution.py
@@ -105,6 +105,7 @@
     max_pages = page_table.shape[1]
     capacity = 3 * tok_rows * TOPK // slot_count
 
+    whole_proj = lax.all_gather(out_proj, "exp", axis=0, tiled=True)
     key_count = pages_here * page_len
     group_keys = exp_count * key_count
     by_head = jnp.concatenate(
@@ -132,14 +133,11 @@
     attention = head_attention(
         query_cols, key_cols, value_cols, row_request, row_position, key_request, key_position
     )
-    mixed_part = jnp.dot(attention, out_proj, preferred_element_type=jnp.float32)
-    mixed = jnp.sum(
-        lax.all_to_all(
-            mixed_part.astype(jnp.bfloat16).reshape(exp_count, tok_rows, model_width),
-            "exp", 0, 0, tiled=True,
-        ).astype(jnp.float32),
-        axis=0,
-    )
+    attention_rows = lax.all_to_all(
+        attention.reshape(exp_count, tok_rows, HEAD_DIM), "exp", 0, 0, tiled=True
+    )
+    attention_rows = attention_rows.transpose(1, 0, 2).reshape(tok_rows, model_width)
+    mixed = jnp.dot(attention_rows, whole_proj, preferred_element_type=jnp.float32)
     stream = resid.astype(jnp.float32) + mixed
     normed = rms_normed(stream, norm_gain)
 

time: 362 us -> 343 us (0.948)
  blocking collectives: 54 us -> 15.7 us
  waiting for transfers between devices: 147 us -> 164 us
    all_to_all x1, blocking collectives: 54 us -> 15.7 us  [shards(): lax.all_to_all(attention.reshape(exp_count, tok_rows, HEAD_DIM), 'exp', 0...]
    all_gather x0 -> x1, waiting for transfers between devices: none -> 8.81 us  [shards(): whole_proj = lax.all_gather(out_proj, 'exp', axis=0, tiled=True)]
    all_to_all x1, waiting for transfers between devices: 32.6 us -> 39.9 us  [shards(): got_cols = lax.all_to_all(by_head, 'exp', 0, 0, tiled=True)]
  transfers between devices with their start and end apart: 5 -> 6, of which waited for: 4 -> 5; matrix products, arithmetic and copies ran while one was open for 25% -> 29% of each run, Pallas kernels for 0% -> 4%
where the time goes in v6:
time: 343 us; the launch traced here: 341 us
  waiting for transfers between devices  164 us (48%)
  local copies, waits for them, and re-layouts  51.3 us (15%)
  matrix products  45.9 us (13%)
  starting transfers between devices  27.5 us (8%)
  blocking collectives  15.7 us (5%)
  Pallas kernels  14.3 us (4%)
  between operations  13.4 us (4%)
  other arithmetic  9.14 us (3%)
    all_gather x1, waiting for transfers between devices, shards(): piece = lax.all_gather(normed, 'exp', axis=0, tiled=True)  63 us
    all_to_all x1, waiting for transfers between devices, shards(): lax.all_to_all(answered, ('req', 'exp'), split_axis=0, concat_axis=0, til...  50.5 us
    all_to_all x1, waiting for transfers between devices, shards(): got_cols = lax.all_to_all(by_head, 'exp', 0, 0, tiled=True)  39.9 us
    dot_general x1, matrix products, expert_block(): jnp.dot(hidden, down_w, preferred_element_type=jnp.float32)  17 us
    all_to_all x1, blocking collectives, shards(): lax.all_to_all(attention.reshape(exp_count, tok_rows, HEAD_DIM), 'exp', 0...  15.7 us
    pallas_call x1, Pallas kernels, head_attention(): pl.pallas_call(head_attention_kernel, grid=(rows // tile,), out_shape=jax...  14.3 us
    all_to_all x1, starting transfers between devices, shards(): lax.all_to_all(answered, ('req', 'exp'), split_axis=0, concat_axis=0, til...  10.3 us
    dot_general x1, matrix products, expert_block(): upper = jnp.dot(rows, up_w, preferred_element_type=jnp.float32)  9.67 us
  transfers between devices with their start and end apart: 6, of which 5 were waited for; matrix products, arithmetic and copies ran while one was open for 29% of the time, Pallas kernels for 4%

profile of v6, /device:TPU:0, one launch (start us, length us, event | category | flops | bytes accessed | tf_op | source)
XLA Modules:
  0.0 341.3 jit_solution(14321337630689822187)
XLA Ops:
  6.5 0.0 copy-start
  6.5 0.0 all-gather.3.cloned.1.call-start
  6.5 0.7 all-gather.3.cloned.1.call-update
  7.3 1.5 copy.59
  8.7 0.2 copy.60
  9.0 0.1 bitcast_bitcast_fusion
  9.0 0.5 copy_bitcast_fusion
  9.6 1.6 pad_maximum_fusion
  11.2 8.1 %all-to-all-start = ((bf16[16,576,128]{2,1,0:T(8,128)(2,1)}), bf16[16,576,128]{2,1,0:T(8,128)(2,1)}, u32[]{:S(2)}, u32[]{:S(2)}) async-start(bf16[16,576,128]{2,1,0:T(8,128)(2,1)} %pad_maximum_fusion), calls=%async_computation | async-start | bytes 4718592 | tf_op jit(solution)/shard_map/all_to_all | solution.py:119
  19.4 0.0 all-gather.5.cloned.1.call-start
  19.4 0.0 copy-done.8
  19.4 1.1 copy.49.rreq_ref
  20.5 0.0 copy-done.9
  20.5 1.0 copy.50.rpos_ref
  21.5 0.0 copy-done.13
  21.5 0.1 select_reduce_fusion.1
  21.6 0.7 iota_add_fusion
  22.3 39.9 %all-to-all-done = bf16[16,576,128]{2,1,0:T(8,128)(2,1)} async-done(((bf16[16,576,128]{2,1,0:T(8,128)(2,1)}), bf16[16,576,128]{2,1,0:T(8,128)(2,1)}, u32[]{:S(2)}, u32[]{:S(2)}) %all-to-all-start) | async-done | bytes 2359328 | tf_op jit(solution)/shard_map/all_to_all | solution.py:119
  62.2 1.7 slice.22
  63.9 3.1 fusion.31
  67.0 0.7 broadcast_in_dim.14
  67.7 14.3 %shard_map.181 = bf16[1024,128]{1,0:T(8,128)(2,1)} custom-call(bf16[1024,128]{1,0:T(8,128)(2,1)} %bitcast.91, bf16[4096,128]{1,0:T(8,128)(2,1)} %bitcast.88, bf16[4096,128]{1,0:T(8,128)(2,1)} %bitcast.87, s32[1024,1]{1,0:T(8,128)} %copy.49.rreq_ref, s32[1024,1]{1,0:T(8,128)} %copy.50.rpos_ref, s32[1,4096]{1,0:T(1,128)} %bitcast.95, s32[1,4096]{1,0:T(1,128)} %bitcast.94), custom_call_target="tpu_custom_call" | custom-call | flops 2147483648 | bytes 3145728 | tf_op jit(solution)/shard_map/pallas_call | solution.py:47
  82.0 15.7 %all_to_all.20 = bf16[16,64,128]{2,1,0:T(8,128)(2,1)S(1)} all-to-all(bf16[16,64,128]{2,1,0:T(8,128)(2,1)} %bitcast.92), channel_id=1, replica_groups=mesh['req'=8,'exp'=16] {'exp'}, dimensions={0} | all-to-all | bytes 524288 | tf_op jit(solution)/shard_map/all_to_all | solution.py:136
  97.7 8.8 %all-gather.3.cloned.1.call-done = bf16[2048,2048]{1,0:T(8,128)(2,1)} async-done(((bf16[128,2048]{1,0:T(8,128)(2,1)}), bf16[2048,2048]{1,0:T(8,128)(2,1)}) %all-gather.3.cloned.1.call-update) | async-done | bytes 8388624 | tf_op jit(solution)/shard_map/all_gather | solution.py:108
  106.5 5.1 %multiply_reduce_fusion.1 = (f32[64]{0:T(128)S(1)}, f32[64,2048]{1,0:T(8,128)S(1)}) fusion(bf16[2048,2048]{1,0:T(8,128)(2,1)} %all-gather.3.cloned.1.call-done, bf16[64,2048]{1,0:T(8,128)(2,1)S(1)} %copy-done.5, bf16[16,64,128]{2,1,0:T(8,128)(2,1)S(1)} %all_to_all.20), kind=kOutput, calls=%fused_computation.28 | convolution fusion | flops 537395136 | bytes 9437440 | tf_op jit(solution)/shard_map/dot_general | solution.py:140
  111.6 0.8 copy-done.2
  112.4 0.8 multiply_convert_fusion.1
  113.2 0.0 all-gather.5.cloned.1.call-update
  113.2 0.8 constant_dynamic-slice_fusion
  114.0 0.1 copy.52
  114.1 0.1 eq.74
  114.2 0.1 eq.65
  114.3 0.1 copy.54
  114.4 0.2 convert_reduce_fusion
  114.6 0.2 fusion.23
  114.9 0.2 select_reduce_fusion
  115.2 1.5 broadcast_in_dim.18
  116.6 0.3 reshape.175
  116.9 4.3 %scatter_custom_fusion = bf16[768,2048]{1,0:T(8,128)(2,1)} fusion(s32[256]{0:T(256)S(1)} %bitcast.98, bf16[256,2048]{1,0:T(8,128)(2,1)S(1)} %reshape.175, bf16[]{:T(256)} %constant.22.clone.1), kind=kCustom, calls=%fused_computation.14 | custom fusion | bytes 3145730 | tf_op jit(solution)/shard_map/scatter | solution.py:176
  121.2 6.3 %reshape.158 = bf16[128,6,2048]{2,1,0:T(8,128)(2,1)} reshape(bf16[768,2048]{1,0:T(8,128)(2,1)} %scatter_custom_fusion) | data formatting | bytes 6291456 | tf_op jit(solution)/shard_map/reshape | solution.py:178
  127.5 8.8 %all-to-all-start.2 = ((bf16[128,6,2048]{2,1,0:T(8,128)(2,1)}), bf16[128,6,2048]{2,1,0:T(8,128)(2,1)}, u32[]{:S(2)}, u32[]{:S(2)}) async-start(bf16[128,6,2048]{2,1,0:T(8,128)(2,1)} %reshape.158), calls=%async_computation.3 | async-start | bytes 8388608 | tf_op jit(solution)/shard_map/all_to_all | solution.py:179
  136.3 0.2 reduce-scatter.2.cloned.1.call-start
  136.5 63.0 %all-gather.5.cloned.1.call-done = bf16[1024,2048]{1,0:T(8,128)(2,1)} async-done(((bf16[64,2048]{1,0:T(8,128)(2,1)}), bf16[1024,2048]{1,0:T(8,128)(2,1)}) %all-gather.5.cloned.1.call-update) | async-done | bytes 4194320 | tf_op jit(solution)/shard_map/all_gather | solution.py:144
  199.5 0.0 copy-done.14
  199.5 5.0 %fusion.32 = f32[1024,352]{0,1:T(8,128)} fusion(bf16[1024,2048]{1,0:T(8,128)(2,1)} %all-gather.5.cloned.1.call-done, bf16[2048,352]{0,1:T(8,128)(2,1)S(1)} %copy-done.14), kind=kOutput, calls=%fused_computation.60 | convolution fusion | flops 1476395008 | bytes 7077888 | tf_op jit(solution)/shard_map/dot_general | solution.py:145
  204.5 0.0 copy-done
  204.5 9.0 %convolution_convert_fusion = bf16[1024,2048]{1,0:T(8,128)(2,1)} fusion(bf16[352,2048]{1,0:T(8,128)(2,1)S(1)} %copy-done, bf16[1024,2048]{1,0:T(8,128)(2,1)} %all-gather.5.cloned.1.call-done, bf16[2048,352]{0,1:T(8,128)(2,1)} %param.32, f32[1024,352]{0,1:T(8,128)} %fusion.32), kind=kOutput, calls=%fused_computation.9 | convolution fusion | flops 2957049856 | bytes 12713984 | tf_op jit(solution)/shard_map/dot_general | solution.py:148
  213.5 0.0 reduce-scatter.2.cloned.1.call-update
  213.5 0.0 all-to-all-done.2
  213.5 6.3 %reshape.159 = bf16[768,2048]{1,0:T(8,128)(2,1)} reshape(bf16[128,6,2048]{2,1,0:T(8,128)(2,1)} %all-to-all-done.2) | data formatting | bytes 6291456 | tf_op jit(solution)/shard_map/reshape | solution.py:181
  219.8 9.7 %fusion.2 = f32[768,1408]{1,0:T(8,128)} fusion(bf16[768,2048]{1,0:T(8,128)(2,1)} %reshape.159, bf16[1,2048,1408]{2,1,0:T(8,128)(2,1)} %param.29), kind=kOutput, calls=%fused_computation.4 | convolution fusion | flops 4429185024 | bytes 13238272 | tf_op jit(solution)/shard_map/dot_general | solution.py:14
  229.5 17.0 %fusion.8 = bf16[768,2048]{1,0:T(8,128)(2,1)} fusion(bf16[1,1408,2048]{2,1,0:T(8,128)(2,1)} %param.30, f32[768,1408]{1,0:T(8,128)} %fusion.2, bf16[768,2048]{1,0:T(8,128)(2,1)} %reshape.159, bf16[1,2048,1408]{2,1,0:T(8,128)(2,1)} %param.28), kind=kOutput, calls=%fused_computation.10 | convolution fusion | flops 8866430976 | bytes 22151168 | tf_op jit(solution)/shard_map/dot_general | solution.py:16
  246.5 6.3 %reshape.160 = bf16[128,6,2048]{2,1,0:T(8,128)(2,1)} reshape(bf16[768,2048]{1,0:T(8,128)(2,1)} %fusion.8) | data formatting | bytes 6291456 | tf_op jit(solution)/shard_map/reshape | solution.py:182
  252.8 10.3 %all-to-all-start.3 = ((bf16[128,6,2048]{2,1,0:T(8,128)(2,1)}), bf16[128,6,2048]{2,1,0:T(8,128)(2,1)}, u32[]{:S(2)}, u32[]{:S(2)}) async-start(bf16[128,6,2048]{2,1,0:T(8,128)(2,1)} %reshape.160), calls=%async_computation.4 | async-start | bytes 8388608 | tf_op jit(solution)/shard_map/all_to_all | solution.py:183
  263.2 0.7 copy.56
  263.9 0.0 copy-done.10
  263.9 0.2 fusion.17
  264.1 50.5 %all-to-all-done.3 = bf16[128,6,2048]{2,1,0:T(8,128)(2,1)} async-done(((bf16[128,6,2048]{2,1,0:T(8,128)(2,1)}), bf16[128,6,2048]{2,1,0:T(8,128)(2,1)}, u32[]{:S(2)}, u32[]{:S(2)}) %all-to-all-start.3) | async-done | bytes 3145760 | tf_op jit(solution)/shard_map/all_to_all | solution.py:183
  314.6 6.3 %reshape.161 = bf16[768,2048]{1,0:T(8,128)(2,1)} reshape(bf16[128,6,2048]{2,1,0:T(8,128)(2,1)} %all-to-all-done.3) | data formatting | bytes 6291456 | tf_op jit(solution)/shard_map/reshape | solution.py:185
  320.9 5.7 %gather_fusion = bf16[256,2048]{1,0:T(8,128)(2,1)} fusion(bf16[768,2048]{1,0:T(8,128)(2,1)} %reshape.161, s32[1024]{0:T(1024)S(1)} %pad_clamp_fusion), kind=kCustom, calls=%fused_computation | custom fusion | bytes 2098176 | tf_op jit(solution)/shard_map/gather | solution.py:186
  326.6 1.7 reshape.162
  328.4 3.1 multiply_reduce_fusion
  331.5 1.1 reduce-scatter.2.cloned.1.call-done
  332.6 2.1 add_convert_fusion
  (35 shorter events, 0.2 us)
Async XLA Ops:
  6.5 198.0 %copy-start = (bf16[352,2048]{1,0:T(8,128)(2,1)S(1)}, bf16[352,2048]{1,0:T(8,128)(2,1)}, u32[]{:S(2)}) copy-start(bf16[352,2048]{1,0:T(8,128)(2,1)} %param.33) | copy-start | bytes 4325380
  6.5 2.2 copy-start.4
  6.5 2.4 copy-start.6
  6.5 100.0 %all-gather.3.cloned.1.call-start = ((), (), s32[]{:S(2)}) async-start(), calls=%async_computation.5 | async-start | bytes 8912896 | tf_op jit(solution)/shard_map/all_gather | solution.py:108
  11.2 8.2 %copy-start.8 = (s32[1024]{0:T(1024)S(1)}, s32[1024]{0:T(1024)}, u32[]{:S(2)}) copy-start(s32[1024]{0:T(1024)} %param.24) | copy-start | bytes 12292
  11.2 9.3 %copy-start.9 = (s32[1024]{0:T(1024)S(1)}, s32[1024]{0:T(1024)}, u32[]{:S(2)}) copy-start(s32[1024]{0:T(1024)} %param.25) | copy-start | bytes 12292
  11.2 10.3 %copy-start.13 = (s32[4,8]{1,0:T(4,128)S(1)}, s32[4,8]{1,0:T(4,128)}, u32[]{:S(2)}) copy-start(s32[4,8]{1,0:T(4,128)} %param.23) | copy-start | bytes 388
  11.2 51.0 %all-to-all-start = ((bf16[16,576,128]{2,1,0:T(8,128)(2,1)}), bf16[16,576,128]{2,1,0:T(8,128)(2,1)}, u32[]{:S(2)}, u32[]{:S(2)}) async-start(bf16[16,576,128]{2,1,0:T(8,128)(2,1)} %pad_maximum_fusion), calls=%async_computation | async-start | bytes 4718592 | tf_op jit(solution)/shard_map/all_to_all | solution.py:119
  19.4 180.1 %all-gather.5.cloned.1.call-start = ((), (), s32[]{:S(2)}) async-start(), calls=%async_computation.6 | async-start | bytes 4456448 | tf_op jit(solution)/shard_map/all_gather | solution.py:144
  67.7 38.8 %copy-start.5 = (bf16[64,2048]{1,0:T(8,128)(2,1)S(1)}, bf16[64,2048]{1,0:T(8,128)(2,1)}, u32[]{:S(2)}) copy-start(bf16[64,2048]{1,0:T(8,128)(2,1)} %param.19) | copy-start | bytes 786436
  97.7 14.7 %copy-start.7 = (f32[2048]{0:T(1024)S(1)}, f32[2048]{0:T(1024)}, u32[]{:S(2)}) copy-start(f32[2048]{0:T(1024)} %param.27) | copy-start | bytes 24580
  97.7 16.7 %copy-start.11 = (s32[128]{0:T(128)S(1)}, s32[128]{0:T(128)}, u32[]{:S(2)}) copy-start(s32[128]{0:T(128)} %param.35) | copy-start | bytes 1540
  111.6 0.8 copy-start.2
  127.5 72.0 %copy-start.14 = (bf16[2048,352]{0,1:T(8,128)(2,1)S(1)}, bf16[2048,352]{0,1:T(8,128)(2,1)}, u32[]{:S(2)}) copy-start(bf16[2048,352]{0,1:T(8,128)(2,1)} %param.31) | copy-start | bytes 4325380
  127.5 86.0 %all-to-all-start.2 = ((bf16[128,6,2048]{2,1,0:T(8,128)(2,1)}), bf16[128,6,2048]{2,1,0:T(8,128)(2,1)}, u32[]{:S(2)}, u32[]{:S(2)}) async-start(bf16[128,6,2048]{2,1,0:T(8,128)(2,1)} %reshape.158), calls=%async_computation.3 | async-start | bytes 8388608 | tf_op jit(solution)/shard_map/all_to_all | solution.py:179
  136.3 196.4 %reduce-scatter.2.cloned.1.call-start = ((), (), s32[]{:S(2)}) async-start(), calls=%async_computation.7 | async-start | bytes 4456448 | tf_op jit(solution)/shard_map/reduce_scatter | solution.py:151
  252.8 10.3 %copy-start.12 = (f32[64,4]{0,1:T(4,128)S(1)}, f32[64,4]{0,1:T(4,128)}, u32[]{:S(2)}) copy-start(f32[64,4]{0,1:T(4,128)} %param.37) | copy-start | bytes 3076
  252.8 11.0 %copy-start.10 = (bf16[2048]{0:T(1024)(128)(2,1)S(1)}, bf16[2048]{0:T(1024)(128)(2,1)}, u32[]{:S(2)}) copy-start(bf16[2048]{0:T(1024)(128)(2,1)} %param.34) | copy-start | bytes 12292
  252.8 11.1 %copy-start.3 = (bf16[64,2048]{1,0:T(8,128)(2,1)S(1)}, bf16[64,2048]{1,0:T(8,128)(2,1)}, u32[]{:S(2)}) copy-start(bf16[64,2048]{1,0:T(8,128)(2,1)} %multiply_convert_fusion.1) | copy-start | bytes 786436
  252.8 61.8 %all-to-all-start.3 = ((bf16[128,6,2048]{2,1,0:T(8,128)(2,1)}), bf16[128,6,2048]{2,1,0:T(8,128)(2,1)}, u32[]{:S(2)}, u32[]{:S(2)}) async-start(bf16[128,6,2048]{2,1,0:T(8,128)(2,1)} %reshape.160), calls=%async_computation.4 | async-start | bytes 8388608 | tf_op jit(solution)/shard_map/all_to_all | solution.py:183
  320.9 13.8 %copy-start.1 = (bf16[352,2048]{1,0:T(8,128)(2,1)S(1)}, bf16[352,2048]{1,0:T(8,128)(2,1)}, u32[]{:S(2)}) copy-start(bf16[352,2048]{1,0:T(8,128)(2,1)} %param.33) | copy-start | bytes 4325380
Sparse Core Ops, SparseCore 0:
  9.5 96.9 all-gather.2
  113.4 86.0 all-gather.4
  213.6 118.9 reduce-scatter.1

commit v7 on v4

--- a/solution.py
+++ b/solution.py
@@ -105,6 +105,7 @@
     max_pages = page_table.shape[1]
     capacity = 3 * tok_rows * TOPK // slot_count
 
+    whole_proj = lax.all_gather(out_proj, "exp", axis=0, tiled=True)
     key_count = pages_here * page_len
     group_keys = exp_count * key_count
     by_head = jnp.concatenate(
@@ -132,18 +133,15 @@
     attention = head_attention(
         query_cols, key_cols, value_cols, row_request, row_position, key_request, key_position
     )
-    mixed_part = jnp.dot(attention, out_proj, preferred_element_type=jnp.float32)
-    mixed = jnp.sum(
-        lax.all_to_all(
-            mixed_part.astype(jnp.bfloat16).reshape(exp_count, tok_rows, model_width),
-            "exp", 0, 0, tiled=True,
-        ).astype(jnp.float32),
-        axis=0,
-    )
+    attention_rows = lax.all_to_all(
+        attention.reshape(exp_count, tok_rows, HEAD_DIM), "exp", 0, 0, tiled=True
+    )
+    attention_rows = attention_rows.transpose(1, 0, 2).reshape(tok_rows, model_width)
+    mixed = jnp.dot(attention_rows, whole_proj, preferred_element_type=jnp.float32)
     stream = resid.astype(jnp.float32) + mixed
     normed = rms_normed(stream, norm_gain)
 
-    piece = gather_exp(normed, exp_count)
+    piece = lax.all_gather(normed, "exp", axis=0, tiled=True)
     gate = jnp.dot(piece, shared_gate, preferred_element_type=jnp.float32)
     upper = jnp.dot(piece, shared_up, preferred_element_type=jnp.float32)
     shared_hidden = (jax.nn.silu(gate) * upper).astype(jnp.bfloat16)

time: 372 us -> 348 us (0.935)
  blocking collectives: 54 us -> 15.7 us
  waiting for transfers between devices: 171 us -> 188 us
    all_gather x0 -> x2, waiting for transfers between devices: none -> 77.8 us  [the longest x1 69 us: shards(): piece = lax.all_gather(normed, 'exp', axis=0, tiled=True)]
    all_to_all x1 -> x0, waiting for transfers between devices: 47.3 us -> none  [gather_exp(): got = lax.all_to_all(spread, 'exp', 0, 0, tiled=True)]
    all_to_all x1, blocking collectives: 54 us -> 15.7 us  [shards(): lax.all_to_all(attention.reshape(exp_count, tok_rows, HEAD_DIM), 'exp', 0...]
    all_to_all x1, waiting for transfers between devices: 38 us -> 0.01 us  [shards(): lax.all_to_all(outgoing, ('req', 'exp'), split_axis=0, concat_axis=0, til...]
    reduce_scatter x1, waiting for transfers between devices: 0.02 us -> 17.6 us  [shards(): lax.psum_scatter(shared_part, 'exp', scatter_dimension=0, tiled=True)]
    all_to_all x1, waiting for transfers between devices: 32.7 us -> 39.9 us  [shards(): got_cols = lax.all_to_all(by_head, 'exp', 0, 0, tiled=True)]
    all_to_all x1 -> x0, starting transfers between devices: 4.68 us -> none  [gather_exp(): got = lax.all_to_all(spread, 'exp', 0, 0, tiled=True)]
  transfers between devices with their start and end apart: 5 -> 6, of which waited for: 4 -> 5; matrix products, arithmetic and copies ran while one was open for 19% -> 23% of each run, Pallas kernels for 0% -> 4%
where the time goes in v7:
time: 348 us; the launch traced here: 347 us
  waiting for transfers between devices  188 us (54%)
  matrix products  59.4 us (17%)
  starting transfers between devices  26.1 us (8%)
  local copies, waits for them, and re-layouts  23.9 us (7%)
  blocking collectives  15.7 us (5%)
  Pallas kernels  14.3 us (4%)
  between operations  13.4 us (4%)
  other arithmetic  5.91 us (2%)
    all_gather x1, waiting for transfers between devices, shards(): piece = lax.all_gather(normed, 'exp', axis=0, tiled=True)  69 us
    all_to_all x1, waiting for transfers between devices, shards(): lax.all_to_all(answered, ('req', 'exp'), split_axis=0, concat_axis=0, til...  52.1 us
    all_to_all x1, waiting for transfers between devices, shards(): got_cols = lax.all_to_all(by_head, 'exp', 0, 0, tiled=True)  39.9 us
    dot_general x1, matrix products, expert_block(): jnp.dot(hidden, down_w, preferred_element_type=jnp.float32)  18.5 us
    reduce_scatter x1, waiting for transfers between devices, shards(): lax.psum_scatter(shared_part, 'exp', scatter_dimension=0, tiled=True)  17.6 us
    all_to_all x1, blocking collectives, shards(): lax.all_to_all(attention.reshape(exp_count, tok_rows, HEAD_DIM), 'exp', 0...  15.7 us
    pallas_call x1, Pallas kernels, head_attention(): pl.pallas_call(head_attention_kernel, grid=(rows // tile,), out_shape=jax...  14.3 us
    dot_general x1, matrix products, expert_block(): upper = jnp.dot(rows, up_w, preferred_element_type=jnp.float32)  11.3 us
  transfers between devices with their start and end apart: 6, of which 5 were waited for; matrix products, arithmetic and copies ran while one was open for 23% of the time, Pallas kernels for 4%

profile of v7, /device:TPU:0, one launch (start us, length us, event | category | flops | bytes accessed | tf_op | source)
XLA Modules:
  0.0 346.9 jit_solution(14860984653984673281)
XLA Ops:
  6.5 0.0 copy-start
  6.5 0.0 all-gather.3.cloned.1.call-start
  6.5 0.7 all-gather.3.cloned.1.call-update
  7.3 1.5 copy.72
  8.7 1.5 copy.73
  10.2 0.1 bitcast_bitcast_fusion
  10.3 0.5 copy_bitcast_fusion
  10.8 0.0 copy-start.6
  10.8 0.0 copy-start.7
  10.8 0.0 copy-start.10
  10.8 1.6 pad_maximum_fusion
  12.5 8.0 %all-to-all-start = ((bf16[16,576,128]{2,1,0:T(8,128)(2,1)}), bf16[16,576,128]{2,1,0:T(8,128)(2,1)}, u32[]{:S(2)}, u32[]{:S(2)}) async-start(bf16[16,576,128]{2,1,0:T(8,128)(2,1)} %pad_maximum_fusion), calls=%async_computation | async-start | bytes 4718592 | tf_op jit(solution)/shard_map/all_to_all | solution.py:119
  20.5 0.0 all-gather.5.cloned.1.call-start
  20.6 1.1 copy.55.rreq_ref
  21.6 1.0 copy.56.rpos_ref
  22.6 0.1 select_reduce_fusion.1
  22.7 0.7 iota_add_fusion
  23.4 39.9 %all-to-all-done = bf16[16,576,128]{2,1,0:T(8,128)(2,1)} async-done(((bf16[16,576,128]{2,1,0:T(8,128)(2,1)}), bf16[16,576,128]{2,1,0:T(8,128)(2,1)}, u32[]{:S(2)}, u32[]{:S(2)}) %all-to-all-start) | async-done | bytes 2359328 | tf_op jit(solution)/shard_map/all_to_all | solution.py:119
  63.3 1.7 slice.20
  65.0 3.1 fusion.55
  68.1 0.7 broadcast_in_dim.10
  68.8 14.3 %shard_map.181 = bf16[1024,128]{1,0:T(8,128)(2,1)} custom-call(bf16[1024,128]{1,0:T(8,128)(2,1)} %bitcast.116, bf16[4096,128]{1,0:T(8,128)(2,1)} %bitcast.113, bf16[4096,128]{1,0:T(8,128)(2,1)} %bitcast.112, s32[1024,1]{1,0:T(8,128)} %copy.55.rreq_ref, s32[1024,1]{1,0:T(8,128)} %copy.56.rpos_ref, s32[1,4096]{1,0:T(1,128)} %bitcast.120, s32[1,4096]{1,0:T(1,128)} %bitcast.119), custom_call_target="tpu_custom_call" | custom-call | flops 2147483648 | bytes 3145728 | tf_op jit(solution)/shard_map/pallas_call | solution.py:47
  83.1 15.7 %all_to_all.20 = bf16[16,64,128]{2,1,0:T(8,128)(2,1)S(1)} all-to-all(bf16[16,64,128]{2,1,0:T(8,128)(2,1)} %bitcast.117), channel_id=1, replica_groups=mesh['req'=8,'exp'=16] {'exp'}, dimensions={0} | all-to-all | bytes 524288 | tf_op jit(solution)/shard_map/all_to_all | solution.py:136
  98.8 8.8 %all-gather.3.cloned.1.call-done = bf16[2048,2048]{1,0:T(8,128)(2,1)} async-done(((bf16[128,2048]{1,0:T(8,128)(2,1)}), bf16[2048,2048]{1,0:T(8,128)(2,1)}) %all-gather.3.cloned.1.call-update) | async-done | bytes 8388624 | tf_op jit(solution)/shard_map/all_gather | solution.py:108
  107.6 5.1 %multiply_reduce_fusion = (f32[64]{0:T(128)S(1)}, f32[64,2048]{1,0:T(8,128)S(1)}) fusion(bf16[2048,2048]{1,0:T(8,128)(2,1)} %all-gather.3.cloned.1.call-done, bf16[64,2048]{1,0:T(8,128)(2,1)S(1)} %copy-done.3, bf16[16,64,128]{2,1,0:T(8,128)(2,1)S(1)} %all_to_all.20), kind=kOutput, calls=%fused_computation.35 | convolution fusion | flops 537395136 | bytes 9437440 | tf_op jit(solution)/shard_map/dot_general | solution.py:140
  112.7 0.0 copy-done.5
  112.7 0.8 multiply_convert_fusion.1
  113.5 0.0 all-gather.5.cloned.1.call-update
  113.6 0.8 constant_dynamic-slice_fusion
  114.3 0.1 copy.58
  114.4 0.1 eq.143
  114.5 0.1 eq.130
  114.7 0.1 copy.61
  114.8 0.2 convert_reduce_fusion
  115.0 0.2 fusion.43
  115.3 0.2 select_reduce_fusion
  115.5 0.1 iota_compare_fusion
  115.6 3.9 %convolution_convert_fusion.1 = bf16[128,6,2048]{2,0,1:T(8,128)(2,1)} fusion(pred[256,6]{0,1:T(8,128)(4,1)S(1)} %iota_compare_fusion.6, pred[256,128]{1,0:T(8,128)(4,1)S(1)} %iota_compare_fusion, bf16[64,2048]{1,0:T(8,128)(2,1)} %multiply_convert_fusion.1, s32[256]{0:T(256)S(1)} %and_select_fusion), kind=kOutput, calls=%fused_computation.8 | convolution fusion | flops 228327424 | bytes 3443200 | tf_op jit(solution)/shard_map/sci,id->scd/dot_general | solution.py:183
  119.5 5.6 %copy.64 = bf16[128,6,2048]{2,1,0:T(8,128)(2,1)} copy(bf16[128,6,2048]{2,0,1:T(8,128)(2,1)} %convolution_convert_fusion.1) | data formatting | bytes 6291456 | tf_op jit(solution)/shard_map/convert_element_type | solution.py:185
  125.1 8.8 %all-to-all-start.2 = ((bf16[128,6,2048]{2,1,0:T(8,128)(2,1)}), bf16[128,6,2048]{2,1,0:T(8,128)(2,1)}, u32[]{:S(2)}, u32[]{:S(2)}) async-start(bf16[128,6,2048]{2,1,0:T(8,128)(2,1)} %copy.64), calls=%async_computation.3 | async-start | bytes 8388608 | tf_op jit(solution)/shard_map/all_to_all | solution.py:186
  133.9 0.2 reduce-scatter.2.cloned.1.call-start
  134.1 69.0 %all-gather.5.cloned.1.call-done = bf16[1024,2048]{1,0:T(8,128)(2,1)} async-done(((bf16[64,2048]{1,0:T(8,128)(2,1)}), bf16[1024,2048]{1,0:T(8,128)(2,1)}) %all-gather.5.cloned.1.call-update) | async-done | bytes 4194320 | tf_op jit(solution)/shard_map/all_gather | solution.py:144
  203.2 5.4 %fusion.56 = f32[1024,352]{0,1:T(8,128)} fusion(bf16[1024,2048]{1,0:T(8,128)(2,1)} %all-gather.5.cloned.1.call-done, bf16[2048,352]{0,1:T(8,128)(2,1)} %param.31), kind=kOutput, calls=%fused_computation.80 | convolution fusion | flops 1476395008 | bytes 7077888 | tf_op jit(solution)/shard_map/dot_general | solution.py:145
  208.6 0.0 copy-done
  208.6 9.0 %convolution_convert_fusion = bf16[1024,2048]{1,0:T(8,128)(2,1)} fusion(bf16[352,2048]{1,0:T(8,128)(2,1)S(1)} %copy-done, bf16[1024,2048]{1,0:T(8,128)(2,1)} %all-gather.5.cloned.1.call-done, bf16[2048,352]{0,1:T(8,128)(2,1)} %param.32, f32[1024,352]{0,1:T(8,128)} %fusion.56), kind=kOutput, calls=%fused_computation.7 | convolution fusion | flops 2957049856 | bytes 12713984 | tf_op jit(solution)/shard_map/dot_general | solution.py:148
  217.6 0.0 reduce-scatter.2.cloned.1.call-update
  217.6 0.0 all-to-all-done.2
  217.6 11.3 %fusion.2 = f32[128,6,1408]{2,0,1:T(8,128)} fusion(bf16[1,2048,1408]{2,1,0:T(8,128)(2,1)} %param.29, bf16[128,6,2048]{2,1,0:T(8,128)(2,1)} %all-to-all-done.2), kind=kOutput, calls=%fused_computation.2 | convolution fusion | flops 4429185024 | bytes 13238272 | tf_op jit(solution)/shard_map/dot_general | solution.py:14
  228.9 18.5 %fusion.8 = bf16[128,6,2048]{2,0,1:T(8,128)(2,1)} fusion(bf16[1,1408,2048]{2,1,0:T(8,128)(2,1)} %param.30, f32[128,6,1408]{2,0,1:T(8,128)} %fusion.2, bf16[1,2048,1408]{2,1,0:T(8,128)(2,1)} %param.28, bf16[128,6,2048]{2,1,0:T(8,128)(2,1)} %all-to-all-done.2), kind=kOutput, calls=%fused_computation.9 | convolution fusion | flops 8866430976 | bytes 22151168 | tf_op jit(solution)/shard_map/dot_general | solution.py:16
  247.4 5.6 %copy.67 = bf16[128,6,2048]{2,1,0:T(8,128)(2,1)} copy(bf16[128,6,2048]{2,0,1:T(8,128)(2,1)} %fusion.8) | data formatting | bytes 6291456 | tf_op jit(solution)/shard_map/convert_element_type | solution.py:16
  253.0 9.0 %all-to-all-start.3 = ((bf16[128,6,2048]{2,1,0:T(8,128)(2,1)}), bf16[128,6,2048]{2,1,0:T(8,128)(2,1)}, u32[]{:S(2)}, u32[]{:S(2)}) async-start(bf16[128,6,2048]{2,1,0:T(8,128)(2,1)} %copy.67), calls=%async_computation.4 | async-start | bytes 8388608 | tf_op jit(solution)/shard_map/all_to_all | solution.py:188
  262.0 0.1 eq.139
  262.1 0.1 sub.13
  262.2 0.1 copy.59
  262.3 0.1 copy.63
  262.4 0.1 iota_compare_fusion.1
  262.5 0.0 copy-start.1
  262.6 0.2 fusion.29
  262.7 52.1 %all-to-all-done.3 = bf16[128,6,2048]{2,1,0:T(8,128)(2,1)} async-done(((bf16[128,6,2048]{2,1,0:T(8,128)(2,1)}), bf16[128,6,2048]{2,1,0:T(8,128)(2,1)}, u32[]{:S(2)}, u32[]{:S(2)}) %all-to-all-start.3) | async-done | bytes 3145760 | tf_op jit(solution)/shard_map/all_to_all | solution.py:188
  314.8 0.0 copy-done.11
  314.8 6.1 %fusion.22 = f32[64,2048]{1,0:T(8,128)S(1)} fusion(bf16[128,6,2048]{2,1,0:T(8,128)(2,1)} %all-to-all-done.3, f32[64,4]{0,1:T(4,128)S(1)} %copy-done.11, pred[64,4,6]{0,2,1:T(8,128)(4,1)S(1)} %iota_compare_fusion.4, pred[64,4,128]{2,0,1:T(8,128)(4,1)S(1)} %iota_compare_fusion.1), kind=kOutput, calls=%fused_computation.20 | convolution fusion | flops 806420480 | bytes 3705344 | tf_op jit(solution)/shard_map/rksc,scd->rkd/dot_general | solution.py:189
  320.9 17.6 %reduce-scatter.2.cloned.1.call-done = bf16[64,2048]{1,0:T(8,128)(2,1)} async-done(((bf16[1024,2048]{1,0:T(8,128)(2,1)}), bf16[64,2048]{1,0:T(8,128)(2,1)}) %reduce-scatter.2.cloned.1.call-update) | async-done | bytes 262160 | tf_op jit(solution)/shard_map/reduce_scatter | solution.py:151
  338.5 1.8 add_convert_fusion
  340.3 0.0 copy-done.1
  (29 shorter events, 0.2 us)
Async XLA Ops:
  6.5 202.1 %copy-start = (bf16[352,2048]{1,0:T(8,128)(2,1)S(1)}, bf16[352,2048]{1,0:T(8,128)(2,1)}, u32[]{:S(2)}) copy-start(bf16[352,2048]{1,0:T(8,128)(2,1)} %param.33) | copy-start | bytes 4325380
  6.5 3.6 %copy-start.4 = (bf16[64,2048]{1,0:T(8,128)(2,1)S(1)}, bf16[64,2048]{1,0:T(8,128)(2,1)}, u32[]{:S(2)}) copy-start(bf16[64,2048]{1,0:T(8,128)(2,1)} %param.20) | copy-start | bytes 786436
  6.5 101.1 %all-gather.3.cloned.1.call-start = ((), (), s32[]{:S(2)}) async-start(), calls=%async_computation.5 | async-start | bytes 8912896 | tf_op jit(solution)/shard_map/all_gather | solution.py:108
  10.8 9.7 %copy-start.6 = (s32[1024]{0:T(1024)S(1)}, s32[1024]{0:T(1024)}, u32[]{:S(2)}) copy-start(s32[1024]{0:T(1024)} %param.24) | copy-start | bytes 12292
  10.8 10.8 %copy-start.7 = (s32[1024]{0:T(1024)S(1)}, s32[1024]{0:T(1024)}, u32[]{:S(2)}) copy-start(s32[1024]{0:T(1024)} %param.25) | copy-start | bytes 12292
  10.8 11.8 %copy-start.10 = (s32[4,8]{1,0:T(4,128)S(1)}, s32[4,8]{1,0:T(4,128)}, u32[]{:S(2)}) copy-start(s32[4,8]{1,0:T(4,128)} %param.23) | copy-start | bytes 388
  12.5 50.9 %all-to-all-start = ((bf16[16,576,128]{2,1,0:T(8,128)(2,1)}), bf16[16,576,128]{2,1,0:T(8,128)(2,1)}, u32[]{:S(2)}, u32[]{:S(2)}) async-start(bf16[16,576,128]{2,1,0:T(8,128)(2,1)} %pad_maximum_fusion), calls=%async_computation | async-start | bytes 4718592 | tf_op jit(solution)/shard_map/all_to_all | solution.py:119
  20.5 182.7 %all-gather.5.cloned.1.call-start = ((), (), s32[]{:S(2)}) async-start(), calls=%async_computation.6 | async-start | bytes 4456448 | tf_op jit(solution)/shard_map/all_gather | solution.py:144
  68.8 38.8 %copy-start.3 = (bf16[64,2048]{1,0:T(8,128)(2,1)S(1)}, bf16[64,2048]{1,0:T(8,128)(2,1)}, u32[]{:S(2)}) copy-start(bf16[64,2048]{1,0:T(8,128)(2,1)} %param.19) | copy-start | bytes 786436
  98.8 13.9 %copy-start.5 = (f32[2048]{0:T(1024)S(1)}, f32[2048]{0:T(1024)}, u32[]{:S(2)}) copy-start(f32[2048]{0:T(1024)} %param.27) | copy-start | bytes 24580
  98.8 16.0 %copy-start.9 = (s32[128]{0:T(128)S(1)}, s32[128]{0:T(128)}, u32[]{:S(2)}) copy-start(s32[128]{0:T(128)} %param.35) | copy-start | bytes 1540
  125.1 92.5 %all-to-all-start.2 = ((bf16[128,6,2048]{2,1,0:T(8,128)(2,1)}), bf16[128,6,2048]{2,1,0:T(8,128)(2,1)}, u32[]{:S(2)}, u32[]{:S(2)}) async-start(bf16[128,6,2048]{2,1,0:T(8,128)(2,1)} %copy.64), calls=%async_computation.3 | async-start | bytes 8388608 | tf_op jit(solution)/shard_map/all_to_all | solution.py:186
  133.9 204.6 %reduce-scatter.2.cloned.1.call-start = ((), (), s32[]{:S(2)}) async-start(), calls=%async_computation.7 | async-start | bytes 4456448 | tf_op jit(solution)/shard_map/reduce_scatter | solution.py:151
  253.0 9.4 %copy-start.8 = (bf16[2048]{0:T(1024)(128)(2,1)S(1)}, bf16[2048]{0:T(1024)(128)(2,1)}, u32[]{:S(2)}) copy-start(bf16[2048]{0:T(1024)(128)(2,1)} %param.34) | copy-start | bytes 12292
  253.0 9.6 %copy-start.2 = (bf16[64,2048]{1,0:T(8,128)(2,1)S(1)}, bf16[64,2048]{1,0:T(8,128)(2,1)}, u32[]{:S(2)}) copy-start(bf16[64,2048]{1,0:T(8,128)(2,1)} %multiply_convert_fusion.1) | copy-start | bytes 786436
  253.0 61.8 %copy-start.11 = (f32[64,4]{0,1:T(4,128)S(1)}, f32[64,4]{0,1:T(4,128)}, u32[]{:S(2)}) copy-start(f32[64,4]{0,1:T(4,128)} %param.37) | copy-start | bytes 3076
  253.0 61.8 %all-to-all-start.3 = ((bf16[128,6,2048]{2,1,0:T(8,128)(2,1)}), bf16[128,6,2048]{2,1,0:T(8,128)(2,1)}, u32[]{:S(2)}, u32[]{:S(2)}) async-start(bf16[128,6,2048]{2,1,0:T(8,128)(2,1)} %copy.67), calls=%async_computation.4 | async-start | bytes 8388608 | tf_op jit(solution)/shard_map/all_to_all | solution.py:188
  262.5 77.8 %copy-start.1 = (bf16[352,2048]{1,0:T(8,128)(2,1)S(1)}, bf16[352,2048]{1,0:T(8,128)(2,1)}, u32[]{:S(2)}) copy-start(bf16[352,2048]{1,0:T(8,128)(2,1)} %param.33) | copy-start | bytes 4325380
Sparse Core Ops, SparseCore 0:
  9.5 98.0 all-gather.2
  113.7 89.4 all-gather.4
  217.7 120.7 reduce-scatter.1

commit v8 on v7

--- a/solution.py
+++ b/solution.py
@@ -148,9 +148,17 @@
     shared_part = jnp.dot(
         shared_hidden, shared_down, preferred_element_type=jnp.float32
     ).astype(jnp.bfloat16)
-    shared_out = lax.psum_scatter(
-        shared_part, "exp", scatter_dimension=0, tiled=True
+    half = model_width // 2
+    shared_left = jnp.sum(
+        lax.all_to_all(
+            shared_part[:, :half].reshape(exp_count, tok_rows, half), "exp", 0, 0, tiled=True
+        ).astype(jnp.float32),
+        axis=0,
+    )
+    shared_right = lax.psum_scatter(
+        shared_part[:, half:], "exp", scatter_dimension=0, tiled=True
     ).astype(jnp.float32)
+    shared_out = jnp.concatenate([shared_left, shared_right], axis=1)
     shared_scale = jax.nn.sigmoid(
         jnp.dot(normed, shared_scalar, preferred_element_type=jnp.float32)
     )

time: 348 us -> 358 us (1.029)
  blocking collectives: 15.7 us -> 60.3 us
  waiting for transfers between devices: 188 us -> 147 us
  local copies, waits for them, and re-layouts: 23.9 us -> 32.3 us
    all_gather x1, waiting for transfers between devices: 69 us -> 0.02 us  [shards(): piece = lax.all_gather(normed, 'exp', axis=0, tiled=True)]
    all_to_all x1, blocking collectives: 15.7 us -> 60.3 us  [shards(): lax.all_to_all(outgoing, ('req', 'exp'), split_axis=0, concat_axis=0, til...]
    all_to_all x1 -> x2, waiting for transfers between devices: 0.01 us -> 34.4 us  [the longest x1 22.6 us: shards(): lax.all_to_all(shared_part[:, :half].reshape(exp_count, tok_rows, half),...]
    all_to_all x1, waiting for transfers between devices: 52.1 us -> 32.6 us  [shards(): lax.all_to_all(answered, ('req', 'exp'), split_axis=0, concat_axis=0, til...]
    reduce_scatter x1, waiting for transfers between devices: 17.6 us -> 32 us  [shards(): lax.psum_scatter(shared_part[:, half:], 'exp', scatter_dimension=0, tiled...]
    slice x0 -> x1, local copies, waits for them, and re-layouts: none -> 4.71 us  [shards(): shared_part[:, :half].reshape(exp_count, tok_rows, half)]
    dot_general x1, matrix products: 11.3 us -> 7.42 us  [expert_block(): upper = jnp.dot(rows, up_w, preferred_element_type=jnp.float32)]
    all_to_all x1 -> x2, starting transfers between devices: 8.79 us -> 9.12 us  [the longest x1 5.59 us: shards(): lax.all_to_all(shared_part[:, :half].reshape(exp_count, tok_rows, half),...]
  transfers between devices with their start and end apart: 6 -> 7, of which waited for: 5 -> 6; matrix products, arithmetic and copies ran while one was open for 23% -> 24% of each run, Pallas kernels for 4% -> 4%
where the time goes in v8:
time: 358 us; the launch traced here: 357 us
  waiting for transfers between devices  147 us (41%)
  blocking collectives  60.3 us (17%)
  matrix products  57 us (16%)
  local copies, waits for them, and re-layouts  32.3 us (9%)
  starting transfers between devices  24.7 us (7%)
  Pallas kernels  14.3 us (4%)
  between operations  13.4 us (4%)
  other arithmetic  8.19 us (2%)
    all_to_all x1, blocking collectives, shards(): lax.all_to_all(outgoing, ('req', 'exp'), split_axis=0, concat_axis=0, til...  60.3 us
    all_to_all x1, waiting for transfers between devices, shards(): got_cols = lax.all_to_all(by_head, 'exp', 0, 0, tiled=True)  38.3 us
    all_to_all x1, waiting for transfers between devices, shards(): lax.all_to_all(answered, ('req', 'exp'), split_axis=0, concat_axis=0, til...  32.6 us
    reduce_scatter x1, waiting for transfers between devices, shards(): lax.psum_scatter(shared_part[:, half:], 'exp', scatter_dimension=0, tiled...  32 us
    all_to_all x1, waiting for transfers between devices, shards(): lax.all_to_all(shared_part[:, :half].reshape(exp_count, tok_rows, half),...  22.6 us
    dot_general x1, matrix products, expert_block(): jnp.dot(hidden, down_w, preferred_element_type=jnp.float32)  18.6 us
    pallas_call x1, Pallas kernels, head_attention(): pl.pallas_call(head_attention_kernel, grid=(rows // tile,), out_shape=jax...  14.3 us
    all_to_all x1, waiting for transfers between devices, shards(): lax.all_to_all(attention.reshape(exp_count, tok_rows, HEAD_DIM), 'exp', 0...  11.8 us
  transfers between devices with their start and end apart: 7, of which 6 were waited for; matrix products, arithmetic and copies ran while one was open for 24% of the time, Pallas kernels for 4%

profile of v8, /device:TPU:0, one launch (start us, length us, event | category | flops | bytes accessed | tf_op | source)
XLA Modules:
  0.0 357.1 jit_solution(9916040036035970135)
XLA Ops:
  6.5 0.7 all-gather.3.cloned.1.call-update
  7.3 1.5 copy.72
  8.7 1.5 copy.73
  10.2 0.1 bitcast_bitcast_fusion
  10.3 0.5 copy_bitcast_fusion
  10.8 0.0 copy-start.9
  10.8 0.0 copy-start.6
  10.8 1.6 pad_maximum_fusion
  12.5 8.1 %all-to-all-start = ((bf16[16,576,128]{2,1,0:T(8,128)(2,1)}), bf16[16,576,128]{2,1,0:T(8,128)(2,1)}, u32[]{:S(2)}, u32[]{:S(2)}) async-start(bf16[16,576,128]{2,1,0:T(8,128)(2,1)} %pad_maximum_fusion), calls=%async_computation | async-start | bytes 4718592 | tf_op jit(solution)/shard_map/all_to_all | solution.py:119
  20.6 0.8 constant_dynamic-slice_fusion
  21.4 0.1 copy.58
  21.5 0.1 eq.143
  21.6 0.1 eq.130
  21.7 0.1 copy.61
  21.8 0.2 convert_reduce_fusion.1
  22.0 0.2 fusion.46
  22.3 1.1 copy.55.rreq_ref
  23.3 1.1 copy.56.rpos_ref
  24.4 0.1 select_reduce_fusion.1
  24.5 0.7 iota_add_fusion
  25.2 38.3 %all-to-all-done = bf16[16,576,128]{2,1,0:T(8,128)(2,1)} async-done(((bf16[16,576,128]{2,1,0:T(8,128)(2,1)}), bf16[16,576,128]{2,1,0:T(8,128)(2,1)}, u32[]{:S(2)}, u32[]{:S(2)}) %all-to-all-start) | async-done | bytes 2359328 | tf_op jit(solution)/shard_map/all_to_all | solution.py:119
  63.4 1.7 slice.28
  65.1 3.1 fusion.59
  68.2 0.7 broadcast_in_dim.10
  68.9 14.3 %shard_map.181 = bf16[1024,128]{1,0:T(8,128)(2,1)} custom-call(bf16[1024,128]{1,0:T(8,128)(2,1)} %bitcast.119, bf16[4096,128]{1,0:T(8,128)(2,1)} %bitcast.115, bf16[4096,128]{1,0:T(8,128)(2,1)} %bitcast.114, s32[1024,1]{1,0:T(8,128)} %copy.55.rreq_ref, s32[1024,1]{1,0:T(8,128)} %copy.56.rpos_ref, s32[1,4096]{1,0:T(1,128)} %bitcast.122, s32[1,4096]{1,0:T(1,128)} %bitcast.121), custom_call_target="tpu_custom_call" | custom-call | flops 2147483648 | bytes 3145728 | tf_op jit(solution)/shard_map/pallas_call | solution.py:47
  83.2 3.5 all-to-all-start.1
  86.8 0.0 all-gather.5.cloned.1.call-start
  86.9 0.2 select_reduce_fusion
  87.1 11.8 %all-to-all-done.1 = bf16[16,64,128]{2,1,0:T(8,128)(2,1)S(1)} async-done(((bf16[16,64,128]{2,1,0:T(8,128)(2,1)}), bf16[16,64,128]{2,1,0:T(8,128)(2,1)S(1)}, u32[]{:S(2)}, u32[]{:S(2)}) %all-to-all-start.1) | async-done | bytes 262176 | tf_op jit(solution)/shard_map/all_to_all | solution.py:136
  98.9 8.8 %all-gather.3.cloned.1.call-done = bf16[2048,2048]{1,0:T(8,128)(2,1)} async-done(((bf16[128,2048]{1,0:T(8,128)(2,1)}), bf16[2048,2048]{1,0:T(8,128)(2,1)}) %all-gather.3.cloned.1.call-update) | async-done | bytes 8388624 | tf_op jit(solution)/shard_map/all_gather | solution.py:108
  107.7 5.1 %multiply_reduce_fusion = (f32[64]{0:T(128)S(1)}, f32[64,2048]{1,0:T(8,128)S(1)}) fusion(bf16[2048,2048]{1,0:T(8,128)(2,1)} %all-gather.3.cloned.1.call-done, bf16[64,2048]{1,0:T(8,128)(2,1)S(1)} %copy-done.3, bf16[16,64,128]{2,1,0:T(8,128)(2,1)S(1)} %all-to-all-done.1), kind=kOutput, calls=%fused_computation.39 | convolution fusion | flops 537395136 | bytes 9437440 | tf_op jit(solution)/shard_map/dot_general | solution.py:140
  112.8 0.8 copy-done.1
  113.6 0.8 multiply_convert_fusion.1
  114.4 0.0 all-gather.5.cloned.1.call-update
  114.5 0.1 iota_compare_fusion
  114.6 3.9 %convolution_convert_fusion.1 = bf16[128,6,2048]{2,0,1:T(8,128)(2,1)} fusion(pred[256,6]{0,1:T(8,128)(4,1)S(1)} %iota_compare_fusion.6, pred[256,128]{1,0:T(8,128)(4,1)S(1)} %iota_compare_fusion, bf16[64,2048]{1,0:T(8,128)(2,1)} %multiply_convert_fusion.1, s32[256]{0:T(256)S(1)} %and_select_fusion), kind=kOutput, calls=%fused_computation.9 | convolution fusion | flops 228327424 | bytes 3443200 | tf_op jit(solution)/shard_map/sci,id->scd/dot_general | solution.py:191
  118.5 3.8 %copy.64 = bf16[128,6,2048]{2,1,0:T(8,128)(2,1)S(1)} copy(bf16[128,6,2048]{2,0,1:T(8,128)(2,1)} %convolution_convert_fusion.1) | data formatting | bytes 6291456 | tf_op jit(solution)/shard_map/convert_element_type | solution.py:193
  122.3 0.0 slice-start.1
  122.3 60.3 %all_to_all.25 = bf16[128,6,2048]{2,1,0:T(8,128)(2,1)S(1)} all-to-all(bf16[128,6,2048]{2,1,0:T(8,128)(2,1)S(1)} %copy.64), channel_id=1, replica_groups=mesh['req'=8,'exp'=16] {'req','exp'}, dimensions={0} | all-to-all | bytes 6291456 | tf_op jit(solution)/shard_map/all_to_all | solution.py:194
  182.6 1.9 copy-done.2
  184.5 7.4 %fusion.2 = f32[128,6,1408]{2,0,1:T(8,128)} fusion(bf16[1,2048,1408]{2,1,0:T(8,128)(2,1)S(1)} %bitcast.126, bf16[128,6,2048]{2,1,0:T(8,128)(2,1)S(1)} %all_to_all.25), kind=kOutput, calls=%fused_computation.2 | convolution fusion | flops 4429185024 | bytes 13238272 | tf_op jit(solution)/shard_map/dot_general | solution.py:14
  192.0 18.6 %fusion.8 = bf16[128,6,2048]{2,0,1:T(8,128)(2,1)} fusion(bf16[1,1408,2048]{2,1,0:T(8,128)(2,1)} %param.30, f32[128,6,1408]{2,0,1:T(8,128)} %fusion.2, bf16[1,2048,1408]{2,1,0:T(8,128)(2,1)} %param.28, bf16[128,6,2048]{2,1,0:T(8,128)(2,1)} %copy-done.2), kind=kOutput, calls=%fused_computation.10 | convolution fusion | flops 8866430976 | bytes 22151168 | tf_op jit(solution)/shard_map/dot_general | solution.py:16
  210.6 5.7 %copy.67 = bf16[128,6,2048]{2,1,0:T(8,128)(2,1)} copy(bf16[128,6,2048]{2,0,1:T(8,128)(2,1)} %fusion.8) | data formatting | bytes 6291456 | tf_op jit(solution)/shard_map/convert_element_type | solution.py:16
  216.2 7.1 %all-to-all-start.4 = ((bf16[128,6,2048]{2,1,0:T(8,128)(2,1)}), bf16[128,6,2048]{2,1,0:T(8,128)(2,1)}, u32[]{:S(2)}, u32[]{:S(2)}) async-start(bf16[128,6,2048]{2,1,0:T(8,128)(2,1)} %copy.67), calls=%async_computation.5 | async-start | bytes 8388608 | tf_op jit(solution)/shard_map/all_to_all | solution.py:196
  223.4 0.3 reduce-scatter.2.cloned.1.call-start
  223.6 0.0 all-gather.5.cloned.1.call-done
  223.7 5.0 %fusion.60 = f32[1024,352]{0,1:T(8,128)} fusion(bf16[1024,2048]{1,0:T(8,128)(2,1)} %all-gather.5.cloned.1.call-done, bf16[2048,352]{0,1:T(8,128)(2,1)S(1)} %copy-done.11), kind=kOutput, calls=%fused_computation.85 | convolution fusion | flops 1476395008 | bytes 7077888 | tf_op jit(solution)/shard_map/dot_general | solution.py:145
  228.7 8.9 %convolution_convert_fusion = bf16[1024,2048]{1,0:T(8,128)(2,1)} fusion(bf16[352,2048]{1,0:T(8,128)(2,1)S(1)} %copy-done, bf16[1024,2048]{1,0:T(8,128)(2,1)} %all-gather.5.cloned.1.call-done, bf16[2048,352]{0,1:T(8,128)(2,1)} %param.32, f32[1024,352]{0,1:T(8,128)} %fusion.60), kind=kOutput, calls=%fused_computation.8 | convolution fusion | flops 2957049856 | bytes 12713984 | tf_op jit(solution)/shard_map/dot_general | solution.py:148
  237.6 4.7 %fusion.58 = (bf16[1024,1024]{1,0:T(8,128)(2,1)}, bf16[1024,1024]{1,0:T(8,128)(2,1)}) fusion(bf16[1024,2048]{1,0:T(8,128)(2,1)} %convolution_convert_fusion), kind=kLoop, calls=%fused_computation.83 | loop fusion | bytes 8388608 | tf_op jit(solution)/shard_map/slice | solution.py:154
  242.4 0.0 reduce-scatter.2.cloned.1.call-update
  242.4 32.6 %all-to-all-done.4 = bf16[128,6,2048]{2,1,0:T(8,128)(2,1)} async-done(((bf16[128,6,2048]{2,1,0:T(8,128)(2,1)}), bf16[128,6,2048]{2,1,0:T(8,128)(2,1)}, u32[]{:S(2)}, u32[]{:S(2)}) %all-to-all-start.4) | async-done | bytes 3145760 | tf_op jit(solution)/shard_map/all_to_all | solution.py:196
  275.0 5.6 %all-to-all-start.2 = ((bf16[16,64,1024]{2,1,0:T(8,128)(2,1)}), bf16[16,64,1024]{2,1,0:T(8,128)(2,1)S(1)}, u32[]{:S(2)}, u32[]{:S(2)}) async-start(bf16[16,64,1024]{2,1,0:T(8,128)(2,1)} %bitcast.109), calls=%async_computation.2 | async-start | bytes 4194304 | tf_op jit(solution)/shard_map/all_to_all | solution.py:153
  280.6 0.7 eq.139
  281.3 0.7 sub.13
  282.0 0.8 copy.59
  282.8 0.8 copy.63
  283.7 0.1 iota_compare_fusion.1
  283.8 1.1 fusion.29
  284.9 6.9 %fusion.22 = f32[64,2048]{1,0:T(8,128)} fusion(bf16[128,6,2048]{2,1,0:T(8,128)(2,1)} %all-to-all-done.4, f32[64,4]{0,1:T(4,128)S(1)} %copy-done.12, pred[64,4,6]{0,2,1:T(8,128)(4,1)S(1)} %iota_compare_fusion.4, pred[64,4,128]{2,0,1:T(8,128)(4,1)S(1)} %iota_compare_fusion.1), kind=kOutput, calls=%fused_computation.21 | convolution fusion | flops 806420480 | bytes 3705344 | tf_op jit(solution)/shard_map/rksc,scd->rkd/dot_general | solution.py:197
  291.9 22.6 %all-to-all-done.2 = bf16[16,64,1024]{2,1,0:T(8,128)(2,1)S(1)} async-done(((bf16[16,64,1024]{2,1,0:T(8,128)(2,1)}), bf16[16,64,1024]{2,1,0:T(8,128)(2,1)S(1)}, u32[]{:S(2)}, u32[]{:S(2)}) %all-to-all-start.2) | async-done | bytes 2097184 | tf_op jit(solution)/shard_map/all_to_all | solution.py:153
  314.5 1.1 convert_reduce_fusion
  315.6 32.0 %reduce-scatter.2.cloned.1.call-done = bf16[64,1024]{1,0:T(8,128)(2,1)} async-done(((bf16[1024,1024]{1,0:T(8,128)(2,1)}), bf16[64,1024]{1,0:T(8,128)(2,1)}) %reduce-scatter.2.cloned.1.call-update) | async-done | bytes 131088 | tf_op jit(solution)/shard_map/reduce_scatter | solution.py:158
  347.6 0.9 convert_element_type.50
  348.5 2.1 fusion.36
  (41 shorter events, 0.2 us)
Async XLA Ops:
  6.5 222.2 %copy-start = (bf16[352,2048]{1,0:T(8,128)(2,1)S(1)}, bf16[352,2048]{1,0:T(8,128)(2,1)}, u32[]{:S(2)}) copy-start(bf16[352,2048]{1,0:T(8,128)(2,1)} %param.33) | copy-start | bytes 4325380
  6.5 3.6 %copy-start.4 = (bf16[64,2048]{1,0:T(8,128)(2,1)S(1)}, bf16[64,2048]{1,0:T(8,128)(2,1)}, u32[]{:S(2)}) copy-start(bf16[64,2048]{1,0:T(8,128)(2,1)} %param.20) | copy-start | bytes 786436
  6.5 101.2 %all-gather.3.cloned.1.call-start = ((), (), s32[]{:S(2)}) async-start(), calls=%async_computation.6 | async-start | bytes 8912896 | tf_op jit(solution)/shard_map/all_gather | solution.py:108
  10.8 11.0 %copy-start.9 = (s32[128]{0:T(128)S(1)}, s32[128]{0:T(128)}, u32[]{:S(2)}) copy-start(s32[128]{0:T(128)} %param.35) | copy-start | bytes 1540
  10.8 11.4 %copy-start.6 = (s32[1024]{0:T(1024)S(1)}, s32[1024]{0:T(1024)}, u32[]{:S(2)}) copy-start(s32[1024]{0:T(1024)} %param.24) | copy-start | bytes 12292
  10.8 12.5 %copy-start.7 = (s32[1024]{0:T(1024)S(1)}, s32[1024]{0:T(1024)}, u32[]{:S(2)}) copy-start(s32[1024]{0:T(1024)} %param.25) | copy-start | bytes 12292
  12.4 11.9 %copy-start.10 = (s32[4,8]{1,0:T(4,128)S(1)}, s32[4,8]{1,0:T(4,128)}, u32[]{:S(2)}) copy-start(s32[4,8]{1,0:T(4,128)} %param.23) | copy-start | bytes 388
  12.5 51.0 %all-to-all-start = ((bf16[16,576,128]{2,1,0:T(8,128)(2,1)}), bf16[16,576,128]{2,1,0:T(8,128)(2,1)}, u32[]{:S(2)}, u32[]{:S(2)}) async-start(bf16[16,576,128]{2,1,0:T(8,128)(2,1)} %pad_maximum_fusion), calls=%async_computation | async-start | bytes 4718592 | tf_op jit(solution)/shard_map/all_to_all | solution.py:119
  68.9 38.9 %copy-start.3 = (bf16[64,2048]{1,0:T(8,128)(2,1)S(1)}, bf16[64,2048]{1,0:T(8,128)(2,1)}, u32[]{:S(2)}) copy-start(bf16[64,2048]{1,0:T(8,128)(2,1)} %param.19) | copy-start | bytes 786436
  83.2 15.7 %all-to-all-start.1 = ((bf16[16,64,128]{2,1,0:T(8,128)(2,1)}), bf16[16,64,128]{2,1,0:T(8,128)(2,1)S(1)}, u32[]{:S(2)}, u32[]{:S(2)}) async-start(bf16[16,64,128]{2,1,0:T(8,128)(2,1)} %bitcast.118), calls=%async_computation.1 | async-start | bytes 524288 | tf_op jit(solution)/shard_map/all_to_all | solution.py:136
  86.8 136.9 %all-gather.5.cloned.1.call-start = ((), (), s32[]{:S(2)}) async-start(), calls=%async_computation.7 | async-start | bytes 4456448 | tf_op jit(solution)/shard_map/all_gather | solution.py:144
  87.1 26.5 %copy-start.5 = (f32[2048]{0:T(1024)S(1)}, f32[2048]{0:T(1024)}, u32[]{:S(2)}) copy-start(f32[2048]{0:T(1024)} %param.27) | copy-start | bytes 24580
  112.8 0.8 copy-start.1
  118.5 66.1 %slice-start = ((s8[5767168]{0:T(1024)(128)(4,1)}), s8[4194304]{0:T(1024)(128)(4,1)S(1)}, s32[]{:S(2)}) async-start(s8[5767168]{0:T(1024)(128)(4,1)} %bitcast.125), calls=%async_computation.9 | async-start | bytes 8388608
  122.3 62.3 %slice-start.1 = ((s8[5767168]{0:T(1024)(128)(4,1)}), s8[1572864]{0:T(1024)(128)(4,1)S(1)}, s32[]{:S(2)}) async-start(s8[5767168]{0:T(1024)(128)(4,1)} %bitcast.125), calls=%async_computation.10 | async-start | bytes 3145728
  182.6 1.9 copy-start.2
  216.2 7.4 %copy-start.11 = (bf16[2048,352]{0,1:T(8,128)(2,1)S(1)}, bf16[2048,352]{0,1:T(8,128)(2,1)}, u32[]{:S(2)}) copy-start(bf16[2048,352]{0,1:T(8,128)(2,1)} %param.31) | copy-start | bytes 4325380
  216.2 58.8 %all-to-all-start.4 = ((bf16[128,6,2048]{2,1,0:T(8,128)(2,1)}), bf16[128,6,2048]{2,1,0:T(8,128)(2,1)}, u32[]{:S(2)}, u32[]{:S(2)}) async-start(bf16[128,6,2048]{2,1,0:T(8,128)(2,1)} %copy.67), calls=%async_computation.5 | async-start | bytes 8388608 | tf_op jit(solution)/shard_map/all_to_all | solution.py:196
  223.4 124.2 %reduce-scatter.2.cloned.1.call-start = ((), (), s32[]{:S(2)}) async-start(), calls=%async_computation.8 | async-start | bytes 2228224 | tf_op jit(solution)/shard_map/reduce_scatter | solution.py:158
  242.4 41.3 %copy-start.8 = (bf16[2048]{0:T(1024)(128)(2,1)S(1)}, bf16[2048]{0:T(1024)(128)(2,1)}, u32[]{:S(2)}) copy-start(bf16[2048]{0:T(1024)(128)(2,1)} %param.34) | copy-start | bytes 12292
  242.4 42.6 %copy-start.12 = (f32[64,4]{0,1:T(4,128)S(1)}, f32[64,4]{0,1:T(4,128)}, u32[]{:S(2)}) copy-start(f32[64,4]{0,1:T(4,128)} %param.37) | copy-start | bytes 3076
  275.0 39.5 %all-to-all-start.2 = ((bf16[16,64,1024]{2,1,0:T(8,128)(2,1)}), bf16[16,64,1024]{2,1,0:T(8,128)(2,1)S(1)}, u32[]{:S(2)}, u32[]{:S(2)}) async-start(bf16[16,64,1024]{2,1,0:T(8,128)(2,1)} %bitcast.109), calls=%async_computation.2 | async-start | bytes 4194304 | tf_op jit(solution)/shard_map/all_to_all | solution.py:153
Sparse Core Ops, SparseCore 0:
  9.5 98.1 all-gather.2
  114.6 94.0 all-gather.4
  242.5 105.0 reduce-scatter.1

commit v9 on v6

--- a/solution.py
+++ b/solution.py
@@ -142,8 +142,14 @@
     normed = rms_normed(stream, norm_gain)
 
     piece = lax.all_gather(normed, "exp", axis=0, tiled=True)
-    gate = jnp.dot(piece, shared_gate, preferred_element_type=jnp.float32)
-    upper = jnp.dot(piece, shared_up, preferred_element_type=jnp.float32)
+    hidden_here = shared_gate.shape[1]
+    both = jnp.dot(
+        piece,
+        jnp.concatenate([shared_gate, shared_up], axis=1),
+        preferred_element_type=jnp.float32,
+    )
+    gate = both[:, :hidden_here]
+    upper = both[:, hidden_here:]
     shared_hidden = (jax.nn.silu(gate) * upper).astype(jnp.bfloat16)
     shared_part = jnp.dot(
         shared_hidden, shared_down, preferred_element_type=jnp.float32

time: 343 us -> 338 us (0.985)
  matrix products: 45.9 us -> 41.7 us
    dot_general x1, matrix products: 8.98 us -> 4.4 us  [shards(): jnp.dot(shared_hidden, shared_down, preferred_element_type=jnp.float32)]
  transfers between devices with their start and end apart: 6 -> 6, of which waited for: 5 -> 5; matrix products, arithmetic and copies ran while one was open for 29% -> 28% of each run, Pallas kernels for 4% -> 4%
where the time goes in v9:
time: 338 us; the launch traced here: 336 us
  waiting for transfers between devices  163 us (48%)
  local copies, waits for them, and re-layouts  51.4 us (15%)
  matrix products  41.7 us (12%)
  starting transfers between devices  27.5 us (8%)
  blocking collectives  15.7 us (5%)
  Pallas kernels  14.3 us (4%)
  between operations  13.4 us (4%)
  other arithmetic  9.14 us (3%)
    all_gather x1, waiting for transfers between devices, shards(): piece = lax.all_gather(normed, 'exp', axis=0, tiled=True)  63 us
    all_to_all x1, waiting for transfers between devices, shards(): lax.all_to_all(answered, ('req', 'exp'), split_axis=0, concat_axis=0, til...  50.5 us
    all_to_all x1, waiting for transfers between devices, shards(): got_cols = lax.all_to_all(by_head, 'exp', 0, 0, tiled=True)  39.9 us
    dot_general x1, matrix products, expert_block(): jnp.dot(hidden, down_w, preferred_element_type=jnp.float32)  17 us
    all_to_all x1, blocking collectives, shards(): lax.all_to_all(attention.reshape(exp_count, tok_rows, HEAD_DIM), 'exp', 0...  15.7 us
    pallas_call x1, Pallas kernels, head_attention(): pl.pallas_call(head_attention_kernel, grid=(rows // tile,), out_shape=jax...  14.3 us
    all_to_all x1, starting transfers between devices, shards(): lax.all_to_all(answered, ('req', 'exp'), split_axis=0, concat_axis=0, til...  10.3 us
    dot_general x1, matrix products, expert_block(): upper = jnp.dot(rows, up_w, preferred_element_type=jnp.float32)  9.67 us
  transfers between devices with their start and end apart: 6, of which 5 were waited for; matrix products, arithmetic and copies ran while one was open for 28% of the time, Pallas kernels for 4%

profile of v9, /device:TPU:0, one launch (start us, length us, event | category | flops | bytes accessed | tf_op | source)
XLA Modules:
  0.0 336.3 jit_solution(9154335356786562249)
XLA Ops:
  6.5 0.0 copy-start
  6.5 0.0 all-gather.3.cloned.1.call-start
  6.5 0.7 all-gather.3.cloned.1.call-update
  7.3 1.5 copy.59
  8.7 0.0 copy-done.4
  8.7 0.2 copy.60
  9.0 0.0 copy-done.6
  9.0 0.1 bitcast_bitcast_fusion
  9.0 0.5 copy_bitcast_fusion
  9.6 1.6 pad_maximum_fusion
  11.2 8.1 %all-to-all-start = ((bf16[16,576,128]{2,1,0:T(8,128)(2,1)}), bf16[16,576,128]{2,1,0:T(8,128)(2,1)}, u32[]{:S(2)}, u32[]{:S(2)}) async-start(bf16[16,576,128]{2,1,0:T(8,128)(2,1)} %pad_maximum_fusion), calls=%async_computation | async-start | bytes 4718592 | tf_op jit(solution)/shard_map/all_to_all | solution.py:119
  19.4 0.0 all-gather.5.cloned.1.call-start
  19.4 1.1 copy.49.rreq_ref
  20.5 0.0 copy-done.9
  20.5 1.0 copy.50.rpos_ref
  21.5 0.0 copy-done.13
  21.5 0.1 select_reduce_fusion.1
  21.6 0.7 iota_add_fusion
  22.3 39.9 %all-to-all-done = bf16[16,576,128]{2,1,0:T(8,128)(2,1)} async-done(((bf16[16,576,128]{2,1,0:T(8,128)(2,1)}), bf16[16,576,128]{2,1,0:T(8,128)(2,1)}, u32[]{:S(2)}, u32[]{:S(2)}) %all-to-all-start) | async-done | bytes 2359328 | tf_op jit(solution)/shard_map/all_to_all | solution.py:119
  62.2 1.7 slice.30
  63.9 3.1 fusion.37
  67.0 0.7 broadcast_in_dim.14
  67.7 14.3 %shard_map.181 = bf16[1024,128]{1,0:T(8,128)(2,1)} custom-call(bf16[1024,128]{1,0:T(8,128)(2,1)} %bitcast.88, bf16[4096,128]{1,0:T(8,128)(2,1)} %bitcast.85, bf16[4096,128]{1,0:T(8,128)(2,1)} %bitcast.84, s32[1024,1]{1,0:T(8,128)} %copy.49.rreq_ref, s32[1024,1]{1,0:T(8,128)} %copy.50.rpos_ref, s32[1,4096]{1,0:T(1,128)} %bitcast.92, s32[1,4096]{1,0:T(1,128)} %bitcast.91), custom_call_target="tpu_custom_call" | custom-call | flops 2147483648 | bytes 3145728 | tf_op jit(solution)/shard_map/pallas_call | solution.py:47
  82.0 15.7 %all_to_all.20 = bf16[16,64,128]{2,1,0:T(8,128)(2,1)S(1)} all-to-all(bf16[16,64,128]{2,1,0:T(8,128)(2,1)} %bitcast.89), channel_id=1, replica_groups=mesh['req'=8,'exp'=16] {'exp'}, dimensions={0} | all-to-all | bytes 524288 | tf_op jit(solution)/shard_map/all_to_all | solution.py:136
  97.7 8.8 %all-gather.3.cloned.1.call-done = bf16[2048,2048]{1,0:T(8,128)(2,1)} async-done(((bf16[128,2048]{1,0:T(8,128)(2,1)}), bf16[2048,2048]{1,0:T(8,128)(2,1)}) %all-gather.3.cloned.1.call-update) | async-done | bytes 8388624 | tf_op jit(solution)/shard_map/all_gather | solution.py:108
  106.5 5.1 %multiply_reduce_fusion.1 = (f32[64]{0:T(128)S(1)}, f32[64,2048]{1,0:T(8,128)S(1)}) fusion(bf16[2048,2048]{1,0:T(8,128)(2,1)} %all-gather.3.cloned.1.call-done, bf16[64,2048]{1,0:T(8,128)(2,1)S(1)} %copy-done.5, bf16[16,64,128]{2,1,0:T(8,128)(2,1)S(1)} %all_to_all.20), kind=kOutput, calls=%fused_computation.32 | convolution fusion | flops 537395136 | bytes 9437440 | tf_op jit(solution)/shard_map/dot_general | solution.py:140
  111.6 0.8 copy-done.2
  112.4 0.8 multiply_convert_fusion.1
  113.3 0.0 all-gather.5.cloned.1.call-update
  113.3 0.8 constant_dynamic-slice_fusion
  114.0 0.1 copy.52
  114.1 0.1 eq.74
  114.2 0.1 eq.65
  114.4 0.1 copy.54
  114.5 0.2 convert_reduce_fusion
  114.7 0.2 fusion.28
  115.0 0.2 select_reduce_fusion
  115.2 1.5 broadcast_in_dim.18
  116.7 0.3 reshape.175
  117.0 4.3 %scatter_custom_fusion = bf16[768,2048]{1,0:T(8,128)(2,1)} fusion(s32[256]{0:T(256)S(1)} %bitcast.95, bf16[256,2048]{1,0:T(8,128)(2,1)S(1)} %reshape.175, bf16[]{:T(256)} %constant.22.clone.1), kind=kCustom, calls=%fused_computation.18 | custom fusion | bytes 3145730 | tf_op jit(solution)/shard_map/scatter | solution.py:182
  121.3 6.3 %reshape.158 = bf16[128,6,2048]{2,1,0:T(8,128)(2,1)} reshape(bf16[768,2048]{1,0:T(8,128)(2,1)} %scatter_custom_fusion) | data formatting | bytes 6291456 | tf_op jit(solution)/shard_map/reshape | solution.py:184
  127.6 8.8 %all-to-all-start.2 = ((bf16[128,6,2048]{2,1,0:T(8,128)(2,1)}), bf16[128,6,2048]{2,1,0:T(8,128)(2,1)}, u32[]{:S(2)}, u32[]{:S(2)}) async-start(bf16[128,6,2048]{2,1,0:T(8,128)(2,1)} %reshape.158), calls=%async_computation.3 | async-start | bytes 8388608 | tf_op jit(solution)/shard_map/all_to_all | solution.py:185
  136.3 0.2 reduce-scatter.2.cloned.1.call-start
  136.5 63.0 %all-gather.5.cloned.1.call-done = bf16[1024,2048]{1,0:T(8,128)(2,1)} async-done(((bf16[64,2048]{1,0:T(8,128)(2,1)}), bf16[1024,2048]{1,0:T(8,128)(2,1)}) %all-gather.5.cloned.1.call-update) | async-done | bytes 4194320 | tf_op jit(solution)/shard_map/all_gather | solution.py:144
  199.5 5.4 %fusion.11 = f32[1024,704]{0,1:T(8,128)S(1)} fusion(bf16[1024,2048]{1,0:T(8,128)(2,1)} %all-gather.5.cloned.1.call-done, bf16[2048,352]{0,1:T(8,128)(2,1)S(1)} %copy-done.14, bf16[2048,352]{0,1:T(8,128)(2,1)} %param.31), kind=kOutput, calls=%fused_computation.11 | convolution fusion | flops 2958557184 | bytes 9961472 | tf_op jit(solution)/shard_map/dot_general | solution.py:146
  204.9 4.4 %convolution_convert_fusion = bf16[1024,2048]{1,0:T(8,128)(2,1)} fusion(bf16[352,2048]{1,0:T(8,128)(2,1)S(1)} %copy-done, f32[1024,704]{0,1:T(8,128)S(1)} %fusion.11), kind=kOutput, calls=%fused_computation.9 | convolution fusion | flops 1480654848 | bytes 8519680 | tf_op jit(solution)/shard_map/dot_general | solution.py:154
  209.3 0.0 reduce-scatter.2.cloned.1.call-update
  209.4 0.0 all-to-all-done.2
  209.4 6.3 %reshape.159 = bf16[768,2048]{1,0:T(8,128)(2,1)} reshape(bf16[128,6,2048]{2,1,0:T(8,128)(2,1)} %all-to-all-done.2) | data formatting | bytes 6291456 | tf_op jit(solution)/shard_map/reshape | solution.py:187
  215.7 9.7 %fusion.2 = f32[768,1408]{1,0:T(8,128)} fusion(bf16[768,2048]{1,0:T(8,128)(2,1)} %reshape.159, bf16[1,2048,1408]{2,1,0:T(8,128)(2,1)} %param.29), kind=kOutput, calls=%fused_computation.4 | convolution fusion | flops 4429185024 | bytes 13238272 | tf_op jit(solution)/shard_map/dot_general | solution.py:14
  225.4 17.0 %fusion.8 = bf16[768,2048]{1,0:T(8,128)(2,1)} fusion(bf16[1,1408,2048]{2,1,0:T(8,128)(2,1)} %param.30, f32[768,1408]{1,0:T(8,128)} %fusion.2, bf16[768,2048]{1,0:T(8,128)(2,1)} %reshape.159, bf16[1,2048,1408]{2,1,0:T(8,128)(2,1)} %param.28), kind=kOutput, calls=%fused_computation.10 | convolution fusion | flops 8866430976 | bytes 22151168 | tf_op jit(solution)/shard_map/dot_general | solution.py:16
  242.3 6.3 %reshape.160 = bf16[128,6,2048]{2,1,0:T(8,128)(2,1)} reshape(bf16[768,2048]{1,0:T(8,128)(2,1)} %fusion.8) | data formatting | bytes 6291456 | tf_op jit(solution)/shard_map/reshape | solution.py:188
  248.7 10.3 %all-to-all-start.3 = ((bf16[128,6,2048]{2,1,0:T(8,128)(2,1)}), bf16[128,6,2048]{2,1,0:T(8,128)(2,1)}, u32[]{:S(2)}, u32[]{:S(2)}) async-start(bf16[128,6,2048]{2,1,0:T(8,128)(2,1)} %reshape.160), calls=%async_computation.4 | async-start | bytes 8388608 | tf_op jit(solution)/shard_map/all_to_all | solution.py:189
  259.0 0.7 copy.56
  259.7 0.0 copy-done.10
  259.8 0.2 fusion.21
  259.9 50.5 %all-to-all-done.3 = bf16[128,6,2048]{2,1,0:T(8,128)(2,1)} async-done(((bf16[128,6,2048]{2,1,0:T(8,128)(2,1)}), bf16[128,6,2048]{2,1,0:T(8,128)(2,1)}, u32[]{:S(2)}, u32[]{:S(2)}) %all-to-all-start.3) | async-done | bytes 3145760 | tf_op jit(solution)/shard_map/all_to_all | solution.py:189
  310.4 6.3 %reshape.161 = bf16[768,2048]{1,0:T(8,128)(2,1)} reshape(bf16[128,6,2048]{2,1,0:T(8,128)(2,1)} %all-to-all-done.3) | data formatting | bytes 6291456 | tf_op jit(solution)/shard_map/reshape | solution.py:191
  316.8 5.7 %gather_fusion = bf16[256,2048]{1,0:T(8,128)(2,1)} fusion(bf16[768,2048]{1,0:T(8,128)(2,1)} %reshape.161, s32[1024]{0:T(1024)S(1)} %pad_clamp_fusion), kind=kCustom, calls=%fused_computation | custom fusion | bytes 2098176 | tf_op jit(solution)/shard_map/gather | solution.py:192
  322.5 1.7 reshape.162
  324.2 3.1 multiply_reduce_fusion
  327.4 0.3 reduce-scatter.2.cloned.1.call-done
  327.7 2.1 add_convert_fusion
  329.8 0.0 copy-done.1
  (35 shorter events, 0.2 us)
Async XLA Ops:
  6.5 198.4 %copy-start = (bf16[352,2048]{1,0:T(8,128)(2,1)S(1)}, bf16[352,2048]{1,0:T(8,128)(2,1)}, u32[]{:S(2)}) copy-start(bf16[352,2048]{1,0:T(8,128)(2,1)} %param.33) | copy-start | bytes 4325380
  6.5 2.2 copy-start.4
  6.5 2.4 copy-start.6
  6.5 100.0 %all-gather.3.cloned.1.call-start = ((), (), s32[]{:S(2)}) async-start(), calls=%async_computation.5 | async-start | bytes 8912896 | tf_op jit(solution)/shard_map/all_gather | solution.py:108
  11.2 8.2 %copy-start.8 = (s32[1024]{0:T(1024)S(1)}, s32[1024]{0:T(1024)}, u32[]{:S(2)}) copy-start(s32[1024]{0:T(1024)} %param.24) | copy-start | bytes 12292
  11.2 9.3 %copy-start.9 = (s32[1024]{0:T(1024)S(1)}, s32[1024]{0:T(1024)}, u32[]{:S(2)}) copy-start(s32[1024]{0:T(1024)} %param.25) | copy-start | bytes 12292
  11.2 10.3 %copy-start.13 = (s32[4,8]{1,0:T(4,128)S(1)}, s32[4,8]{1,0:T(4,128)}, u32[]{:S(2)}) copy-start(s32[4,8]{1,0:T(4,128)} %param.23) | copy-start | bytes 388
  11.2 51.0 %all-to-all-start = ((bf16[16,576,128]{2,1,0:T(8,128)(2,1)}), bf16[16,576,128]{2,1,0:T(8,128)(2,1)}, u32[]{:S(2)}, u32[]{:S(2)}) async-start(bf16[16,576,128]{2,1,0:T(8,128)(2,1)} %pad_maximum_fusion), calls=%async_computation | async-start | bytes 4718592 | tf_op jit(solution)/shard_map/all_to_all | solution.py:119
  19.4 180.1 %all-gather.5.cloned.1.call-start = ((), (), s32[]{:S(2)}) async-start(), calls=%async_computation.6 | async-start | bytes 4456448 | tf_op jit(solution)/shard_map/all_gather | solution.py:144
  67.7 38.8 %copy-start.5 = (bf16[64,2048]{1,0:T(8,128)(2,1)S(1)}, bf16[64,2048]{1,0:T(8,128)(2,1)}, u32[]{:S(2)}) copy-start(bf16[64,2048]{1,0:T(8,128)(2,1)} %param.19) | copy-start | bytes 786436
  97.7 14.7 %copy-start.7 = (f32[2048]{0:T(1024)S(1)}, f32[2048]{0:T(1024)}, u32[]{:S(2)}) copy-start(f32[2048]{0:T(1024)} %param.27) | copy-start | bytes 24580
  97.7 16.8 %copy-start.11 = (s32[128]{0:T(128)S(1)}, s32[128]{0:T(128)}, u32[]{:S(2)}) copy-start(s32[128]{0:T(128)} %param.35) | copy-start | bytes 1540
  111.6 0.8 copy-start.2
  127.6 72.0 %copy-start.14 = (bf16[2048,352]{0,1:T(8,128)(2,1)S(1)}, bf16[2048,352]{0,1:T(8,128)(2,1)}, u32[]{:S(2)}) copy-start(bf16[2048,352]{0,1:T(8,128)(2,1)} %param.32) | copy-start | bytes 4325380
  127.6 81.8 %all-to-all-start.2 = ((bf16[128,6,2048]{2,1,0:T(8,128)(2,1)}), bf16[128,6,2048]{2,1,0:T(8,128)(2,1)}, u32[]{:S(2)}, u32[]{:S(2)}) async-start(bf16[128,6,2048]{2,1,0:T(8,128)(2,1)} %reshape.158), calls=%async_computation.3 | async-start | bytes 8388608 | tf_op jit(solution)/shard_map/all_to_all | solution.py:185
  136.3 191.4 %reduce-scatter.2.cloned.1.call-start = ((), (), s32[]{:S(2)}) async-start(), calls=%async_computation.7 | async-start | bytes 4456448 | tf_op jit(solution)/shard_map/reduce_scatter | solution.py:157
  248.7 10.3 %copy-start.12 = (f32[64,4]{0,1:T(4,128)S(1)}, f32[64,4]{0,1:T(4,128)}, u32[]{:S(2)}) copy-start(f32[64,4]{0,1:T(4,128)} %param.37) | copy-start | bytes 3076
  248.7 11.1 %copy-start.10 = (bf16[2048]{0:T(1024)(128)(2,1)S(1)}, bf16[2048]{0:T(1024)(128)(2,1)}, u32[]{:S(2)}) copy-start(bf16[2048]{0:T(1024)(128)(2,1)} %param.34) | copy-start | bytes 12292
  248.7 11.1 %copy-start.3 = (bf16[64,2048]{1,0:T(8,128)(2,1)S(1)}, bf16[64,2048]{1,0:T(8,128)(2,1)}, u32[]{:S(2)}) copy-start(bf16[64,2048]{1,0:T(8,128)(2,1)} %multiply_convert_fusion.1) | copy-start | bytes 786436
  248.7 61.7 %all-to-all-start.3 = ((bf16[128,6,2048]{2,1,0:T(8,128)(2,1)}), bf16[128,6,2048]{2,1,0:T(8,128)(2,1)}, u32[]{:S(2)}, u32[]{:S(2)}) async-start(bf16[128,6,2048]{2,1,0:T(8,128)(2,1)} %reshape.160), calls=%async_computation.4 | async-start | bytes 8388608 | tf_op jit(solution)/shard_map/all_to_all | solution.py:189
  316.8 13.0 %copy-start.1 = (bf16[352,2048]{1,0:T(8,128)(2,1)S(1)}, bf16[352,2048]{1,0:T(8,128)(2,1)}, u32[]{:S(2)}) copy-start(bf16[352,2048]{1,0:T(8,128)(2,1)} %param.33) | copy-start | bytes 4325380
Sparse Core Ops, SparseCore 0:
  9.5 96.9 all-gather.2
  113.4 86.0 all-gather.4
  209.5 118.1 reduce-scatter.1

commit v10 on v7

--- a/solution.py
+++ b/solution.py
@@ -142,8 +142,14 @@
     normed = rms_normed(stream, norm_gain)
 
     piece = lax.all_gather(normed, "exp", axis=0, tiled=True)
-    gate = jnp.dot(piece, shared_gate, preferred_element_type=jnp.float32)
-    upper = jnp.dot(piece, shared_up, preferred_element_type=jnp.float32)
+    hidden_here = shared_gate.shape[1]
+    both = jnp.dot(
+        piece,
+        jnp.concatenate([shared_gate, shared_up], axis=1),
+        preferred_element_type=jnp.float32,
+    )
+    gate = both[:, :hidden_here]
+    upper = both[:, hidden_here:]
     shared_hidden = (jax.nn.silu(gate) * upper).astype(jnp.bfloat16)
     shared_part = jnp.dot(
         shared_hidden, shared_down, preferred_element_type=jnp.float32

time: 348 us -> 347 us (level)
  matrix products: 59.4 us -> 55 us
  waiting for transfers between devices: 188 us -> 192 us
    dot_general x1, matrix products: 8.99 us -> 4.4 us  [shards(): jnp.dot(shared_hidden, shared_down, preferred_element_type=jnp.float32)]
  transfers between devices with their start and end apart: 6 -> 6, of which waited for: 5 -> 5; matrix products, arithmetic and copies ran while one was open for 23% -> 22% of each run, Pallas kernels for 4% -> 4%
where the time goes in v10:
time: 347 us; the launch traced here: 346 us
  waiting for transfers between devices  192 us (55%)
  matrix products  55 us (16%)
  starting transfers between devices  25.7 us (7%)
  local copies, waits for them, and re-layouts  23.9 us (7%)
  blocking collectives  15.7 us (5%)
  Pallas kernels  14.3 us (4%)
  between operations  13.4 us (4%)
  other arithmetic  5.91 us (2%)
    all_gather x1, waiting for transfers between devices, shards(): piece = lax.all_gather(normed, 'exp', axis=0, tiled=True)  72.3 us
    all_to_all x1, waiting for transfers between devices, shards(): lax.all_to_all(answered, ('req', 'exp'), split_axis=0, concat_axis=0, til...  52.6 us
    all_to_all x1, waiting for transfers between devices, shards(): got_cols = lax.all_to_all(by_head, 'exp', 0, 0, tiled=True)  39.9 us
    dot_general x1, matrix products, expert_block(): jnp.dot(hidden, down_w, preferred_element_type=jnp.float32)  18.5 us
    reduce_scatter x1, waiting for transfers between devices, shards(): lax.psum_scatter(shared_part, 'exp', scatter_dimension=0, tiled=True)  17.6 us
    all_to_all x1, blocking collectives, shards(): lax.all_to_all(attention.reshape(exp_count, tok_rows, HEAD_DIM), 'exp', 0...  15.7 us
    pallas_call x1, Pallas kernels, head_attention(): pl.pallas_call(head_attention_kernel, grid=(rows // tile,), out_shape=jax...  14.3 us
    dot_general x1, matrix products, expert_block(): upper = jnp.dot(rows, up_w, preferred_element_type=jnp.float32)  11.1 us
  transfers between devices with their start and end apart: 6, of which 5 were waited for; matrix products, arithmetic and copies ran while one was open for 22% of the time, Pallas kernels for 4%

profile of v10, /device:TPU:0, one launch (start us, length us, event | category | flops | bytes accessed | tf_op | source)
XLA Modules:
  0.0 345.7 jit_solution(5091740879747078875)
XLA Ops:
  6.5 0.0 copy-start
  6.5 0.0 all-gather.3.cloned.1.call-start
  6.5 0.7 all-gather.3.cloned.1.call-update
  7.3 1.5 copy.72
  8.7 1.5 copy.73
  10.2 0.0 copy-done.4
  10.2 0.1 bitcast_bitcast_fusion
  10.3 0.5 copy_bitcast_fusion
  10.8 0.0 copy-start.6
  10.8 0.0 copy-start.7
  10.8 0.0 copy-start.10
  10.8 1.6 pad_maximum_fusion
  12.5 8.0 %all-to-all-start = ((bf16[16,576,128]{2,1,0:T(8,128)(2,1)}), bf16[16,576,128]{2,1,0:T(8,128)(2,1)}, u32[]{:S(2)}, u32[]{:S(2)}) async-start(bf16[16,576,128]{2,1,0:T(8,128)(2,1)} %pad_maximum_fusion), calls=%async_computation | async-start | bytes 4718592 | tf_op jit(solution)/shard_map/all_to_all | solution.py:119
  20.5 0.0 all-gather.5.cloned.1.call-start
  20.5 0.0 copy-done.6
  20.6 1.1 copy.55.rreq_ref
  21.6 0.0 copy-done.7
  21.6 1.0 copy.56.rpos_ref
  22.6 0.1 select_reduce_fusion.1
  22.7 0.7 iota_add_fusion
  23.4 39.9 %all-to-all-done = bf16[16,576,128]{2,1,0:T(8,128)(2,1)} async-done(((bf16[16,576,128]{2,1,0:T(8,128)(2,1)}), bf16[16,576,128]{2,1,0:T(8,128)(2,1)}, u32[]{:S(2)}, u32[]{:S(2)}) %all-to-all-start) | async-done | bytes 2359328 | tf_op jit(solution)/shard_map/all_to_all | solution.py:119
  63.3 1.7 slice.28
  65.0 3.1 fusion.61
  68.1 0.7 broadcast_in_dim.10
  68.8 14.3 %shard_map.181 = bf16[1024,128]{1,0:T(8,128)(2,1)} custom-call(bf16[1024,128]{1,0:T(8,128)(2,1)} %bitcast.113, bf16[4096,128]{1,0:T(8,128)(2,1)} %bitcast.110, bf16[4096,128]{1,0:T(8,128)(2,1)} %bitcast.109, s32[1024,1]{1,0:T(8,128)} %copy.55.rreq_ref, s32[1024,1]{1,0:T(8,128)} %copy.56.rpos_ref, s32[1,4096]{1,0:T(1,128)} %bitcast.117, s32[1,4096]{1,0:T(1,128)} %bitcast.116), custom_call_target="tpu_custom_call" | custom-call | flops 2147483648 | bytes 3145728 | tf_op jit(solution)/shard_map/pallas_call | solution.py:47
  83.1 15.7 %all_to_all.20 = bf16[16,64,128]{2,1,0:T(8,128)(2,1)S(1)} all-to-all(bf16[16,64,128]{2,1,0:T(8,128)(2,1)} %bitcast.114), channel_id=1, replica_groups=mesh['req'=8,'exp'=16] {'exp'}, dimensions={0} | all-to-all | bytes 524288 | tf_op jit(solution)/shard_map/all_to_all | solution.py:136
  98.8 8.8 %all-gather.3.cloned.1.call-done = bf16[2048,2048]{1,0:T(8,128)(2,1)} async-done(((bf16[128,2048]{1,0:T(8,128)(2,1)}), bf16[2048,2048]{1,0:T(8,128)(2,1)}) %all-gather.3.cloned.1.call-update) | async-done | bytes 8388624 | tf_op jit(solution)/shard_map/all_gather | solution.py:108
  107.6 5.1 %multiply_reduce_fusion = (f32[64]{0:T(128)S(1)}, f32[64,2048]{1,0:T(8,128)S(1)}) fusion(bf16[2048,2048]{1,0:T(8,128)(2,1)} %all-gather.3.cloned.1.call-done, bf16[64,2048]{1,0:T(8,128)(2,1)S(1)} %copy-done.3, bf16[16,64,128]{2,1,0:T(8,128)(2,1)S(1)} %all_to_all.20), kind=kOutput, calls=%fused_computation.39 | convolution fusion | flops 537395136 | bytes 9437440 | tf_op jit(solution)/shard_map/dot_general | solution.py:140
  112.7 0.0 copy-done.5
  112.7 0.8 multiply_convert_fusion.1
  113.5 0.0 all-gather.5.cloned.1.call-update
  113.6 0.8 constant_dynamic-slice_fusion
  114.3 0.1 copy.58
  114.4 0.1 eq.143
  114.5 0.1 eq.130
  114.7 0.1 copy.61
  114.8 0.2 convert_reduce_fusion
  115.0 0.2 fusion.48
  115.3 0.2 select_reduce_fusion
  115.5 0.1 iota_compare_fusion
  115.6 3.9 %convolution_convert_fusion.1 = bf16[128,6,2048]{2,0,1:T(8,128)(2,1)} fusion(pred[256,6]{0,1:T(8,128)(4,1)S(1)} %iota_compare_fusion.6, pred[256,128]{1,0:T(8,128)(4,1)S(1)} %iota_compare_fusion, bf16[64,2048]{1,0:T(8,128)(2,1)} %multiply_convert_fusion.1, s32[256]{0:T(256)S(1)} %and_select_fusion), kind=kOutput, calls=%fused_computation.8 | convolution fusion | flops 228327424 | bytes 3443200 | tf_op jit(solution)/shard_map/sci,id->scd/dot_general | solution.py:189
  119.5 5.6 %copy.64 = bf16[128,6,2048]{2,1,0:T(8,128)(2,1)} copy(bf16[128,6,2048]{2,0,1:T(8,128)(2,1)} %convolution_convert_fusion.1) | data formatting | bytes 6291456 | tf_op jit(solution)/shard_map/convert_element_type | solution.py:191
  125.1 8.8 %all-to-all-start.2 = ((bf16[128,6,2048]{2,1,0:T(8,128)(2,1)}), bf16[128,6,2048]{2,1,0:T(8,128)(2,1)}, u32[]{:S(2)}, u32[]{:S(2)}) async-start(bf16[128,6,2048]{2,1,0:T(8,128)(2,1)} %copy.64), calls=%async_computation.3 | async-start | bytes 8388608 | tf_op jit(solution)/shard_map/all_to_all | solution.py:192
  133.9 0.0 reduce-scatter.2.cloned.1.call-start
  133.9 72.3 %all-gather.5.cloned.1.call-done = bf16[1024,2048]{1,0:T(8,128)(2,1)} async-done(((bf16[64,2048]{1,0:T(8,128)(2,1)}), bf16[1024,2048]{1,0:T(8,128)(2,1)}) %all-gather.5.cloned.1.call-update) | async-done | bytes 4194320 | tf_op jit(solution)/shard_map/all_gather | solution.py:144
  206.2 5.8 %fusion.14 = f32[1024,704]{0,1:T(8,128)S(1)} fusion(bf16[1024,2048]{1,0:T(8,128)(2,1)} %all-gather.5.cloned.1.call-done, bf16[2048,352]{0,1:T(8,128)(2,1)} %param.32, bf16[2048,352]{0,1:T(8,128)(2,1)} %param.31), kind=kOutput, calls=%fused_computation.13 | convolution fusion | flops 2958557184 | bytes 9961472 | tf_op jit(solution)/shard_map/dot_general | solution.py:146
  212.1 4.4 %convolution_convert_fusion = bf16[1024,2048]{1,0:T(8,128)(2,1)} fusion(bf16[352,2048]{1,0:T(8,128)(2,1)S(1)} %copy-done, f32[1024,704]{0,1:T(8,128)S(1)} %fusion.14), kind=kOutput, calls=%fused_computation.7 | convolution fusion | flops 1480654848 | bytes 8519680 | tf_op jit(solution)/shard_map/dot_general | solution.py:154
  216.5 0.0 reduce-scatter.2.cloned.1.call-update
  216.5 0.0 all-to-all-done.2
  216.5 11.1 %fusion.2 = f32[128,6,1408]{2,0,1:T(8,128)} fusion(bf16[1,2048,1408]{2,1,0:T(8,128)(2,1)} %param.29, bf16[128,6,2048]{2,1,0:T(8,128)(2,1)} %all-to-all-done.2), kind=kOutput, calls=%fused_computation.2 | convolution fusion | flops 4429185024 | bytes 13238272 | tf_op jit(solution)/shard_map/dot_general | solution.py:14
  227.6 18.5 %fusion.8 = bf16[128,6,2048]{2,0,1:T(8,128)(2,1)} fusion(bf16[1,1408,2048]{2,1,0:T(8,128)(2,1)} %param.30, f32[128,6,1408]{2,0,1:T(8,128)} %fusion.2, bf16[1,2048,1408]{2,1,0:T(8,128)(2,1)} %param.28, bf16[128,6,2048]{2,1,0:T(8,128)(2,1)} %all-to-all-done.2), kind=kOutput, calls=%fused_computation.9 | convolution fusion | flops 8866430976 | bytes 22151168 | tf_op jit(solution)/shard_map/dot_general | solution.py:16
  246.1 5.6 %copy.67 = bf16[128,6,2048]{2,1,0:T(8,128)(2,1)} copy(bf16[128,6,2048]{2,0,1:T(8,128)(2,1)} %fusion.8) | data formatting | bytes 6291456 | tf_op jit(solution)/shard_map/convert_element_type | solution.py:16
  251.7 8.8 %all-to-all-start.3 = ((bf16[128,6,2048]{2,1,0:T(8,128)(2,1)}), bf16[128,6,2048]{2,1,0:T(8,128)(2,1)}, u32[]{:S(2)}, u32[]{:S(2)}) async-start(bf16[128,6,2048]{2,1,0:T(8,128)(2,1)} %copy.67), calls=%async_computation.4 | async-start | bytes 8388608 | tf_op jit(solution)/shard_map/all_to_all | solution.py:194
  260.5 0.1 eq.139
  260.6 0.1 sub.13
  260.7 0.1 copy.59
  260.8 0.1 copy.63
  260.9 0.1 iota_compare_fusion.1
  261.0 0.0 copy-start.1
  261.0 0.2 fusion.33
  261.2 52.6 %all-to-all-done.3 = bf16[128,6,2048]{2,1,0:T(8,128)(2,1)} async-done(((bf16[128,6,2048]{2,1,0:T(8,128)(2,1)}), bf16[128,6,2048]{2,1,0:T(8,128)(2,1)}, u32[]{:S(2)}, u32[]{:S(2)}) %all-to-all-start.3) | async-done | bytes 3145760 | tf_op jit(solution)/shard_map/all_to_all | solution.py:194
  313.8 6.1 %fusion.27 = f32[64,2048]{1,0:T(8,128)S(1)} fusion(bf16[128,6,2048]{2,1,0:T(8,128)(2,1)} %all-to-all-done.3, f32[64,4]{0,1:T(4,128)S(1)} %copy-done.11, pred[64,4,6]{0,2,1:T(8,128)(4,1)S(1)} %iota_compare_fusion.4, pred[64,4,128]{2,0,1:T(8,128)(4,1)S(1)} %iota_compare_fusion.1), kind=kOutput, calls=%fused_computation.25 | convolution fusion | flops 806420480 | bytes 3705344 | tf_op jit(solution)/shard_map/rksc,scd->rkd/dot_general | solution.py:195
  319.9 17.6 %reduce-scatter.2.cloned.1.call-done = bf16[64,2048]{1,0:T(8,128)(2,1)} async-done(((bf16[1024,2048]{1,0:T(8,128)(2,1)}), bf16[64,2048]{1,0:T(8,128)(2,1)}) %reduce-scatter.2.cloned.1.call-update) | async-done | bytes 262160 | tf_op jit(solution)/shard_map/reduce_scatter | solution.py:157
  337.4 1.8 add_convert_fusion
  (29 shorter events, 0.2 us)
Async XLA Ops:
  6.5 205.6 %copy-start = (bf16[352,2048]{1,0:T(8,128)(2,1)S(1)}, bf16[352,2048]{1,0:T(8,128)(2,1)}, u32[]{:S(2)}) copy-start(bf16[352,2048]{1,0:T(8,128)(2,1)} %param.33) | copy-start | bytes 4325380
  6.5 3.6 %copy-start.4 = (bf16[64,2048]{1,0:T(8,128)(2,1)S(1)}, bf16[64,2048]{1,0:T(8,128)(2,1)}, u32[]{:S(2)}) copy-start(bf16[64,2048]{1,0:T(8,128)(2,1)} %param.20) | copy-start | bytes 786436
  6.5 101.1 %all-gather.3.cloned.1.call-start = ((), (), s32[]{:S(2)}) async-start(), calls=%async_computation.5 | async-start | bytes 8912896 | tf_op jit(solution)/shard_map/all_gather | solution.py:108
  10.8 9.7 %copy-start.6 = (s32[1024]{0:T(1024)S(1)}, s32[1024]{0:T(1024)}, u32[]{:S(2)}) copy-start(s32[1024]{0:T(1024)} %param.24) | copy-start | bytes 12292
  10.8 10.8 %copy-start.7 = (s32[1024]{0:T(1024)S(1)}, s32[1024]{0:T(1024)}, u32[]{:S(2)}) copy-start(s32[1024]{0:T(1024)} %param.25) | copy-start | bytes 12292
  10.8 11.8 %copy-start.10 = (s32[4,8]{1,0:T(4,128)S(1)}, s32[4,8]{1,0:T(4,128)}, u32[]{:S(2)}) copy-start(s32[4,8]{1,0:T(4,128)} %param.23) | copy-start | bytes 388
  12.5 50.9 %all-to-all-start = ((bf16[16,576,128]{2,1,0:T(8,128)(2,1)}), bf16[16,576,128]{2,1,0:T(8,128)(2,1)}, u32[]{:S(2)}, u32[]{:S(2)}) async-start(bf16[16,576,128]{2,1,0:T(8,128)(2,1)} %pad_maximum_fusion), calls=%async_computation | async-start | bytes 4718592 | tf_op jit(solution)/shard_map/all_to_all | solution.py:119
  20.5 185.8 %all-gather.5.cloned.1.call-start = ((), (), s32[]{:S(2)}) async-start(), calls=%async_computation.6 | async-start | bytes 4456448 | tf_op jit(solution)/shard_map/all_gather | solution.py:144
  68.8 38.8 %copy-start.3 = (bf16[64,2048]{1,0:T(8,128)(2,1)S(1)}, bf16[64,2048]{1,0:T(8,128)(2,1)}, u32[]{:S(2)}) copy-start(bf16[64,2048]{1,0:T(8,128)(2,1)} %param.19) | copy-start | bytes 786436
  98.8 13.9 %copy-start.5 = (f32[2048]{0:T(1024)S(1)}, f32[2048]{0:T(1024)}, u32[]{:S(2)}) copy-start(f32[2048]{0:T(1024)} %param.27) | copy-start | bytes 24580
  98.8 16.0 %copy-start.9 = (s32[128]{0:T(128)S(1)}, s32[128]{0:T(128)}, u32[]{:S(2)}) copy-start(s32[128]{0:T(128)} %param.35) | copy-start | bytes 1540
  125.1 91.5 %all-to-all-start.2 = ((bf16[128,6,2048]{2,1,0:T(8,128)(2,1)}), bf16[128,6,2048]{2,1,0:T(8,128)(2,1)}, u32[]{:S(2)}, u32[]{:S(2)}) async-start(bf16[128,6,2048]{2,1,0:T(8,128)(2,1)} %copy.64), calls=%async_computation.3 | async-start | bytes 8388608 | tf_op jit(solution)/shard_map/all_to_all | solution.py:192
  133.9 203.5 %reduce-scatter.2.cloned.1.call-start = ((), (), s32[]{:S(2)}) async-start(), calls=%async_computation.7 | async-start | bytes 4456448 | tf_op jit(solution)/shard_map/reduce_scatter | solution.py:157
  251.7 9.1 %copy-start.8 = (bf16[2048]{0:T(1024)(128)(2,1)S(1)}, bf16[2048]{0:T(1024)(128)(2,1)}, u32[]{:S(2)}) copy-start(bf16[2048]{0:T(1024)(128)(2,1)} %param.34) | copy-start | bytes 12292
  251.7 9.3 %copy-start.2 = (bf16[64,2048]{1,0:T(8,128)(2,1)S(1)}, bf16[64,2048]{1,0:T(8,128)(2,1)}, u32[]{:S(2)}) copy-start(bf16[64,2048]{1,0:T(8,128)(2,1)} %multiply_convert_fusion.1) | copy-start | bytes 786436
  251.7 62.1 %copy-start.11 = (f32[64,4]{0,1:T(4,128)S(1)}, f32[64,4]{0,1:T(4,128)}, u32[]{:S(2)}) copy-start(f32[64,4]{0,1:T(4,128)} %param.37) | copy-start | bytes 3076
  251.7 62.1 %all-to-all-start.3 = ((bf16[128,6,2048]{2,1,0:T(8,128)(2,1)}), bf16[128,6,2048]{2,1,0:T(8,128)(2,1)}, u32[]{:S(2)}, u32[]{:S(2)}) async-start(bf16[128,6,2048]{2,1,0:T(8,128)(2,1)} %copy.67), calls=%async_computation.4 | async-start | bytes 8388608 | tf_op jit(solution)/shard_map/all_to_all | solution.py:194
  261.0 78.2 %copy-start.1 = (bf16[352,2048]{1,0:T(8,128)(2,1)S(1)}, bf16[352,2048]{1,0:T(8,128)(2,1)}, u32[]{:S(2)}) copy-start(bf16[352,2048]{1,0:T(8,128)(2,1)} %param.33) | copy-start | bytes 4325380
Sparse Core Ops, SparseCore 0:
  9.5 98.0 all-gather.2
  113.7 92.5 all-gather.4
  216.7 120.7 reduce-scatter.1

commit v11 on v9

--- a/solution.py
+++ b/solution.py
@@ -188,9 +188,17 @@
     ).reshape(slot_count, capacity, model_width)
     returned = lax.all_to_all(
         answered, ("req", "exp"), split_axis=0, concat_axis=0, tiled=True
-    ).reshape(-1, model_width)
-    expert_out = returned[buffer_index].reshape(tok_rows, TOPK, model_width)
-    routed = jnp.sum(expert_out.astype(jnp.float32) * route_gate[:, :, None], axis=1)
+    )
+    entry_of = (target[:, None, None] == slot_ids[None, :, None]) & (
+        position[:, None, None] == jnp.arange(capacity, dtype=jnp.int32)[None, None, :]
+    )
+    chosen_rows = jnp.einsum(
+        "rksc,scd->rkd",
+        entry_of.reshape(tok_rows, TOPK, slot_count, capacity).astype(jnp.bfloat16),
+        returned,
+        preferred_element_type=jnp.float32,
+    )
+    routed = jnp.sum(chosen_rows * route_gate[:, :, None], axis=1)
     return (stream + shared_scale[:, None] * shared_out + routed).astype(jnp.bfloat16)
 
 

time: 338 us -> 339 us (level)
  local copies, waits for them, and re-layouts: 51.4 us -> 38 us
  waiting for transfers between devices: 163 us -> 175 us
  matrix products: 41.7 us -> 48.2 us
    reduce_scatter x1, waiting for transfers between devices: 0.32 us -> 11.8 us  [shards(): lax.psum_scatter(shared_part, 'exp', scatter_dimension=0, tiled=True)]
    reshape x1 -> x0, local copies, waits for them, and re-layouts: 6.35 us -> none  [shards(): returned = lax.all_to_all(answered, ('req', 'exp'), split_axis=0, concat_...]
    dot_general x0 -> x1, matrix products: none -> 6.09 us  [shards(): jnp.einsum('rksc,scd->rkd', entry_of.reshape(tok_rows, TOPK, slot_count,...]
    gather x1 -> x0, local copies, waits for them, and re-layouts: 5.73 us -> none  [shards(): expert_out = returned[buffer_index].reshape(tok_rows, TOPK, model_width)]
  transfers between devices with their start and end apart: 6 -> 6, of which waited for: 5 -> 5; matrix products, arithmetic and copies ran while one was open for 28% -> 25% of each run, Pallas kernels for 4% -> 4%
where the time goes in v11:
time: 339 us; the launch traced here: 338 us
  waiting for transfers between devices  175 us (52%)
  matrix products  48.2 us (14%)
  local copies, waits for them, and re-layouts  38 us (11%)
  starting transfers between devices  27.7 us (8%)
  blocking collectives  15.7 us (5%)
  Pallas kernels  14.3 us (4%)
  between operations  13.4 us (4%)
  other arithmetic  5.77 us (2%)
    all_gather x1, waiting for transfers between devices, shards(): piece = lax.all_gather(normed, 'exp', axis=0, tiled=True)  62.8 us
    all_to_all x1, waiting for transfers between devices, shards(): lax.all_to_all(answered, ('req', 'exp'), split_axis=0, concat_axis=0, til...  50.7 us
    all_to_all x1, waiting for transfers between devices, shards(): got_cols = lax.all_to_all(by_head, 'exp', 0, 0, tiled=True)  39.8 us
    dot_general x1, matrix products, expert_block(): jnp.dot(hidden, down_w, preferred_element_type=jnp.float32)  17 us
    all_to_all x1, blocking collectives, shards(): lax.all_to_all(attention.reshape(exp_count, tok_rows, HEAD_DIM), 'exp', 0...  15.7 us
    pallas_call x1, Pallas kernels, head_attention(): pl.pallas_call(head_attention_kernel, grid=(rows // tile,), out_shape=jax...  14.3 us
    reduce_scatter x1, waiting for transfers between devices, shards(): lax.psum_scatter(shared_part, 'exp', scatter_dimension=0, tiled=True)  11.8 us
    all_to_all x1, starting transfers between devices, shards(): lax.all_to_all(answered, ('req', 'exp'), split_axis=0, concat_axis=0, til...  10.5 us
  transfers between devices with their start and end apart: 6, of which 5 were waited for; matrix products, arithmetic and copies ran while one was open for 25% of the time, Pallas kernels for 4%

profile of v11, /device:TPU:0, one launch (start us, length us, event | category | flops | bytes accessed | tf_op | source)
XLA Modules:
  0.0 337.8 jit_solution(9795679644074749436)
XLA Ops:
  6.5 0.0 copy-start
  6.5 0.0 all-gather.3.cloned.1.call-start
  6.5 0.7 all-gather.3.cloned.1.call-update
  7.3 1.5 copy.66
  8.7 0.0 copy-done.3
  8.7 0.2 copy.67
  9.0 0.0 copy-done.5
  9.0 0.1 bitcast_bitcast_fusion
  9.0 0.5 copy_bitcast_fusion
  9.6 1.6 pad_maximum_fusion
  11.2 8.1 %all-to-all-start = ((bf16[16,576,128]{2,1,0:T(8,128)(2,1)}), bf16[16,576,128]{2,1,0:T(8,128)(2,1)}, u32[]{:S(2)}, u32[]{:S(2)}) async-start(bf16[16,576,128]{2,1,0:T(8,128)(2,1)} %pad_maximum_fusion), calls=%async_computation | async-start | bytes 4718592 | tf_op jit(solution)/shard_map/all_to_all | solution.py:119
  19.3 0.0 all-gather.5.cloned.1.call-start
  19.4 1.1 copy.53.rreq_ref
  20.5 0.0 copy-done.8
  20.5 1.1 copy.54.rpos_ref
  21.6 0.1 select_reduce_fusion.1
  21.7 0.7 iota_add_fusion
  22.3 39.8 %all-to-all-done = bf16[16,576,128]{2,1,0:T(8,128)(2,1)} async-done(((bf16[16,576,128]{2,1,0:T(8,128)(2,1)}), bf16[16,576,128]{2,1,0:T(8,128)(2,1)}, u32[]{:S(2)}, u32[]{:S(2)}) %all-to-all-start) | async-done | bytes 2359328 | tf_op jit(solution)/shard_map/all_to_all | solution.py:119
  62.2 1.7 slice.28
  63.9 3.1 fusion.52
  67.0 0.7 broadcast_in_dim.14
  67.6 14.3 %shard_map.181 = bf16[1024,128]{1,0:T(8,128)(2,1)} custom-call(bf16[1024,128]{1,0:T(8,128)(2,1)} %bitcast.104, bf16[4096,128]{1,0:T(8,128)(2,1)} %bitcast.101, bf16[4096,128]{1,0:T(8,128)(2,1)} %bitcast.100, s32[1024,1]{1,0:T(8,128)} %copy.53.rreq_ref, s32[1024,1]{1,0:T(8,128)} %copy.54.rpos_ref, s32[1,4096]{1,0:T(1,128)} %bitcast.108, s32[1,4096]{1,0:T(1,128)} %bitcast.107), custom_call_target="tpu_custom_call" | custom-call | flops 2147483648 | bytes 3145728 | tf_op jit(solution)/shard_map/pallas_call | solution.py:47
  81.9 15.7 %all_to_all.20 = bf16[16,64,128]{2,1,0:T(8,128)(2,1)S(1)} all-to-all(bf16[16,64,128]{2,1,0:T(8,128)(2,1)} %bitcast.105), channel_id=1, replica_groups=mesh['req'=8,'exp'=16] {'exp'}, dimensions={0} | all-to-all | bytes 524288 | tf_op jit(solution)/shard_map/all_to_all | solution.py:136
  97.6 8.9 %all-gather.3.cloned.1.call-done = bf16[2048,2048]{1,0:T(8,128)(2,1)} async-done(((bf16[128,2048]{1,0:T(8,128)(2,1)}), bf16[2048,2048]{1,0:T(8,128)(2,1)}) %all-gather.3.cloned.1.call-update) | async-done | bytes 8388624 | tf_op jit(solution)/shard_map/all_gather | solution.py:108
  106.5 5.1 %multiply_reduce_fusion = (f32[64]{0:T(128)S(1)}, f32[64,2048]{1,0:T(8,128)S(1)}) fusion(bf16[2048,2048]{1,0:T(8,128)(2,1)} %all-gather.3.cloned.1.call-done, bf16[64,2048]{1,0:T(8,128)(2,1)S(1)} %copy-done.4, bf16[16,64,128]{2,1,0:T(8,128)(2,1)S(1)} %all_to_all.20), kind=kOutput, calls=%fused_computation.37 | convolution fusion | flops 537395136 | bytes 9437440 | tf_op jit(solution)/shard_map/dot_general | solution.py:140
  111.6 0.8 multiply_convert_fusion.1
  112.4 0.0 all-gather.5.cloned.1.call-update
  112.4 0.8 constant_dynamic-slice_fusion
  113.2 0.1 copy.56
  113.3 0.1 eq.116
  113.4 0.1 eq.103
  113.5 0.1 copy.59
  113.6 0.0 copy-done.10
  113.6 0.2 convert_reduce_fusion
  113.8 0.2 fusion.43
  114.1 0.2 fusion.44
  114.4 1.5 broadcast_in_dim.18
  115.8 1.1 reshape.219
  117.0 5.0 %scatter_custom_fusion = bf16[768,2048]{1,0:T(8,128)(2,1)} fusion(s32[256]{0:T(256)S(1)} %bitcast.112, bf16[256,2048]{1,0:T(8,128)(2,1)} %reshape.219, bf16[]{:T(256)} %constant.46.clone.1), kind=kCustom, calls=%fused_computation.21 | custom fusion | bytes 3146240 | tf_op jit(solution)/shard_map/scatter | solution.py:182
  121.9 6.3 %reshape.212 = bf16[128,6,2048]{2,1,0:T(8,128)(2,1)} reshape(bf16[768,2048]{1,0:T(8,128)(2,1)} %scatter_custom_fusion) | data formatting | bytes 6291456 | tf_op jit(solution)/shard_map/reshape | solution.py:184
  128.2 8.8 %all-to-all-start.2 = ((bf16[128,6,2048]{2,1,0:T(8,128)(2,1)}), bf16[128,6,2048]{2,1,0:T(8,128)(2,1)}, u32[]{:S(2)}, u32[]{:S(2)}) async-start(bf16[128,6,2048]{2,1,0:T(8,128)(2,1)} %reshape.212), calls=%async_computation.3 | async-start | bytes 8388608 | tf_op jit(solution)/shard_map/all_to_all | solution.py:185
  137.0 0.2 reduce-scatter.2.cloned.1.call-start
  137.3 62.8 %all-gather.5.cloned.1.call-done = bf16[1024,2048]{1,0:T(8,128)(2,1)} async-done(((bf16[64,2048]{1,0:T(8,128)(2,1)}), bf16[1024,2048]{1,0:T(8,128)(2,1)}) %all-gather.5.cloned.1.call-update) | async-done | bytes 4194320 | tf_op jit(solution)/shard_map/all_gather | solution.py:144
  200.1 5.8 %fusion.14 = f32[1024,704]{0,1:T(8,128)S(1)} fusion(bf16[1024,2048]{1,0:T(8,128)(2,1)} %all-gather.5.cloned.1.call-done, bf16[2048,352]{0,1:T(8,128)(2,1)} %param.32, bf16[2048,352]{0,1:T(8,128)(2,1)} %param.31), kind=kOutput, calls=%fused_computation.13 | convolution fusion | flops 2958557184 | bytes 9961472 | tf_op jit(solution)/shard_map/dot_general | solution.py:146
  205.9 4.4 %convolution_convert_fusion = bf16[1024,2048]{1,0:T(8,128)(2,1)} fusion(bf16[352,2048]{1,0:T(8,128)(2,1)S(1)} %copy-done, f32[1024,704]{0,1:T(8,128)S(1)} %fusion.14), kind=kOutput, calls=%fused_computation.8 | convolution fusion | flops 1480654848 | bytes 8519680 | tf_op jit(solution)/shard_map/dot_general | solution.py:154
  210.3 0.0 reduce-scatter.2.cloned.1.call-update
  210.3 0.0 all-to-all-done.2
  210.3 6.3 %reshape.213 = bf16[768,2048]{1,0:T(8,128)(2,1)} reshape(bf16[128,6,2048]{2,1,0:T(8,128)(2,1)} %all-to-all-done.2) | data formatting | bytes 6291456 | tf_op jit(solution)/shard_map/reshape | solution.py:187
  216.7 9.7 %fusion.2 = f32[768,1408]{1,0:T(8,128)} fusion(bf16[768,2048]{1,0:T(8,128)(2,1)} %reshape.213, bf16[1,2048,1408]{2,1,0:T(8,128)(2,1)} %param.29), kind=kOutput, calls=%fused_computation.3 | convolution fusion | flops 4429185024 | bytes 13238272 | tf_op jit(solution)/shard_map/dot_general | solution.py:14
  226.3 17.0 %fusion.8 = bf16[768,2048]{1,0:T(8,128)(2,1)} fusion(bf16[1,1408,2048]{2,1,0:T(8,128)(2,1)} %param.30, f32[768,1408]{1,0:T(8,128)} %fusion.2, bf16[768,2048]{1,0:T(8,128)(2,1)} %reshape.213, bf16[1,2048,1408]{2,1,0:T(8,128)(2,1)} %param.28), kind=kOutput, calls=%fused_computation.9 | convolution fusion | flops 8866430976 | bytes 22151168 | tf_op jit(solution)/shard_map/dot_general | solution.py:16
  243.4 6.3 %reshape.214 = bf16[128,6,2048]{2,1,0:T(8,128)(2,1)} reshape(bf16[768,2048]{1,0:T(8,128)(2,1)} %fusion.8) | data formatting | bytes 6291456 | tf_op jit(solution)/shard_map/reshape | solution.py:188
  249.7 10.5 %all-to-all-start.3 = ((bf16[128,6,2048]{2,1,0:T(8,128)(2,1)}), bf16[128,6,2048]{2,1,0:T(8,128)(2,1)}, u32[]{:S(2)}, u32[]{:S(2)}) async-start(bf16[128,6,2048]{2,1,0:T(8,128)(2,1)} %reshape.214), calls=%async_computation.4 | async-start | bytes 8388608 | tf_op jit(solution)/shard_map/all_to_all | solution.py:189
  260.2 0.1 eq.112
  260.3 0.1 sub.7
  260.4 0.1 copy.61
  260.5 0.1 copy.57
  260.6 0.1 iota_compare_fusion
  260.7 0.0 copy-done.2
  260.7 0.0 copy-start.1
  260.7 0.2 fusion.33
  260.9 50.7 %all-to-all-done.3 = bf16[128,6,2048]{2,1,0:T(8,128)(2,1)} async-done(((bf16[128,6,2048]{2,1,0:T(8,128)(2,1)}), bf16[128,6,2048]{2,1,0:T(8,128)(2,1)}, u32[]{:S(2)}, u32[]{:S(2)}) %all-to-all-start.3) | async-done | bytes 3145760 | tf_op jit(solution)/shard_map/all_to_all | solution.py:189
  311.6 6.1 %fusion.27 = f32[64,2048]{1,0:T(8,128)S(1)} fusion(bf16[128,6,2048]{2,1,0:T(8,128)(2,1)} %all-to-all-done.3, f32[64,4]{0,1:T(4,128)S(1)} %copy-done.12, pred[64,4,6]{0,2,1:T(8,128)(4,1)S(1)} %iota_compare_fusion.2, pred[64,4,128]{2,0,1:T(8,128)(4,1)S(1)} %iota_compare_fusion), kind=kOutput, calls=%fused_computation.25 | convolution fusion | flops 806420480 | bytes 3705344 | tf_op jit(solution)/shard_map/rksc,scd->rkd/dot_general | solution.py:195
  317.7 11.8 %reduce-scatter.2.cloned.1.call-done = bf16[64,2048]{1,0:T(8,128)(2,1)} async-done(((bf16[1024,2048]{1,0:T(8,128)(2,1)}), bf16[64,2048]{1,0:T(8,128)(2,1)}) %reduce-scatter.2.cloned.1.call-update) | async-done | bytes 262160 | tf_op jit(solution)/shard_map/reduce_scatter | solution.py:157
  329.4 1.8 add_convert_fusion
  (32 shorter events, 0.2 us)
Async XLA Ops:
  6.5 199.4 %copy-start = (bf16[352,2048]{1,0:T(8,128)(2,1)S(1)}, bf16[352,2048]{1,0:T(8,128)(2,1)}, u32[]{:S(2)}) copy-start(bf16[352,2048]{1,0:T(8,128)(2,1)} %param.33) | copy-start | bytes 4325380
  6.5 2.2 copy-start.3
  6.5 2.4 copy-start.5
  6.5 99.9 %all-gather.3.cloned.1.call-start = ((), (), s32[]{:S(2)}) async-start(), calls=%async_computation.5 | async-start | bytes 8912896 | tf_op jit(solution)/shard_map/all_gather | solution.py:108
  11.2 8.2 %copy-start.7 = (s32[1024]{0:T(1024)S(1)}, s32[1024]{0:T(1024)}, u32[]{:S(2)}) copy-start(s32[1024]{0:T(1024)} %param.24) | copy-start | bytes 12292
  11.2 9.3 %copy-start.8 = (s32[1024]{0:T(1024)S(1)}, s32[1024]{0:T(1024)}, u32[]{:S(2)}) copy-start(s32[1024]{0:T(1024)} %param.25) | copy-start | bytes 12292
  11.2 10.4 %copy-start.11 = (s32[4,8]{1,0:T(4,128)S(1)}, s32[4,8]{1,0:T(4,128)}, u32[]{:S(2)}) copy-start(s32[4,8]{1,0:T(4,128)} %param.23) | copy-start | bytes 388
  11.2 51.0 %all-to-all-start = ((bf16[16,576,128]{2,1,0:T(8,128)(2,1)}), bf16[16,576,128]{2,1,0:T(8,128)(2,1)}, u32[]{:S(2)}, u32[]{:S(2)}) async-start(bf16[16,576,128]{2,1,0:T(8,128)(2,1)} %pad_maximum_fusion), calls=%async_computation | async-start | bytes 4718592 | tf_op jit(solution)/shard_map/all_to_all | solution.py:119
  19.3 180.7 %all-gather.5.cloned.1.call-start = ((), (), s32[]{:S(2)}) async-start(), calls=%async_computation.6 | async-start | bytes 4456448 | tf_op jit(solution)/shard_map/all_gather | solution.py:144
  67.6 38.9 %copy-start.4 = (bf16[64,2048]{1,0:T(8,128)(2,1)S(1)}, bf16[64,2048]{1,0:T(8,128)(2,1)}, u32[]{:S(2)}) copy-start(bf16[64,2048]{1,0:T(8,128)(2,1)} %param.19) | copy-start | bytes 786436
  97.6 14.0 %copy-start.6 = (f32[2048]{0:T(1024)S(1)}, f32[2048]{0:T(1024)}, u32[]{:S(2)}) copy-start(f32[2048]{0:T(1024)} %param.27) | copy-start | bytes 24580
  97.6 16.0 %copy-start.10 = (s32[128]{0:T(128)S(1)}, s32[128]{0:T(128)}, u32[]{:S(2)}) copy-start(s32[128]{0:T(128)} %param.35) | copy-start | bytes 1540
  128.2 82.1 %all-to-all-start.2 = ((bf16[128,6,2048]{2,1,0:T(8,128)(2,1)}), bf16[128,6,2048]{2,1,0:T(8,128)(2,1)}, u32[]{:S(2)}, u32[]{:S(2)}) async-start(bf16[128,6,2048]{2,1,0:T(8,128)(2,1)} %reshape.212), calls=%async_computation.3 | async-start | bytes 8388608 | tf_op jit(solution)/shard_map/all_to_all | solution.py:185
  137.0 192.4 %reduce-scatter.2.cloned.1.call-start = ((), (), s32[]{:S(2)}) async-start(), calls=%async_computation.7 | async-start | bytes 4456448 | tf_op jit(solution)/shard_map/reduce_scatter | solution.py:157
  249.7 10.9 %copy-start.9 = (bf16[2048]{0:T(1024)(128)(2,1)S(1)}, bf16[2048]{0:T(1024)(128)(2,1)}, u32[]{:S(2)}) copy-start(bf16[2048]{0:T(1024)(128)(2,1)} %param.34) | copy-start | bytes 12292
  249.7 11.0 %copy-start.2 = (bf16[64,2048]{1,0:T(8,128)(2,1)S(1)}, bf16[64,2048]{1,0:T(8,128)(2,1)}, u32[]{:S(2)}) copy-start(bf16[64,2048]{1,0:T(8,128)(2,1)} %multiply_convert_fusion.1) | copy-start | bytes 786436
  249.7 61.9 %copy-start.12 = (f32[64,4]{0,1:T(4,128)S(1)}, f32[64,4]{0,1:T(4,128)}, u32[]{:S(2)}) copy-start(f32[64,4]{0,1:T(4,128)} %param.37) | copy-start | bytes 3076
  249.7 61.9 %all-to-all-start.3 = ((bf16[128,6,2048]{2,1,0:T(8,128)(2,1)}), bf16[128,6,2048]{2,1,0:T(8,128)(2,1)}, u32[]{:S(2)}, u32[]{:S(2)}) async-start(bf16[128,6,2048]{2,1,0:T(8,128)(2,1)} %reshape.214), calls=%async_computation.4 | async-start | bytes 8388608 | tf_op jit(solution)/shard_map/all_to_all | solution.py:189
  260.7 70.5 %copy-start.1 = (bf16[352,2048]{1,0:T(8,128)(2,1)S(1)}, bf16[352,2048]{1,0:T(8,128)(2,1)}, u32[]{:S(2)}) copy-start(bf16[352,2048]{1,0:T(8,128)(2,1)} %param.33) | copy-start | bytes 4325380
Sparse Core Ops, SparseCore 0:
  9.5 96.9 all-gather.2
  112.5 87.4 all-gather.4
  210.4 118.9 reduce-scatter.1

commit v12 on v9

--- a/solution.py
+++ b/solution.py
@@ -39,7 +39,7 @@
 def head_attention(query_cols, key_cols, value_cols, row_request, row_position, key_request, key_position):
     rows, width = query_cols.shape
     keys = key_cols.shape[0]
-    tile = 128
+    tile = 256
     row_spec = pl.BlockSpec((tile, width), lambda i: (i, 0))
     whole = pl.BlockSpec((keys, width), lambda i: (0, 0))
     row_int = pl.BlockSpec((tile, 1), lambda i: (i, 0))

time: 338 us -> 338 us (level)
  no operation moved by 1% of the time
where the time goes in v12:
time: 338 us; the launch traced here: 336 us
  waiting for transfers between devices  164 us (49%)
  local copies, waits for them, and re-layouts  51.4 us (15%)
  matrix products  41.7 us (12%)
  starting transfers between devices  27.5 us (8%)
  blocking collectives  15.7 us (5%)
  Pallas kernels  13.4 us (4%)
  between operations  13.4 us (4%)
  other arithmetic  9.14 us (3%)
    all_gather x1, waiting for transfers between devices, shards(): piece = lax.all_gather(normed, 'exp', axis=0, tiled=True)  63 us
    all_to_all x1, waiting for transfers between devices, shards(): lax.all_to_all(answered, ('req', 'exp'), split_axis=0, concat_axis=0, til...  50.5 us
    all_to_all x1, waiting for transfers between devices, shards(): got_cols = lax.all_to_all(by_head, 'exp', 0, 0, tiled=True)  39.9 us
    dot_general x1, matrix products, expert_block(): jnp.dot(hidden, down_w, preferred_element_type=jnp.float32)  17 us
    all_to_all x1, blocking collectives, shards(): lax.all_to_all(attention.reshape(exp_count, tok_rows, HEAD_DIM), 'exp', 0...  15.7 us
    pallas_call x1, Pallas kernels, head_attention(): pl.pallas_call(head_attention_kernel, grid=(rows // tile,), out_shape=jax...  13.4 us
    all_to_all x1, starting transfers between devices, shards(): lax.all_to_all(answered, ('req', 'exp'), split_axis=0, concat_axis=0, til...  10.3 us
    all_gather x1, waiting for transfers between devices, shards(): whole_proj = lax.all_gather(out_proj, 'exp', axis=0, tiled=True)  9.79 us
  transfers between devices with their start and end apart: 6, of which 5 were waited for; matrix products, arithmetic and copies ran while one was open for 28% of the time, Pallas kernels for 4%

profile of v12, /device:TPU:0, one launch (start us, length us, event | category | flops | bytes accessed | tf_op | source)
XLA Modules:
  0.0 336.3 jit_solution(6922655124413533878)
XLA Ops:
  6.5 0.0 copy-start
  6.5 0.0 all-gather.3.cloned.1.call-start
  6.5 0.7 all-gather.3.cloned.1.call-update
  7.3 1.5 copy.59
  8.7 0.0 copy-done.4
  8.7 0.2 copy.60
  9.0 0.0 copy-done.6
  9.0 0.1 bitcast_bitcast_fusion
  9.0 0.5 copy_bitcast_fusion
  9.6 1.6 pad_maximum_fusion
  11.2 8.1 %all-to-all-start = ((bf16[16,576,128]{2,1,0:T(8,128)(2,1)}), bf16[16,576,128]{2,1,0:T(8,128)(2,1)}, u32[]{:S(2)}, u32[]{:S(2)}) async-start(bf16[16,576,128]{2,1,0:T(8,128)(2,1)} %pad_maximum_fusion), calls=%async_computation | async-start | bytes 4718592 | tf_op jit(solution)/shard_map/all_to_all | solution.py:119
  19.4 0.0 all-gather.5.cloned.1.call-start
  19.4 1.1 copy.49.rreq_ref
  20.5 0.0 copy-done.9
  20.5 1.0 copy.50.rpos_ref
  21.5 0.0 copy-done.13
  21.5 0.1 select_reduce_fusion.1
  21.6 0.7 iota_add_fusion
  22.3 39.9 %all-to-all-done = bf16[16,576,128]{2,1,0:T(8,128)(2,1)} async-done(((bf16[16,576,128]{2,1,0:T(8,128)(2,1)}), bf16[16,576,128]{2,1,0:T(8,128)(2,1)}, u32[]{:S(2)}, u32[]{:S(2)}) %all-to-all-start) | async-done | bytes 2359328 | tf_op jit(solution)/shard_map/all_to_all | solution.py:119
  62.2 1.7 slice.30
  63.9 3.1 fusion.37
  67.0 0.7 broadcast_in_dim.14
  67.7 13.4 %shard_map.181 = bf16[1024,128]{1,0:T(8,128)(2,1)} custom-call(bf16[1024,128]{1,0:T(8,128)(2,1)} %bitcast.88, bf16[4096,128]{1,0:T(8,128)(2,1)} %bitcast.85, bf16[4096,128]{1,0:T(8,128)(2,1)} %bitcast.84, s32[1024,1]{1,0:T(8,128)} %copy.49.rreq_ref, s32[1024,1]{1,0:T(8,128)} %copy.50.rpos_ref, s32[1,4096]{1,0:T(1,128)} %bitcast.92, s32[1,4096]{1,0:T(1,128)} %bitcast.91), custom_call_target="tpu_custom_call" | custom-call | flops 2147483648 | bytes 3145728 | tf_op jit(solution)/shard_map/pallas_call | solution.py:47
  81.1 15.7 %all_to_all.20 = bf16[16,64,128]{2,1,0:T(8,128)(2,1)S(1)} all-to-all(bf16[16,64,128]{2,1,0:T(8,128)(2,1)} %bitcast.89), channel_id=1, replica_groups=mesh['req'=8,'exp'=16] {'exp'}, dimensions={0} | all-to-all | bytes 524288 | tf_op jit(solution)/shard_map/all_to_all | solution.py:136
  96.7 9.8 %all-gather.3.cloned.1.call-done = bf16[2048,2048]{1,0:T(8,128)(2,1)} async-done(((bf16[128,2048]{1,0:T(8,128)(2,1)}), bf16[2048,2048]{1,0:T(8,128)(2,1)}) %all-gather.3.cloned.1.call-update) | async-done | bytes 8388624 | tf_op jit(solution)/shard_map/all_gather | solution.py:108
  106.5 5.1 %multiply_reduce_fusion.1 = (f32[64]{0:T(128)S(1)}, f32[64,2048]{1,0:T(8,128)S(1)}) fusion(bf16[2048,2048]{1,0:T(8,128)(2,1)} %all-gather.3.cloned.1.call-done, bf16[64,2048]{1,0:T(8,128)(2,1)S(1)} %copy-done.5, bf16[16,64,128]{2,1,0:T(8,128)(2,1)S(1)} %all_to_all.20), kind=kOutput, calls=%fused_computation.32 | convolution fusion | flops 537395136 | bytes 9437440 | tf_op jit(solution)/shard_map/dot_general | solution.py:140
  111.6 0.8 copy-done.2
  112.4 0.8 multiply_convert_fusion.1
  113.3 0.0 all-gather.5.cloned.1.call-update
  113.3 0.8 constant_dynamic-slice_fusion
  114.0 0.1 copy.52
  114.1 0.1 eq.74
  114.2 0.1 eq.65
  114.4 0.1 copy.54
  114.5 0.2 convert_reduce_fusion
  114.7 0.2 fusion.28
  115.0 0.2 select_reduce_fusion
  115.2 1.5 broadcast_in_dim.18
  116.7 0.3 reshape.175
  117.0 4.3 %scatter_custom_fusion = bf16[768,2048]{1,0:T(8,128)(2,1)} fusion(s32[256]{0:T(256)S(1)} %bitcast.95, bf16[256,2048]{1,0:T(8,128)(2,1)S(1)} %reshape.175, bf16[]{:T(256)} %constant.22.clone.1), kind=kCustom, calls=%fused_computation.18 | custom fusion | bytes 3145730 | tf_op jit(solution)/shard_map/scatter | solution.py:182
  121.3 6.3 %reshape.158 = bf16[128,6,2048]{2,1,0:T(8,128)(2,1)} reshape(bf16[768,2048]{1,0:T(8,128)(2,1)} %scatter_custom_fusion) | data formatting | bytes 6291456 | tf_op jit(solution)/shard_map/reshape | solution.py:184
  127.6 8.8 %all-to-all-start.2 = ((bf16[128,6,2048]{2,1,0:T(8,128)(2,1)}), bf16[128,6,2048]{2,1,0:T(8,128)(2,1)}, u32[]{:S(2)}, u32[]{:S(2)}) async-start(bf16[128,6,2048]{2,1,0:T(8,128)(2,1)} %reshape.158), calls=%async_computation.3 | async-start | bytes 8388608 | tf_op jit(solution)/shard_map/all_to_all | solution.py:185
  136.3 0.2 reduce-scatter.2.cloned.1.call-start
  136.5 63.0 %all-gather.5.cloned.1.call-done = bf16[1024,2048]{1,0:T(8,128)(2,1)} async-done(((bf16[64,2048]{1,0:T(8,128)(2,1)}), bf16[1024,2048]{1,0:T(8,128)(2,1)}) %all-gather.5.cloned.1.call-update) | async-done | bytes 4194320 | tf_op jit(solution)/shard_map/all_gather | solution.py:144
  199.5 5.4 %fusion.11 = f32[1024,704]{0,1:T(8,128)S(1)} fusion(bf16[1024,2048]{1,0:T(8,128)(2,1)} %all-gather.5.cloned.1.call-done, bf16[2048,352]{0,1:T(8,128)(2,1)S(1)} %copy-done.14, bf16[2048,352]{0,1:T(8,128)(2,1)} %param.31), kind=kOutput, calls=%fused_computation.11 | convolution fusion | flops 2958557184 | bytes 9961472 | tf_op jit(solution)/shard_map/dot_general | solution.py:146
  204.9 4.4 %convolution_convert_fusion = bf16[1024,2048]{1,0:T(8,128)(2,1)} fusion(bf16[352,2048]{1,0:T(8,128)(2,1)S(1)} %copy-done, f32[1024,704]{0,1:T(8,128)S(1)} %fusion.11), kind=kOutput, calls=%fused_computation.9 | convolution fusion | flops 1480654848 | bytes 8519680 | tf_op jit(solution)/shard_map/dot_general | solution.py:154
  209.3 0.0 reduce-scatter.2.cloned.1.call-update
  209.4 0.0 all-to-all-done.2
  209.4 6.3 %reshape.159 = bf16[768,2048]{1,0:T(8,128)(2,1)} reshape(bf16[128,6,2048]{2,1,0:T(8,128)(2,1)} %all-to-all-done.2) | data formatting | bytes 6291456 | tf_op jit(solution)/shard_map/reshape | solution.py:187
  215.7 9.7 %fusion.2 = f32[768,1408]{1,0:T(8,128)} fusion(bf16[768,2048]{1,0:T(8,128)(2,1)} %reshape.159, bf16[1,2048,1408]{2,1,0:T(8,128)(2,1)} %param.29), kind=kOutput, calls=%fused_computation.4 | convolution fusion | flops 4429185024 | bytes 13238272 | tf_op jit(solution)/shard_map/dot_general | solution.py:14
  225.4 17.0 %fusion.8 = bf16[768,2048]{1,0:T(8,128)(2,1)} fusion(bf16[1,1408,2048]{2,1,0:T(8,128)(2,1)} %param.30, f32[768,1408]{1,0:T(8,128)} %fusion.2, bf16[768,2048]{1,0:T(8,128)(2,1)} %reshape.159, bf16[1,2048,1408]{2,1,0:T(8,128)(2,1)} %param.28), kind=kOutput, calls=%fused_computation.10 | convolution fusion | flops 8866430976 | bytes 22151168 | tf_op jit(solution)/shard_map/dot_general | solution.py:16
  242.3 6.3 %reshape.160 = bf16[128,6,2048]{2,1,0:T(8,128)(2,1)} reshape(bf16[768,2048]{1,0:T(8,128)(2,1)} %fusion.8) | data formatting | bytes 6291456 | tf_op jit(solution)/shard_map/reshape | solution.py:188
  248.7 10.3 %all-to-all-start.3 = ((bf16[128,6,2048]{2,1,0:T(8,128)(2,1)}), bf16[128,6,2048]{2,1,0:T(8,128)(2,1)}, u32[]{:S(2)}, u32[]{:S(2)}) async-start(bf16[128,6,2048]{2,1,0:T(8,128)(2,1)} %reshape.160), calls=%async_computation.4 | async-start | bytes 8388608 | tf_op jit(solution)/shard_map/all_to_all | solution.py:189
  259.0 0.7 copy.56
  259.7 0.0 copy-done.10
  259.8 0.2 fusion.21
  259.9 50.5 %all-to-all-done.3 = bf16[128,6,2048]{2,1,0:T(8,128)(2,1)} async-done(((bf16[128,6,2048]{2,1,0:T(8,128)(2,1)}), bf16[128,6,2048]{2,1,0:T(8,128)(2,1)}, u32[]{:S(2)}, u32[]{:S(2)}) %all-to-all-start.3) | async-done | bytes 3145760 | tf_op jit(solution)/shard_map/all_to_all | solution.py:189
  310.4 6.3 %reshape.161 = bf16[768,2048]{1,0:T(8,128)(2,1)} reshape(bf16[128,6,2048]{2,1,0:T(8,128)(2,1)} %all-to-all-done.3) | data formatting | bytes 6291456 | tf_op jit(solution)/shard_map/reshape | solution.py:191
  316.8 5.7 %gather_fusion = bf16[256,2048]{1,0:T(8,128)(2,1)} fusion(bf16[768,2048]{1,0:T(8,128)(2,1)} %reshape.161, s32[1024]{0:T(1024)S(1)} %pad_clamp_fusion), kind=kCustom, calls=%fused_computation | custom fusion | bytes 2098176 | tf_op jit(solution)/shard_map/gather | solution.py:192
  322.5 1.7 reshape.162
  324.2 3.1 multiply_reduce_fusion
  327.4 0.3 reduce-scatter.2.cloned.1.call-done
  327.7 2.1 add_convert_fusion
  329.8 0.0 copy-done.1
  (35 shorter events, 0.2 us)
Async XLA Ops:
  6.5 198.4 %copy-start = (bf16[352,2048]{1,0:T(8,128)(2,1)S(1)}, bf16[352,2048]{1,0:T(8,128)(2,1)}, u32[]{:S(2)}) copy-start(bf16[352,2048]{1,0:T(8,128)(2,1)} %param.33) | copy-start | bytes 4325380
  6.5 2.2 copy-start.4
  6.5 2.4 copy-start.6
  6.5 100.0 %all-gather.3.cloned.1.call-start = ((), (), s32[]{:S(2)}) async-start(), calls=%async_computation.5 | async-start | bytes 8912896 | tf_op jit(solution)/shard_map/all_gather | solution.py:108
  11.2 8.2 %copy-start.8 = (s32[1024]{0:T(1024)S(1)}, s32[1024]{0:T(1024)}, u32[]{:S(2)}) copy-start(s32[1024]{0:T(1024)} %param.24) | copy-start | bytes 12292
  11.2 9.3 %copy-start.9 = (s32[1024]{0:T(1024)S(1)}, s32[1024]{0:T(1024)}, u32[]{:S(2)}) copy-start(s32[1024]{0:T(1024)} %param.25) | copy-start | bytes 12292
  11.2 10.3 %copy-start.13 = (s32[4,8]{1,0:T(4,128)S(1)}, s32[4,8]{1,0:T(4,128)}, u32[]{:S(2)}) copy-start(s32[4,8]{1,0:T(4,128)} %param.23) | copy-start | bytes 388
  11.2 51.0 %all-to-all-start = ((bf16[16,576,128]{2,1,0:T(8,128)(2,1)}), bf16[16,576,128]{2,1,0:T(8,128)(2,1)}, u32[]{:S(2)}, u32[]{:S(2)}) async-start(bf16[16,576,128]{2,1,0:T(8,128)(2,1)} %pad_maximum_fusion), calls=%async_computation | async-start | bytes 4718592 | tf_op jit(solution)/shard_map/all_to_all | solution.py:119
  19.4 180.1 %all-gather.5.cloned.1.call-start = ((), (), s32[]{:S(2)}) async-start(), calls=%async_computation.6 | async-start | bytes 4456448 | tf_op jit(solution)/shard_map/all_gather | solution.py:144
  67.7 38.8 %copy-start.5 = (bf16[64,2048]{1,0:T(8,128)(2,1)S(1)}, bf16[64,2048]{1,0:T(8,128)(2,1)}, u32[]{:S(2)}) copy-start(bf16[64,2048]{1,0:T(8,128)(2,1)} %param.19) | copy-start | bytes 786436
  96.7 15.7 %copy-start.7 = (f32[2048]{0:T(1024)S(1)}, f32[2048]{0:T(1024)}, u32[]{:S(2)}) copy-start(f32[2048]{0:T(1024)} %param.27) | copy-start | bytes 24580
  96.7 17.7 %copy-start.11 = (s32[128]{0:T(128)S(1)}, s32[128]{0:T(128)}, u32[]{:S(2)}) copy-start(s32[128]{0:T(128)} %param.35) | copy-start | bytes 1540
  111.6 0.8 copy-start.2
  127.6 72.0 %copy-start.14 = (bf16[2048,352]{0,1:T(8,128)(2,1)S(1)}, bf16[2048,352]{0,1:T(8,128)(2,1)}, u32[]{:S(2)}) copy-start(bf16[2048,352]{0,1:T(8,128)(2,1)} %param.32) | copy-start | bytes 4325380
  127.6 81.8 %all-to-all-start.2 = ((bf16[128,6,2048]{2,1,0:T(8,128)(2,1)}), bf16[128,6,2048]{2,1,0:T(8,128)(2,1)}, u32[]{:S(2)}, u32[]{:S(2)}) async-start(bf16[128,6,2048]{2,1,0:T(8,128)(2,1)} %reshape.158), calls=%async_computation.3 | async-start | bytes 8388608 | tf_op jit(solution)/shard_map/all_to_all | solution.py:185
  136.3 191.4 %reduce-scatter.2.cloned.1.call-start = ((), (), s32[]{:S(2)}) async-start(), calls=%async_computation.7 | async-start | bytes 4456448 | tf_op jit(solution)/shard_map/reduce_scatter | solution.py:157
  248.7 10.3 %copy-start.12 = (f32[64,4]{0,1:T(4,128)S(1)}, f32[64,4]{0,1:T(4,128)}, u32[]{:S(2)}) copy-start(f32[64,4]{0,1:T(4,128)} %param.37) | copy-start | bytes 3076
  248.7 11.1 %copy-start.10 = (bf16[2048]{0:T(1024)(128)(2,1)S(1)}, bf16[2048]{0:T(1024)(128)(2,1)}, u32[]{:S(2)}) copy-start(bf16[2048]{0:T(1024)(128)(2,1)} %param.34) | copy-start | bytes 12292
  248.7 11.1 %copy-start.3 = (bf16[64,2048]{1,0:T(8,128)(2,1)S(1)}, bf16[64,2048]{1,0:T(8,128)(2,1)}, u32[]{:S(2)}) copy-start(bf16[64,2048]{1,0:T(8,128)(2,1)} %multiply_convert_fusion.1) | copy-start | bytes 786436
  248.7 61.7 %all-to-all-start.3 = ((bf16[128,6,2048]{2,1,0:T(8,128)(2,1)}), bf16[128,6,2048]{2,1,0:T(8,128)(2,1)}, u32[]{:S(2)}, u32[]{:S(2)}) async-start(bf16[128,6,2048]{2,1,0:T(8,128)(2,1)} %reshape.160), calls=%async_computation.4 | async-start | bytes 8388608 | tf_op jit(solution)/shard_map/all_to_all | solution.py:189
  316.8 13.0 %copy-start.1 = (bf16[352,2048]{1,0:T(8,128)(2,1)S(1)}, bf16[352,2048]{1,0:T(8,128)(2,1)}, u32[]{:S(2)}) copy-start(bf16[352,2048]{1,0:T(8,128)(2,1)} %param.33) | copy-start | bytes 4325380
Sparse Core Ops, SparseCore 0:
  9.5 96.9 all-gather.2
  113.4 86.0 all-gather.4
  209.5 118.1 reduce-scatter.1
